TPU v7x, 512 devices: a whole 4x4x16 slice. The times are simulated.
512 devices in a mesh: tile: 32 (over z_lo, x, core), head: 16 (over z_hi, y).
Axes of the slice: x: 4, y: 4, z: 16 (z_hi: 4, z_lo: 4; z = z_hi * 4 + z_lo), core: 2. Of those that a mesh axis runs over, the one named last changes fastest.
Arguments:
- tokens: bfloat16 [8192, 1024], P('tile'), may hold values from -40 to 40
- w_qkv: bfloat16 [3072, 1024], P('head'), may hold values from -0.125 to 0.125
- grad_out: bfloat16 [8192, 1024], P('tile', 'head'), may hold values from -6 to 6
- edge_valid: int32 [32, 8], P('tile'), may hold values 0 or 1
Outputs:
- grad_x: bfloat16 [8192, 1024], P(('tile', 'head'))
- grad_w: float32 [1024, 3072], P('tile', 'head')
All inputs are finite; a program needn't handle non-finite values. No bound on the sum of `edge_valid` on one device may be relied on, other than what follows from the above.
Results may differ from a plain program's by a relative error of at most 0.024.
Values may be sent and summed in bfloat16 or wider, within the bound.
No kernel may reach another device: no remote copies, remote signals or barrier semaphores. Data moves between devices by JAX's collectives and lax.ppermute only.
A program may use at most 64 MiB of HBM per device.

v0:
```python
import jax
import jax.numpy as jnp
from jax import lax
from jax.sharding import PartitionSpec as P

D = 1024
HEADS = 16
HALO = 12
S = 16
GRID_ROWS = 4


directions = ((-1, -1), (-1, 0), (-1, 1), (0, -1), (0, 1), (1, -1), (1, 0), (1, 1))
band_height = 16


def passed_along(value, axis, steps):
    count = lax.axis_size(axis)
    first, last = (max(0, -steps), min(count, count - steps))
    return lax.ppermute(value, axis, [(source, source + steps) for source in range(first, last)])


def source_span(offset, side, halo):
    if offset == -1:
        return (side - halo, side)
    if offset == 1:
        return (0, halo)
    return (0, side)


def target_span(offset, side, halo):
    if offset == -1:
        return (0, halo)
    if offset == 1:
        return (halo + side, side + 2 * halo)
    return (halo, halo + side)


def usable_region(flags, grid_row, grid_col, columns, side, halo):
    width = side + 2 * halo
    place = jnp.arange(width)
    bands = (place >= halo).astype(jnp.int32) + (place >= halo + side).astype(jnp.int32)
    usable = ((bands[:, None] == 1) & (bands[None, :] == 1)).astype(jnp.int32)
    for number, (row_step, column_step) in enumerate(directions):
        inside = (grid_row + row_step >= 0) & (grid_row + row_step < GRID_ROWS)
        inside = inside & (grid_col + column_step >= 0) & (grid_col + column_step < columns)
        flag = flags[number] * inside.astype(jnp.int32)
        strike = (bands[:, None] == row_step + 1) & (bands[None, :] == column_step + 1)
        usable = usable + flag * strike.astype(jnp.int32)
    return usable > 0


def window_mask(height, side, halo):
    width = side + 2 * halo
    query_row = jnp.arange(height)[:, None, None, None]
    query_column = jnp.arange(side)[None, :, None, None]
    key_row = jnp.arange(height + 2 * halo)[None, None, :, None]
    key_column = jnp.arange(width)[None, None, None, :]
    near = (jnp.abs(key_row - query_row - halo) <= halo) & (
        jnp.abs(key_column - query_column - halo) <= halo
    )
    return near.reshape(height * side, (height + 2 * halo) * width)


def band_backward(query, keys, values, grads, allowed):
    scale = query.shape[-1] ** (-0.5)
    scores = jnp.einsum("qhe,khe->hqk", query, keys, preferred_element_type=jnp.float32) * scale
    scores = jnp.where(allowed[None], scores, -1e30)
    highest = jnp.max(scores, axis=2, keepdims=True)
    lifted = jnp.exp(scores - highest)
    probs = lifted / jnp.sum(lifted, axis=2, keepdims=True)
    probs_low = probs.astype(jnp.bfloat16)
    attended = jnp.einsum("hqk,khe->qhe", probs_low, values, preferred_element_type=jnp.float32)
    row_dot = jnp.sum(grads.astype(jnp.float32) * attended, axis=2)
    grad_probs = jnp.einsum("qhe,khe->hqk", grads, values, preferred_element_type=jnp.float32)
    grad_scores = (probs * (grad_probs - jnp.transpose(row_dot)[:, :, None])).astype(jnp.bfloat16)
    grad_query = (
        jnp.einsum("hqk,khe->qhe", grad_scores, keys, preferred_element_type=jnp.float32) * scale
    )
    grad_keys = (
        jnp.einsum("hqk,qhe->khe", grad_scores, query, preferred_element_type=jnp.float32) * scale
    )
    grad_values = jnp.einsum("hqk,qhe->khe", probs_low, grads, preferred_element_type=jnp.float32)
    return (grad_query, grad_keys, grad_values)


def shards(tokens, w_qkv, grad_out, edge_valid):
    side = S
    halo = HALO
    width = side + 2 * halo
    head_width = D // HEADS
    tiles = lax.axis_size("tile")
    columns = tiles // GRID_ROWS
    number = lax.axis_index("tile")
    grid_row = number // columns
    grid_col = number % columns
    local_heads = w_qkv.shape[0] // (3 * head_width)
    projected = lax.dot_general(
        tokens, w_qkv, (((1,), (1,)), ((), ())), preferred_element_type=jnp.float32
    ).astype(jnp.bfloat16)
    arranged = projected.reshape(side, side, local_heads, 3 * head_width)
    queries = arranged[:, :, :, :head_width]
    pairs = arranged[:, :, :, head_width:]
    region = jnp.zeros((width, width, local_heads, 2 * head_width), jnp.bfloat16)
    region = region.at[halo : halo + side, halo : halo + side].set(pairs)
    for row_step, column_step in directions:
        from_top, from_bottom = source_span(row_step, side, halo)
        from_left, from_right = source_span(column_step, side, halo)
        moved = passed_along(
            pairs[from_top:from_bottom, from_left:from_right],
            "tile",
            -(row_step * columns + column_step),
        )
        into_top, into_bottom = target_span(row_step, side, halo)
        into_left, into_right = target_span(column_step, side, halo)
        region = region.at[into_top:into_bottom, into_left:into_right].set(moved)
    usable = usable_region(edge_valid[0], grid_row, grid_col, columns, side, halo)
    near = window_mask(band_height, side, halo)
    grads_grid = grad_out.reshape(side, side, local_heads, head_width)
    grad_region = jnp.zeros((width, width, local_heads, 2 * head_width), jnp.float32)
    query_block = queries.reshape(band_height * side, local_heads, head_width)
    grad_block = grads_grid.reshape(band_height * side, local_heads, head_width)
    key_block = region.reshape(-1, local_heads, 2 * head_width)
    allowed = near & usable.reshape(1, -1)
    grad_query, grad_keys, grad_values = band_backward(
        query_block, key_block[:, :, :head_width], key_block[:, :, head_width:], grad_block, allowed
    )
    query_grads = grad_query.reshape(band_height, side, local_heads, head_width)
    joined = jnp.concatenate([grad_keys, grad_values], axis=2).reshape(
        band_height + 2 * halo, width, local_heads, 2 * head_width
    )
    grad_region = grad_region.at[0 : band_height + 2 * halo].add(joined)
    own = grad_region[halo : halo + side, halo : halo + side]
    for row_step, column_step in directions:
        into_top, into_bottom = target_span(row_step, side, halo)
        into_left, into_right = target_span(column_step, side, halo)
        moved = passed_along(
            grad_region[into_top:into_bottom, into_left:into_right].astype(jnp.bfloat16),
            "tile",
            row_step * columns + column_step,
        ).astype(jnp.float32)
        from_top, from_bottom = source_span(row_step, side, halo)
        from_left, from_right = source_span(column_step, side, halo)
        own = own.at[from_top:from_bottom, from_left:from_right].add(moved)
    grad_qkv = (
        jnp.concatenate([query_grads, own], axis=3)
        .reshape(side * side, local_heads * 3 * head_width)
        .astype(jnp.bfloat16)
    )
    grad_w = lax.psum_scatter(
        lax.dot_general(
            tokens, grad_qkv, (((0,), (0,)), ((), ())), preferred_element_type=jnp.float32
        ).astype(jnp.bfloat16),
        "tile",
        scatter_dimension=0,
        tiled=True,
    ).astype(jnp.float32)
    partial_value = jnp.dot(grad_qkv, w_qkv, preferred_element_type=jnp.float32)
    grad_x = lax.psum_scatter(
        partial_value.astype(jnp.bfloat16), "head", scatter_dimension=0, tiled=True
    )
    return (grad_x, grad_w)


def solution(mesh):
    in_specs = (P("tile", None), P("head", None), P("tile", "head"), P("tile", None))
    out_specs = (P(("tile", "head"), None), P("tile", "head"))
    return jax.shard_map(shards, mesh=mesh, in_specs=in_specs, out_specs=out_specs, check_vma=False)
```

profile of v0, /device:TPU:1, one launch (start us, length us, event | category | flops | bytes accessed | tf_op | source)
XLA Modules:
  0.0 368.0 jit_solution(13340325871058889950)
XLA Ops:
  8.2 1.3 convolution_convert_fusion.2
  9.8 5.8 %collective-permute-start = (bf16[12,12,1,128]{3,1,0,2:T(8,128)(2,1)S(1)}, bf16[12,12,1,128]{3,1,0,2:T(8,128)(2,1)S(1)}, u32[]{:S(2)}, u32[]{:S(2)}) collective-permute-start(bf16[12,12,1,128]{3,1,0,2:T(8,128)(2,1)S(1)} %get-tuple-element.247), channel_id=1, source_target_pairs={{0,144},{16,160},{32,176},{48,192},{64,208},{80,224},{96,240},{112... | collective-permute-start | bytes 110600 | tf_op jit(solution)/shard_map/ppermute | solution.py:20
  15.8 3.6 collective-permute-start.1
  19.3 2.6 collective-permute-start.2
  22.1 4.3 %collective-permute-start.3 = (bf16[16,12,1,128]{3,1,0,2:T(8,128)(2,1)S(1)}, bf16[16,12,1,128]{3,1,0,2:T(8,128)(2,1)S(1)}, u32[]{:S(2)}, u32[]{:S(2)}) collective-permute-start(bf16[16,12,1,128]{3,1,0,2:T(8,128)(2,1)S(1)} %get-tuple-element.251), channel_id=1, source_target_pairs={{0,16},{16,32},{32,48},{48,64},{64,80},{80,96},{96,112},{112,128},... | collective-permute-start | bytes 147464 | tf_op jit(solution)/shard_map/ppermute | solution.py:20
  26.4 1.9 collective-permute-start.4
  39.3 2.0 and.331
  42.0 1.3 collective-permute-start.5
  44.8 1.9 dynamic-slice_select_fusion.1
  46.8 1.5 scatter.34
  48.4 1.3 collective-permute-start.7
  49.7 1.9 dynamic-slice_select_fusion
  51.6 1.5 scatter.35
  54.2 1.8 collective-permute-done.7
  62.2 1.3 collective-permute-start.9
  64.8 2.6 collective-permute-start.11
  67.4 3.0 collective-permute-start.12
  70.5 7.3 %collective-permute-start.13 = (bf16[12,12,1,128]{3,1,0,2:T(8,128)(2,1)S(1)}, bf16[12,12,1,128]{3,1,0,2:T(8,128)(2,1)S(1)}, u32[]{:S(2)}, u32[]{:S(2)}) collective-permute-start(bf16[12,12,1,128]{3,1,0,2:T(8,128)(2,1)S(1)} %get-tuple-element.237), channel_id=1, source_target_pairs={{0,112},{16,128},{32,144},{48,160},{64,176},{80,192},{96,208},{112... | collective-permute-start | bytes 110600 | tf_op jit(solution)/shard_map/ppermute | solution.py:20
  78.0 6.7 %collective-permute-start.14 = (bf16[12,16,1,128]{3,1,0,2:T(8,128)(2,1)S(1)}, bf16[12,16,1,128]{3,1,0,2:T(8,128)(2,1)S(1)}, u32[]{:S(2)}, u32[]{:S(2)}) collective-permute-start(bf16[12,16,1,128]{3,1,0,2:T(8,128)(2,1)S(1)} %get-tuple-element.240), channel_id=1, source_target_pairs={{0,128},{16,144},{32,160},{48,176},{64,192},{80,208},{96,224},{112... | collective-permute-start | bytes 147464 | tf_op jit(solution)/shard_map/ppermute | solution.py:20
  84.8 4.0 %collective-permute-start.15 = (bf16[12,12,1,128]{3,1,0,2:T(8,128)(2,1)S(1)}, bf16[12,12,1,128]{3,1,0,2:T(8,128)(2,1)S(1)}, u32[]{:S(2)}, u32[]{:S(2)}) collective-permute-start(bf16[12,12,1,128]{3,1,0,2:T(8,128)(2,1)S(1)} %get-tuple-element.236), channel_id=1, source_target_pairs={{0,144},{16,160},{32,176},{48,192},{64,208},{80,224},{96,240},{112... | collective-permute-start | bytes 110600 | tf_op jit(solution)/shard_map/ppermute | solution.py:20
  89.5 2.0 add_select_fusion
  91.5 1.4 scatter-add.35
  95.9 148.6 %reduce-scatter.7.cloned.1.call-done = bf16[32,192]{1,0:T(8,128)(2,1)} async-done(((bf16[1024,192]{1,0:T(8,128)(2,1)}), bf16[32,192]{1,0:T(8,128)(2,1)}) %reduce-scatter.7.cloned.1.call-update) | async-done | bytes 12304
  246.0 115.2 %reduce-scatter.5.cloned.1.call-done = bf16[16,1024]{1,0:T(8,128)(2,1)} async-done(((bf16[256,1024]{1,0:T(8,128)(2,1)}), bf16[16,1024]{1,0:T(8,128)(2,1)}) %reduce-scatter.5.cloned.1.call-update) | async-done | bytes 32784 | tf_op jit(solution)/shard_map/reduce_scatter | solution.py:159
  (100 shorter events, 23.2 us)
Async XLA Ops:
  7.2 1.1 copy-start
  7.2 22.5 %copy-start.6 = (s32[4]{0:T(128)S(1)}, s32[4]{0:T(128)}, u32[]{:S(2)}) copy-start(s32[4]{0:T(128)} %constant.571.clone.1) | copy-start | bytes 52
  7.2 23.2 %copy-start.5 = (s32[4]{0:T(128)S(1)}, s32[4]{0:T(128)}, u32[]{:S(2)}) copy-start(s32[4]{0:T(128)} %constant.574.clone.1) | copy-start | bytes 52
  7.2 30.4 %copy-start.4 = (s32[4]{0:T(128)S(1)}, s32[4]{0:T(128)}, u32[]{:S(2)}) copy-start(s32[4]{0:T(128)} %constant.589.clone.1) | copy-start | bytes 52
  7.2 24.6 %copy-start.3 = (s32[1,8]{1,0:T(1,128)S(1)}, s32[1,8]{1,0:T(1,128)}, u32[]{:S(2)}) copy-start(s32[1,8]{1,0:T(1,128)} %param.45) | copy-start | bytes 100
  7.2 237.2 %reduce-scatter.7.cloned.1.call-start = ((), (), s32[]{:S(2)}) async-start(), calls=%async_computation.3 | async-start | bytes 540672
  9.8 32.2 %collective-permute-start = (bf16[12,12,1,128]{3,1,0,2:T(8,128)(2,1)S(1)}, bf16[12,12,1,128]{3,1,0,2:T(8,128)(2,1)S(1)}, u32[]{:S(2)}, u32[]{:S(2)}) collective-permute-start(bf16[12,12,1,128]{3,1,0,2:T(8,128)(2,1)S(1)} %get-tuple-element.247), channel_id=1, source_target_pairs={{0,144},{16,160},{32,176},{48,192},{64,208},{80,224},{96,240},{112... | collective-permute-start | bytes 110600 | tf_op jit(solution)/shard_map/ppermute | solution.py:20
  15.8 27.8 %collective-permute-start.1 = (bf16[12,16,1,128]{3,1,0,2:T(8,128)(2,1)S(1)}, bf16[12,16,1,128]{3,1,0,2:T(8,128)(2,1)S(1)}, u32[]{:S(2)}, u32[]{:S(2)}) collective-permute-start(bf16[12,16,1,128]{3,1,0,2:T(8,128)(2,1)S(1)} %get-tuple-element.249), channel_id=1, source_target_pairs={{0,128},{16,144},{32,160},{48,176},{64,192},{80,208},{96,224},{112... | collective-permute-start | bytes 147464 | tf_op jit(solution)/shard_map/ppermute | solution.py:20
  19.3 29.0 %collective-permute-start.2 = (bf16[12,12,1,128]{3,1,0,2:T(8,128)(2,1)S(1)}, bf16[12,12,1,128]{3,1,0,2:T(8,128)(2,1)S(1)}, u32[]{:S(2)}, u32[]{:S(2)}) collective-permute-start(bf16[12,12,1,128]{3,1,0,2:T(8,128)(2,1)S(1)} %get-tuple-element.246), channel_id=1, source_target_pairs={{0,112},{16,128},{32,144},{48,160},{64,176},{80,192},{96,208},{112... | collective-permute-start | bytes 110600 | tf_op jit(solution)/shard_map/ppermute | solution.py:20
  22.1 31.0 %collective-permute-start.3 = (bf16[16,12,1,128]{3,1,0,2:T(8,128)(2,1)S(1)}, bf16[16,12,1,128]{3,1,0,2:T(8,128)(2,1)S(1)}, u32[]{:S(2)}, u32[]{:S(2)}) collective-permute-start(bf16[16,12,1,128]{3,1,0,2:T(8,128)(2,1)S(1)} %get-tuple-element.251), channel_id=1, source_target_pairs={{0,16},{16,32},{32,48},{48,64},{64,80},{80,96},{96,112},{112,128},... | collective-permute-start | bytes 147464 | tf_op jit(solution)/shard_map/ppermute | solution.py:20
  26.4 27.0 %collective-permute-start.4 = (bf16[16,12,1,128]{3,1,0,2:T(8,128)(2,1)S(1)}, bf16[16,12,1,128]{3,1,0,2:T(8,128)(2,1)S(1)}, u32[]{:S(2)}, u32[]{:S(2)}) collective-permute-start(bf16[16,12,1,128]{3,1,0,2:T(8,128)(2,1)S(1)} %get-tuple-element.250), channel_id=1, source_target_pairs={{16,0},{32,16},{48,32},{64,48},{80,64},{96,80},{112,96},{128,112},... | collective-permute-start | bytes 147464 | tf_op jit(solution)/shard_map/ppermute | solution.py:20
  42.0 11.7 %collective-permute-start.5 = (bf16[12,12,1,128]{3,1,0,2:T(8,128)(2,1)S(1)}, bf16[12,12,1,128]{3,1,0,2:T(8,128)(2,1)S(1)}, u32[]{:S(2)}, u32[]{:S(2)}) collective-permute-start(bf16[12,12,1,128]{3,1,0,2:T(8,128)(2,1)S(1)} %get-tuple-element.245), channel_id=1, source_target_pairs={{112,0},{128,16},{144,32},{160,48},{176,64},{192,80},{208,96},{224... | collective-permute-start | bytes 110600 | tf_op jit(solution)/shard_map/ppermute | solution.py:20
  43.5 10.4 %collective-permute-start.6 = (bf16[12,16,1,128]{3,1,0,2:T(8,128)(2,1)S(1)}, bf16[12,16,1,128]{3,1,0,2:T(8,128)(2,1)S(1)}, u32[]{:S(2)}, u32[]{:S(2)}) collective-permute-start(bf16[12,16,1,128]{3,1,0,2:T(8,128)(2,1)S(1)} %get-tuple-element.248), channel_id=1, source_target_pairs={{128,0},{144,16},{160,32},{176,48},{192,64},{208,80},{224,96},{240... | collective-permute-start | bytes 147464 | tf_op jit(solution)/shard_map/ppermute | solution.py:20
  48.4 7.6 %collective-permute-start.7 = (bf16[12,12,1,128]{3,1,0,2:T(8,128)(2,1)S(1)}, bf16[12,12,1,128]{3,1,0,2:T(8,128)(2,1)S(1)}, u32[]{:S(2)}, u32[]{:S(2)}) collective-permute-start(bf16[12,12,1,128]{3,1,0,2:T(8,128)(2,1)S(1)} %get-tuple-element.244), channel_id=1, source_target_pairs={{144,0},{160,16},{176,32},{192,48},{208,64},{224,80},{240,96},{256... | collective-permute-start | bytes 110600 | tf_op jit(solution)/shard_map/ppermute | solution.py:20
  60.8 9.7 %collective-permute-start.8 = (bf16[12,12,1,128]{3,1,0,2:T(8,128)(2,1)S(1)}, bf16[12,12,1,128]{3,1,0,2:T(8,128)(2,1)S(1)}, u32[]{:S(2)}, u32[]{:S(2)}) collective-permute-start(bf16[12,12,1,128]{3,1,0,2:T(8,128)(2,1)S(1)} %get-tuple-element.239), channel_id=1, source_target_pairs={{144,0},{160,16},{176,32},{192,48},{208,64},{224,80},{240,96},{256... | collective-permute-start | bytes 110600 | tf_op jit(solution)/shard_map/ppermute | solution.py:20
  62.2 15.8 %collective-permute-start.9 = (bf16[12,16,1,128]{3,1,0,2:T(8,128)(2,1)S(1)}, bf16[12,16,1,128]{3,1,0,2:T(8,128)(2,1)S(1)}, u32[]{:S(2)}, u32[]{:S(2)}) collective-permute-start(bf16[12,16,1,128]{3,1,0,2:T(8,128)(2,1)S(1)} %get-tuple-element.241), channel_id=1, source_target_pairs={{128,0},{144,16},{160,32},{176,48},{192,64},{208,80},{224,96},{240... | collective-permute-start | bytes 147464 | tf_op jit(solution)/shard_map/ppermute | solution.py:20
  63.5 21.3 %collective-permute-start.10 = (bf16[12,12,1,128]{3,1,0,2:T(8,128)(2,1)S(1)}, bf16[12,12,1,128]{3,1,0,2:T(8,128)(2,1)S(1)}, u32[]{:S(2)}, u32[]{:S(2)}) collective-permute-start(bf16[12,12,1,128]{3,1,0,2:T(8,128)(2,1)S(1)} %get-tuple-element.238), channel_id=1, source_target_pairs={{112,0},{128,16},{144,32},{160,48},{176,64},{192,80},{208,96},{224... | collective-permute-start | bytes 110600 | tf_op jit(solution)/shard_map/ppermute | solution.py:20
  64.8 24.3 %collective-permute-start.11 = (bf16[16,12,1,128]{3,1,0,2:T(8,128)(2,1)S(1)}, bf16[16,12,1,128]{3,1,0,2:T(8,128)(2,1)S(1)}, u32[]{:S(2)}, u32[]{:S(2)}) collective-permute-start(bf16[16,12,1,128]{3,1,0,2:T(8,128)(2,1)S(1)} %get-tuple-element.243), channel_id=1, source_target_pairs={{16,0},{32,16},{48,32},{64,48},{80,64},{96,80},{112,96},{128,112},... | collective-permute-start | bytes 147464 | tf_op jit(solution)/shard_map/ppermute | solution.py:20
  67.4 21.9 %collective-permute-start.12 = (bf16[16,12,1,128]{3,1,0,2:T(8,128)(2,1)S(1)}, bf16[16,12,1,128]{3,1,0,2:T(8,128)(2,1)S(1)}, u32[]{:S(2)}, u32[]{:S(2)}) collective-permute-start(bf16[16,12,1,128]{3,1,0,2:T(8,128)(2,1)S(1)} %get-tuple-element.242), channel_id=1, source_target_pairs={{0,16},{16,32},{32,48},{48,64},{64,80},{80,96},{96,112},{112,128},... | collective-permute-start | bytes 147464 | tf_op jit(solution)/shard_map/ppermute | solution.py:20
  70.5 19.0 %collective-permute-start.13 = (bf16[12,12,1,128]{3,1,0,2:T(8,128)(2,1)S(1)}, bf16[12,12,1,128]{3,1,0,2:T(8,128)(2,1)S(1)}, u32[]{:S(2)}, u32[]{:S(2)}) collective-permute-start(bf16[12,12,1,128]{3,1,0,2:T(8,128)(2,1)S(1)} %get-tuple-element.237), channel_id=1, source_target_pairs={{0,112},{16,128},{32,144},{48,160},{64,176},{80,192},{96,208},{112... | collective-permute-start | bytes 110600 | tf_op jit(solution)/shard_map/ppermute | solution.py:20
  78.0 14.9 %collective-permute-start.14 = (bf16[12,16,1,128]{3,1,0,2:T(8,128)(2,1)S(1)}, bf16[12,16,1,128]{3,1,0,2:T(8,128)(2,1)S(1)}, u32[]{:S(2)}, u32[]{:S(2)}) collective-permute-start(bf16[12,16,1,128]{3,1,0,2:T(8,128)(2,1)S(1)} %get-tuple-element.240), channel_id=1, source_target_pairs={{0,128},{16,144},{32,160},{48,176},{64,192},{80,208},{96,224},{112... | collective-permute-start | bytes 147464 | tf_op jit(solution)/shard_map/ppermute | solution.py:20
  84.8 8.2 %collective-permute-start.15 = (bf16[12,12,1,128]{3,1,0,2:T(8,128)(2,1)S(1)}, bf16[12,12,1,128]{3,1,0,2:T(8,128)(2,1)S(1)}, u32[]{:S(2)}, u32[]{:S(2)}) collective-permute-start(bf16[12,12,1,128]{3,1,0,2:T(8,128)(2,1)S(1)} %get-tuple-element.236), channel_id=1, source_target_pairs={{0,144},{16,160},{32,176},{48,192},{64,208},{80,224},{96,240},{112... | collective-permute-start | bytes 110600 | tf_op jit(solution)/shard_map/ppermute | solution.py:20
  93.0 1.7 copy-start.1
  94.6 266.5 %reduce-scatter.5.cloned.1.call-start = ((), (), s32[]{:S(2)}) async-start(), calls=%async_computation.2 | async-start | bytes 557056 | tf_op jit(solution)/shard_map/reduce_scatter | solution.py:159
  (1 other events, 0.8 us)
Sparse Core Ops, SparseCore 0:
  94.8 149.6 reduce-scatter.6
  249.1 112.0 reduce-scatter.4
where the time goes:
time: 370 us; the launch traced here: 368 us
  waiting for transfers between devices  266 us (72%)
  starting transfers between devices  49.7 us (13%)
  between operations  19.9 us (5%)
  local copies, waits for them, and re-layouts  17.2 us (5%)
  other arithmetic  9.63 us (3%)
  matrix products  5.95 us (2%)
    unnamed x3, waiting for transfers between devices  149 us
    reduce_scatter x1, waiting for transfers between devices, shards(): lax.psum_scatter(partial_value.astype(jnp.bfloat16), 'head', scatter_dime...  115 us
    ppermute x16, starting transfers between devices, passed_along(): lax.ppermute(value, axis, [(source, source + steps) for source in range(f...  49.6 us
    another operation x11, other arithmetic  8.14 us
  transfers between devices with their start and end apart: 18, of which 3 were waited for; matrix products, arithmetic and copies ran while one was open for 6% of the time, Pallas kernels for 0%

commit v1 on v0

--- a/solution.py
+++ b/solution.py
@@ -12,6 +12,15 @@
 
 directions = ((-1, -1), (-1, 0), (-1, 1), (0, -1), (0, 1), (1, -1), (1, 0), (1, 1))
 band_height = 16
+NEAR = 4
+HIGH = 4
+near_groups = [[high * NEAR + near for near in range(NEAR)] for high in range(HIGH)]
+far_groups = [[high * NEAR + near for high in range(HIGH)] for near in range(NEAR)]
+
+
+def summed_exchange(chunks, axis, groups):
+    received = lax.all_to_all(chunks, axis, 0, 0, axis_index_groups=groups)
+    return jnp.sum(received.astype(jnp.float32), axis=0)
 
 
 def passed_along(value, axis, steps):
@@ -147,18 +156,19 @@
         .reshape(side * side, local_heads * 3 * head_width)
         .astype(jnp.bfloat16)
     )
-    grad_w = lax.psum_scatter(
-        lax.dot_general(
-            tokens, grad_qkv, (((0,), (0,)), ((), ())), preferred_element_type=jnp.float32
-        ).astype(jnp.bfloat16),
-        "tile",
-        scatter_dimension=0,
-        tiled=True,
-    ).astype(jnp.float32)
-    partial_value = jnp.dot(grad_qkv, w_qkv, preferred_element_type=jnp.float32)
-    grad_x = lax.psum_scatter(
-        partial_value.astype(jnp.bfloat16), "head", scatter_dimension=0, tiled=True
+    grad_w_term = lax.dot_general(
+        tokens, grad_qkv, (((0,), (0,)), ((), ())), preferred_element_type=jnp.float32
+    ).astype(jnp.bfloat16)
+    grad_w = summed_exchange(grad_w_term.reshape(tiles, D // tiles, -1), "tile", None)
+    rows = side * side // HEADS
+    by_owner = grad_qkv.reshape(HIGH, NEAR, rows, -1).transpose(1, 0, 2, 3).reshape(side * side, -1)
+    partial_value = jnp.dot(by_owner, w_qkv, preferred_element_type=jnp.float32)
+    near_sum = summed_exchange(
+        partial_value.astype(jnp.bfloat16).reshape(NEAR, HIGH * rows, D), "head", near_groups
     )
+    grad_x = summed_exchange(
+        near_sum.astype(jnp.bfloat16).reshape(HIGH, rows, D), "head", far_groups
+    ).astype(jnp.bfloat16)
     return (grad_x, grad_w)
 
 

time: 370 us -> 151 us (0.41)
  waiting for transfers between devices: 266 us -> 28.6 us
  starting transfers between devices: 49.7 us -> 69.4 us
  between operations: 19.9 us -> 6.58 us
  blocking collectives: 0 us -> 12.7 us
    unnamed x3 -> x0, waiting for transfers between devices: 149 us -> none
    reduce_scatter x1 -> x0, waiting for transfers between devices: 115 us -> none  [shards(): lax.psum_scatter(partial_value.astype(jnp.bfloat16), 'head', scatter_dime...]
    all_to_all x0 -> x2, waiting for transfers between devices: none -> 26.7 us  [summed_exchange(): received = lax.all_to_all(chunks, axis, 0, 0, axis_index_groups=groups)]
    all_to_all x0 -> x2, starting transfers between devices: none -> 19.8 us  [summed_exchange(): received = lax.all_to_all(chunks, axis, 0, 0, axis_index_groups=groups)]
    all_to_all x0 -> x1, blocking collectives: none -> 12.7 us  [summed_exchange(): received = lax.all_to_all(chunks, axis, 0, 0, axis_index_groups=groups)]
  transfers between devices with their start and end apart: 18 -> 18, of which waited for: 3 -> 3; matrix products, arithmetic and copies ran while one was open for 6% -> 15% of each run, Pallas kernels for 0% -> 0%
where the time goes in v1:
time: 151 us; the launch traced here: 150 us
  starting transfers between devices  69.4 us (46%)
  waiting for transfers between devices  28.6 us (19%)
  local copies, waits for them, and re-layouts  15.9 us (11%)
  blocking collectives  12.7 us (8%)
  other arithmetic  11.6 us (8%)
  between operations  6.58 us (4%)
  matrix products  5.11 us (3%)
    ppermute x16, starting transfers between devices, passed_along(): lax.ppermute(value, axis, [(source, source + steps) for source in range(f...  49.6 us
    all_to_all x2, waiting for transfers between devices, summed_exchange(): received = lax.all_to_all(chunks, axis, 0, 0, axis_index_groups=groups)  26.7 us
    all_to_all x2, starting transfers between devices, summed_exchange(): received = lax.all_to_all(chunks, axis, 0, 0, axis_index_groups=groups)  19.8 us
    all_to_all x1, blocking collectives, summed_exchange(): received = lax.all_to_all(chunks, axis, 0, 0, axis_index_groups=groups)  12.7 us
    another operation x11, other arithmetic  7.93 us
    scatter x8, local copies, waits for them, and re-layouts, shards(): region = region.at[into_top:into_bottom, into_left:into_right].set(moved)  4.51 us
  transfers between devices with their start and end apart: 18, of which 3 were waited for; matrix products, arithmetic and copies ran while one was open for 15% of the time, Pallas kernels for 0%

profile of v1, /device:TPU:1, one launch (start us, length us, event | category | flops | bytes accessed | tf_op | source)
XLA Modules:
  0.0 149.9 jit_solution(16401291053183177139)
XLA Ops:
  1.7 1.3 convolution_convert_fusion.2
  3.3 5.8 %collective-permute-start = (bf16[12,12,1,128]{3,1,0,2:T(8,128)(2,1)S(1)}, bf16[12,12,1,128]{3,1,0,2:T(8,128)(2,1)S(1)}, u32[]{:S(2)}, u32[]{:S(2)}) collective-permute-start(bf16[12,12,1,128]{3,1,0,2:T(8,128)(2,1)S(1)} %get-tuple-element.241), channel_id=1, source_target_pairs={{0,144},{16,160},{32,176},{48,192},{64,208},{80,224},{96,240},{112... | collective-permute-start | bytes 110600 | tf_op jit(solution)/shard_map/ppermute | solution.py:29
  9.2 3.6 %collective-permute-start.1 = (bf16[12,16,1,128]{3,1,0,2:T(8,128)(2,1)S(1)}, bf16[12,16,1,128]{3,1,0,2:T(8,128)(2,1)S(1)}, u32[]{:S(2)}, u32[]{:S(2)}) collective-permute-start(bf16[12,16,1,128]{3,1,0,2:T(8,128)(2,1)S(1)} %get-tuple-element.243), channel_id=1, source_target_pairs={{0,128},{16,144},{32,160},{48,176},{64,192},{80,208},{96,224},{112... | collective-permute-start | bytes 147464 | tf_op jit(solution)/shard_map/ppermute | solution.py:29
  12.8 2.6 %collective-permute-start.2 = (bf16[12,12,1,128]{3,1,0,2:T(8,128)(2,1)S(1)}, bf16[12,12,1,128]{3,1,0,2:T(8,128)(2,1)S(1)}, u32[]{:S(2)}, u32[]{:S(2)}) collective-permute-start(bf16[12,12,1,128]{3,1,0,2:T(8,128)(2,1)S(1)} %get-tuple-element.240), channel_id=1, source_target_pairs={{0,112},{16,128},{32,144},{48,160},{64,176},{80,192},{96,208},{112... | collective-permute-start | bytes 110600 | tf_op jit(solution)/shard_map/ppermute | solution.py:29
  15.5 4.3 %collective-permute-start.3 = (bf16[16,12,1,128]{3,1,0,2:T(8,128)(2,1)S(1)}, bf16[16,12,1,128]{3,1,0,2:T(8,128)(2,1)S(1)}, u32[]{:S(2)}, u32[]{:S(2)}) collective-permute-start(bf16[16,12,1,128]{3,1,0,2:T(8,128)(2,1)S(1)} %get-tuple-element.245), channel_id=1, source_target_pairs={{0,16},{16,32},{32,48},{48,64},{64,80},{80,96},{96,112},{112,128},... | collective-permute-start | bytes 147464 | tf_op jit(solution)/shard_map/ppermute | solution.py:29
  19.8 1.9 %collective-permute-start.4 = (bf16[16,12,1,128]{3,1,0,2:T(8,128)(2,1)S(1)}, bf16[16,12,1,128]{3,1,0,2:T(8,128)(2,1)S(1)}, u32[]{:S(2)}, u32[]{:S(2)}) collective-permute-start(bf16[16,12,1,128]{3,1,0,2:T(8,128)(2,1)S(1)} %get-tuple-element.244), channel_id=1, source_target_pairs={{16,0},{32,16},{48,32},{64,48},{80,64},{96,80},{112,96},{128,112},... | collective-permute-start | bytes 147464 | tf_op jit(solution)/shard_map/ppermute | solution.py:29
  32.6 2.0 %and.331 = pred[256,1600]{1,0:T(32,128)(4,1)S(1)} reshape(pred[16,16,40,40]{3,2,1,0:T(8,128)(4,1)S(1)} %broadcast_and_fusion) | data formatting | bytes 819200 | tf_op jit(solution)/shard_map/and | solution.py:68
  38.2 2.0 %dynamic-slice_select_fusion.1 = bf16[12,16,1,128]{3,1,0,2:T(8,128)(2,1)S(1)} fusion(bf16[12,16,1,128]{3,1,0,2:T(8,128)(2,1)S(1)} %collective-permute-done.1, bf16[40,40,1,128]{3,1,0,2:T(8,128)(2,1)S(1)} %scatter.31, s32[]{:T(128)} %bitcast.1, s32[]{:T(128)} %bitcast.2, pred[]{:T(512)} %and_reduce_fusion.2), kind=kLoop, calls=%fused_computation.40 | loop fusion | flops 24576 | bytes 147465 | tf_op jit(solution)/shard_map/select.20
  40.1 1.5 %scatter.34 = bf16[40,40,1,128]{3,1,0,2:T(8,128)(2,1)S(1)} dynamic-update-slice(bf16[40,40,1,128]{3,1,0,2:T(8,128)(2,1)S(1)} %scatter.31, bf16[12,16,1,128]{3,1,0,2:T(8,128)(2,1)S(1)} %dynamic-slice_select_fusion.1, s32[]{:T(128)} %bitcast.1, s32[]{:T(128)} %bitcast.2, s32[]{:T(128)} %constant.570.clone.1, s32[]{:T(128)} %constant.570.clone.1) | dynamic-update-slice | bytes 98308 | tf_op jit(solution)/shard_map/scatter | solution.py:125
  43.0 1.8 %dynamic-slice_select_fusion = bf16[12,12,1,128]{3,1,0,2:T(8,128)(2,1)S(1)} fusion(bf16[12,12,1,128]{3,1,0,2:T(8,128)(2,1)S(1)} %collective-permute-done.2, bf16[40,40,1,128]{3,1,0,2:T(8,128)(2,1)S(1)} %scatter.34, s32[]{:T(128)} %bitcast.3, s32[]{:T(128)} %bitcast.4, pred[]{:T(512)} %and_reduce_fusion.1), kind=kLoop, calls=%fused_computation.39 | loop fusion | flops 18432 | bytes 110601 | tf_op jit(solution)/shard_map/select.21
  44.8 1.5 scatter.35
  47.4 1.9 %collective-permute-done.7 = bf16[12,12,1,128]{3,1,0,2:T(8,128)(2,1)S(1)} collective-permute-done((bf16[12,12,1,128]{3,1,0,2:T(8,128)(2,1)S(1)}, bf16[12,12,1,128]{3,1,0,2:T(8,128)(2,1)S(1)}, u32[]{:S(2)}, u32[]{:S(2)}) %collective-permute-start.7) | collective-permute-done | bytes 36896 | tf_op jit(solution)/shard_map/ppermute | solution.py:29
  58.1 2.6 %collective-permute-start.11 = (bf16[16,12,1,128]{3,1,0,2:T(8,128)(2,1)S(1)}, bf16[16,12,1,128]{3,1,0,2:T(8,128)(2,1)S(1)}, u32[]{:S(2)}, u32[]{:S(2)}) collective-permute-start(bf16[16,12,1,128]{3,1,0,2:T(8,128)(2,1)S(1)} %get-tuple-element.237), channel_id=1, source_target_pairs={{16,0},{32,16},{48,32},{64,48},{80,64},{96,80},{112,96},{128,112},... | collective-permute-start | bytes 147464 | tf_op jit(solution)/shard_map/ppermute | solution.py:29
  60.7 3.0 %collective-permute-start.12 = (bf16[16,12,1,128]{3,1,0,2:T(8,128)(2,1)S(1)}, bf16[16,12,1,128]{3,1,0,2:T(8,128)(2,1)S(1)}, u32[]{:S(2)}, u32[]{:S(2)}) collective-permute-start(bf16[16,12,1,128]{3,1,0,2:T(8,128)(2,1)S(1)} %get-tuple-element.236), channel_id=1, source_target_pairs={{0,16},{16,32},{32,48},{48,64},{64,80},{80,96},{96,112},{112,128},... | collective-permute-start | bytes 147464 | tf_op jit(solution)/shard_map/ppermute | solution.py:29
  63.8 7.3 %collective-permute-start.13 = (bf16[12,12,1,128]{3,1,0,2:T(8,128)(2,1)S(1)}, bf16[12,12,1,128]{3,1,0,2:T(8,128)(2,1)S(1)}, u32[]{:S(2)}, u32[]{:S(2)}) collective-permute-start(bf16[12,12,1,128]{3,1,0,2:T(8,128)(2,1)S(1)} %get-tuple-element.231), channel_id=1, source_target_pairs={{0,112},{16,128},{32,144},{48,160},{64,176},{80,192},{96,208},{112... | collective-permute-start | bytes 110600 | tf_op jit(solution)/shard_map/ppermute | solution.py:29
  71.4 6.7 %collective-permute-start.14 = (bf16[12,16,1,128]{3,1,0,2:T(8,128)(2,1)S(1)}, bf16[12,16,1,128]{3,1,0,2:T(8,128)(2,1)S(1)}, u32[]{:S(2)}, u32[]{:S(2)}) collective-permute-start(bf16[12,16,1,128]{3,1,0,2:T(8,128)(2,1)S(1)} %get-tuple-element.234), channel_id=1, source_target_pairs={{0,128},{16,144},{32,160},{48,176},{64,192},{80,208},{96,224},{112... | collective-permute-start | bytes 147464 | tf_op jit(solution)/shard_map/ppermute | solution.py:29
  78.2 4.0 %collective-permute-start.15 = (bf16[12,12,1,128]{3,1,0,2:T(8,128)(2,1)S(1)}, bf16[12,12,1,128]{3,1,0,2:T(8,128)(2,1)S(1)}, u32[]{:S(2)}, u32[]{:S(2)}) collective-permute-start(bf16[12,12,1,128]{3,1,0,2:T(8,128)(2,1)S(1)} %get-tuple-element.230), channel_id=1, source_target_pairs={{0,144},{16,160},{32,176},{48,192},{64,208},{80,224},{96,240},{112... | collective-permute-start | bytes 110600 | tf_op jit(solution)/shard_map/ppermute | solution.py:29
  82.9 2.0 %add_select_fusion = f32[12,12,1,128]{3,1,0,2:T(8,128)S(1)} fusion(bf16[12,12,1,128]{3,1,0,2:T(8,128)(2,1)S(1)} %collective-permute-done.13, f32[16,16,1,128]{3,1,0,2:T(8,128)S(1)} %scatter-add.34, s32[]{:T(128)} %bitcast.30, s32[]{:T(128)} %bitcast.31, pred[]{:T(512)} %and_reduce_fusion), kind=kLoop, calls=%fused_computation.27 | loop fusion | flops 55296 | bytes 184329 | tf_op jit(solution)/shard_map/select.33
  84.9 1.6 %scatter-add.35 = f32[16,16,1,128]{3,1,0,2:T(8,128)S(1)} dynamic-update-slice(f32[16,16,1,128]{3,1,0,2:T(8,128)S(1)} %scatter-add.34, f32[12,12,1,128]{3,1,0,2:T(8,128)S(1)} %add_select_fusion, s32[]{:T(128)} %bitcast.30, s32[]{:T(128)} %bitcast.31, s32[]{:T(128)} %constant.570.clone.1, s32[]{:T(128)} %constant.570.clone.1) | dynamic-update-slice | bytes 147460 | tf_op jit(solution)/shard_map/scatter-add | solution.py:153
  87.1 12.7 %all_to_all.15 = bf16[4,64,1024]{2,1,0:T(8,128)(2,1)S(1)} all-to-all(bf16[4,64,1024]{2,1,0:T(8,128)(2,1)S(1)} %bitcast.98), channel_id=1, replica_groups={{0,1,2,3},{4,5,6,7},{8,9,10,11},{12,13,14,15},{16,17,18,19},{20,21,22,2..., dimensions={0} | all-to-all | bytes 1048576 | tf_op jit(solution)/shard_map/all_to_all | solution.py:22
  100.5 12.1 %all-to-all-start.1 = ((bf16[4,16,1024]{2,1,0:T(8,128)(2,1)}), bf16[4,16,1024]{2,1,0:T(8,128)(2,1)S(1)}, u32[]{:S(2)}, u32[]{:S(2)}) async-start(bf16[4,16,1024]{2,1,0:T(8,128)(2,1)} %bitcast.36), calls=%async_computation.1 | async-start | bytes 262144 | tf_op jit(solution)/shard_map/all_to_all | solution.py:22
  114.1 10.9 %all-to-all-done.1 = bf16[4,16,1024]{2,1,0:T(8,128)(2,1)S(1)} async-done(((bf16[4,16,1024]{2,1,0:T(8,128)(2,1)}), bf16[4,16,1024]{2,1,0:T(8,128)(2,1)S(1)}, u32[]{:S(2)}, u32[]{:S(2)}) %all-to-all-start.1) | async-done | bytes 131104 | tf_op jit(solution)/shard_map/all_to_all | solution.py:22
  125.0 7.7 %all-to-all-start.2 = ((bf16[32,32,192]{2,1,0:T(8,128)(2,1)}), bf16[32,32,192]{2,1,0:T(8,128)(2,1)S(1)}, u32[]{:S(2)}, u32[]{:S(2)}) async-start(bf16[32,32,192]{2,1,0:T(8,128)(2,1)} %bitcast.41), calls=%async_computation.2 | async-start | bytes 1048576 | tf_op jit(solution)/shard_map/all_to_all | solution.py:22
  133.4 15.8 %all-to-all-done.2 = bf16[32,32,192]{2,1,0:T(8,128)(2,1)S(1)} async-done(((bf16[32,32,192]{2,1,0:T(8,128)(2,1)}), bf16[32,32,192]{2,1,0:T(8,128)(2,1)S(1)}, u32[]{:S(2)}, u32[]{:S(2)}) %all-to-all-start.2) | async-done | bytes 393248 | tf_op jit(solution)/shard_map/all_to_all | solution.py:22
  (103 shorter events, 26.8 us)
Async XLA Ops:
  0.6 1.1 copy-start
  0.6 22.5 %copy-start.6 = (s32[4]{0:T(128)S(1)}, s32[4]{0:T(128)}, u32[]{:S(2)}) copy-start(s32[4]{0:T(128)} %constant.573.clone.1) | copy-start | bytes 52
  0.7 23.2 %copy-start.5 = (s32[4]{0:T(128)S(1)}, s32[4]{0:T(128)}, u32[]{:S(2)}) copy-start(s32[4]{0:T(128)} %constant.576.clone.1) | copy-start | bytes 52
  0.7 30.3 %copy-start.4 = (s32[4]{0:T(128)S(1)}, s32[4]{0:T(128)}, u32[]{:S(2)}) copy-start(s32[4]{0:T(128)} %constant.591.clone.1) | copy-start | bytes 52
  0.7 24.5 %copy-start.3 = (s32[1,8]{1,0:T(1,128)S(1)}, s32[1,8]{1,0:T(1,128)}, u32[]{:S(2)}) copy-start(s32[1,8]{1,0:T(1,128)} %param.45) | copy-start | bytes 100
  3.3 32.0 %collective-permute-start = (bf16[12,12,1,128]{3,1,0,2:T(8,128)(2,1)S(1)}, bf16[12,12,1,128]{3,1,0,2:T(8,128)(2,1)S(1)}, u32[]{:S(2)}, u32[]{:S(2)}) collective-permute-start(bf16[12,12,1,128]{3,1,0,2:T(8,128)(2,1)S(1)} %get-tuple-element.241), channel_id=1, source_target_pairs={{0,144},{16,160},{32,176},{48,192},{64,208},{80,224},{96,240},{112... | collective-permute-start | bytes 110600 | tf_op jit(solution)/shard_map/ppermute | solution.py:29
  9.2 27.6 %collective-permute-start.1 = (bf16[12,16,1,128]{3,1,0,2:T(8,128)(2,1)S(1)}, bf16[12,16,1,128]{3,1,0,2:T(8,128)(2,1)S(1)}, u32[]{:S(2)}, u32[]{:S(2)}) collective-permute-start(bf16[12,16,1,128]{3,1,0,2:T(8,128)(2,1)S(1)} %get-tuple-element.243), channel_id=1, source_target_pairs={{0,128},{16,144},{32,160},{48,176},{64,192},{80,208},{96,224},{112... | collective-permute-start | bytes 147464 | tf_op jit(solution)/shard_map/ppermute | solution.py:29
  12.8 28.9 %collective-permute-start.2 = (bf16[12,12,1,128]{3,1,0,2:T(8,128)(2,1)S(1)}, bf16[12,12,1,128]{3,1,0,2:T(8,128)(2,1)S(1)}, u32[]{:S(2)}, u32[]{:S(2)}) collective-permute-start(bf16[12,12,1,128]{3,1,0,2:T(8,128)(2,1)S(1)} %get-tuple-element.240), channel_id=1, source_target_pairs={{0,112},{16,128},{32,144},{48,160},{64,176},{80,192},{96,208},{112... | collective-permute-start | bytes 110600 | tf_op jit(solution)/shard_map/ppermute | solution.py:29
  15.5 30.8 %collective-permute-start.3 = (bf16[16,12,1,128]{3,1,0,2:T(8,128)(2,1)S(1)}, bf16[16,12,1,128]{3,1,0,2:T(8,128)(2,1)S(1)}, u32[]{:S(2)}, u32[]{:S(2)}) collective-permute-start(bf16[16,12,1,128]{3,1,0,2:T(8,128)(2,1)S(1)} %get-tuple-element.245), channel_id=1, source_target_pairs={{0,16},{16,32},{32,48},{48,64},{64,80},{80,96},{96,112},{112,128},... | collective-permute-start | bytes 147464 | tf_op jit(solution)/shard_map/ppermute | solution.py:29
  19.8 26.8 %collective-permute-start.4 = (bf16[16,12,1,128]{3,1,0,2:T(8,128)(2,1)S(1)}, bf16[16,12,1,128]{3,1,0,2:T(8,128)(2,1)S(1)}, u32[]{:S(2)}, u32[]{:S(2)}) collective-permute-start(bf16[16,12,1,128]{3,1,0,2:T(8,128)(2,1)S(1)} %get-tuple-element.244), channel_id=1, source_target_pairs={{16,0},{32,16},{48,32},{64,48},{80,64},{96,80},{112,96},{128,112},... | collective-permute-start | bytes 147464 | tf_op jit(solution)/shard_map/ppermute | solution.py:29
  35.3 11.6 %collective-permute-start.5 = (bf16[12,12,1,128]{3,1,0,2:T(8,128)(2,1)S(1)}, bf16[12,12,1,128]{3,1,0,2:T(8,128)(2,1)S(1)}, u32[]{:S(2)}, u32[]{:S(2)}) collective-permute-start(bf16[12,12,1,128]{3,1,0,2:T(8,128)(2,1)S(1)} %get-tuple-element.239), channel_id=1, source_target_pairs={{112,0},{128,16},{144,32},{160,48},{176,64},{192,80},{208,96},{224... | collective-permute-start | bytes 110600 | tf_op jit(solution)/shard_map/ppermute | solution.py:29
  36.9 10.3 %collective-permute-start.6 = (bf16[12,16,1,128]{3,1,0,2:T(8,128)(2,1)S(1)}, bf16[12,16,1,128]{3,1,0,2:T(8,128)(2,1)S(1)}, u32[]{:S(2)}, u32[]{:S(2)}) collective-permute-start(bf16[12,16,1,128]{3,1,0,2:T(8,128)(2,1)S(1)} %get-tuple-element.242), channel_id=1, source_target_pairs={{128,0},{144,16},{160,32},{176,48},{192,64},{208,80},{224,96},{240... | collective-permute-start | bytes 147464 | tf_op jit(solution)/shard_map/ppermute | solution.py:29
  41.7 7.6 %collective-permute-start.7 = (bf16[12,12,1,128]{3,1,0,2:T(8,128)(2,1)S(1)}, bf16[12,12,1,128]{3,1,0,2:T(8,128)(2,1)S(1)}, u32[]{:S(2)}, u32[]{:S(2)}) collective-permute-start(bf16[12,12,1,128]{3,1,0,2:T(8,128)(2,1)S(1)} %get-tuple-element.238), channel_id=1, source_target_pairs={{144,0},{160,16},{176,32},{192,48},{208,64},{224,80},{240,96},{256... | collective-permute-start | bytes 110600 | tf_op jit(solution)/shard_map/ppermute | solution.py:29
  54.2 9.7 %collective-permute-start.8 = (bf16[12,12,1,128]{3,1,0,2:T(8,128)(2,1)S(1)}, bf16[12,12,1,128]{3,1,0,2:T(8,128)(2,1)S(1)}, u32[]{:S(2)}, u32[]{:S(2)}) collective-permute-start(bf16[12,12,1,128]{3,1,0,2:T(8,128)(2,1)S(1)} %get-tuple-element.233), channel_id=1, source_target_pairs={{144,0},{160,16},{176,32},{192,48},{208,64},{224,80},{240,96},{256... | collective-permute-start | bytes 110600 | tf_op jit(solution)/shard_map/ppermute | solution.py:29
  55.5 15.8 %collective-permute-start.9 = (bf16[12,16,1,128]{3,1,0,2:T(8,128)(2,1)S(1)}, bf16[12,16,1,128]{3,1,0,2:T(8,128)(2,1)S(1)}, u32[]{:S(2)}, u32[]{:S(2)}) collective-permute-start(bf16[12,16,1,128]{3,1,0,2:T(8,128)(2,1)S(1)} %get-tuple-element.235), channel_id=1, source_target_pairs={{128,0},{144,16},{160,32},{176,48},{192,64},{208,80},{224,96},{240... | collective-permute-start | bytes 147464 | tf_op jit(solution)/shard_map/ppermute | solution.py:29
  56.8 21.3 %collective-permute-start.10 = (bf16[12,12,1,128]{3,1,0,2:T(8,128)(2,1)S(1)}, bf16[12,12,1,128]{3,1,0,2:T(8,128)(2,1)S(1)}, u32[]{:S(2)}, u32[]{:S(2)}) collective-permute-start(bf16[12,12,1,128]{3,1,0,2:T(8,128)(2,1)S(1)} %get-tuple-element.232), channel_id=1, source_target_pairs={{112,0},{128,16},{144,32},{160,48},{176,64},{192,80},{208,96},{224... | collective-permute-start | bytes 110600 | tf_op jit(solution)/shard_map/ppermute | solution.py:29
  58.1 24.3 %collective-permute-start.11 = (bf16[16,12,1,128]{3,1,0,2:T(8,128)(2,1)S(1)}, bf16[16,12,1,128]{3,1,0,2:T(8,128)(2,1)S(1)}, u32[]{:S(2)}, u32[]{:S(2)}) collective-permute-start(bf16[16,12,1,128]{3,1,0,2:T(8,128)(2,1)S(1)} %get-tuple-element.237), channel_id=1, source_target_pairs={{16,0},{32,16},{48,32},{64,48},{80,64},{96,80},{112,96},{128,112},... | collective-permute-start | bytes 147464 | tf_op jit(solution)/shard_map/ppermute | solution.py:29
  60.7 22.0 %collective-permute-start.12 = (bf16[16,12,1,128]{3,1,0,2:T(8,128)(2,1)S(1)}, bf16[16,12,1,128]{3,1,0,2:T(8,128)(2,1)S(1)}, u32[]{:S(2)}, u32[]{:S(2)}) collective-permute-start(bf16[16,12,1,128]{3,1,0,2:T(8,128)(2,1)S(1)} %get-tuple-element.236), channel_id=1, source_target_pairs={{0,16},{16,32},{32,48},{48,64},{64,80},{80,96},{96,112},{112,128},... | collective-permute-start | bytes 147464 | tf_op jit(solution)/shard_map/ppermute | solution.py:29
  63.8 19.1 %collective-permute-start.13 = (bf16[12,12,1,128]{3,1,0,2:T(8,128)(2,1)S(1)}, bf16[12,12,1,128]{3,1,0,2:T(8,128)(2,1)S(1)}, u32[]{:S(2)}, u32[]{:S(2)}) collective-permute-start(bf16[12,12,1,128]{3,1,0,2:T(8,128)(2,1)S(1)} %get-tuple-element.231), channel_id=1, source_target_pairs={{0,112},{16,128},{32,144},{48,160},{64,176},{80,192},{96,208},{112... | collective-permute-start | bytes 110600 | tf_op jit(solution)/shard_map/ppermute | solution.py:29
  71.4 15.1 %collective-permute-start.14 = (bf16[12,16,1,128]{3,1,0,2:T(8,128)(2,1)S(1)}, bf16[12,16,1,128]{3,1,0,2:T(8,128)(2,1)S(1)}, u32[]{:S(2)}, u32[]{:S(2)}) collective-permute-start(bf16[12,16,1,128]{3,1,0,2:T(8,128)(2,1)S(1)} %get-tuple-element.234), channel_id=1, source_target_pairs={{0,128},{16,144},{32,160},{48,176},{64,192},{80,208},{96,224},{112... | collective-permute-start | bytes 147464 | tf_op jit(solution)/shard_map/ppermute | solution.py:29
  78.2 8.3 %collective-permute-start.15 = (bf16[12,12,1,128]{3,1,0,2:T(8,128)(2,1)S(1)}, bf16[12,12,1,128]{3,1,0,2:T(8,128)(2,1)S(1)}, u32[]{:S(2)}, u32[]{:S(2)}) collective-permute-start(bf16[12,12,1,128]{3,1,0,2:T(8,128)(2,1)S(1)} %get-tuple-element.230), channel_id=1, source_target_pairs={{0,144},{16,160},{32,176},{48,192},{64,208},{80,224},{96,240},{112... | collective-permute-start | bytes 110600 | tf_op jit(solution)/shard_map/ppermute | solution.py:29
  82.2 4.6 %copy-start.1 = (bf16[192,1024]{1,0:T(8,128)(2,1)S(1)}, bf16[192,1024]{1,0:T(8,128)(2,1)}, u32[]{:S(2)}) copy-start(bf16[192,1024]{1,0:T(8,128)(2,1)} %param.43) | copy-start | bytes 1179652
  100.5 24.5 %all-to-all-start.1 = ((bf16[4,16,1024]{2,1,0:T(8,128)(2,1)}), bf16[4,16,1024]{2,1,0:T(8,128)(2,1)S(1)}, u32[]{:S(2)}, u32[]{:S(2)}) async-start(bf16[4,16,1024]{2,1,0:T(8,128)(2,1)} %bitcast.36), calls=%async_computation.1 | async-start | bytes 262144 | tf_op jit(solution)/shard_map/all_to_all | solution.py:22
  125.0 24.1 %all-to-all-start.2 = ((bf16[32,32,192]{2,1,0:T(8,128)(2,1)}), bf16[32,32,192]{2,1,0:T(8,128)(2,1)S(1)}, u32[]{:S(2)}, u32[]{:S(2)}) async-start(bf16[32,32,192]{2,1,0:T(8,128)(2,1)} %bitcast.41), calls=%async_computation.2 | async-start | bytes 1048576 | tf_op jit(solution)/shard_map/all_to_all | solution.py:22
  (1 other events, 0.8 us)

commit v2 on v1

v2 whole, which is shorter than its diff:
```python
import jax
import jax.numpy as jnp
from jax import lax
from jax.experimental import pallas as pl
from jax.experimental.pallas import tpu as pltpu
from jax.sharding import PartitionSpec as P

D = 1024
HEADS = 16
WIDTH = D // HEADS
HALO = 12
S = 16
GRID_ROWS = 4
GRID_COLS = 8
TILES = 32
OWN = S * S
RIM = HALO * S
COLUMN = OWN + 2 * RIM
NEAR = 4
HIGH = 4
BARRED = -1e30

directions = ((-1, -1), (-1, 0), (-1, 1), (0, -1), (0, 1), (1, -1), (1, 0), (1, 1))
near_groups = [[high * NEAR + near for near in range(NEAR)] for high in range(HIGH)]
far_groups = [[high * NEAR + near for high in range(HIGH)] for near in range(NEAR)]

down_pairs = [(tile, tile + GRID_COLS) for tile in range(TILES - GRID_COLS)]
up_pairs = [(target, source) for source, target in down_pairs]
right_pairs = [(tile, tile + 1) for tile in range(TILES) if tile % GRID_COLS < GRID_COLS - 1]
left_pairs = [(target, source) for source, target in right_pairs]


def summed_exchange(chunks, axis, groups):
    received = lax.all_to_all(chunks, axis, 0, 0, axis_index_groups=groups)
    return jnp.sum(received.astype(jnp.float32), axis=0)


def contract(left, right, left_axis, right_axis):
    return lax.dot_general(
        left, right, (((left_axis,), (right_axis,)), ((), ())), preferred_element_type=jnp.float32
    )


def usable(flags_ref, number, row_step, column_step):
    if (row_step, column_step) == (0, 0):
        return jnp.ones((), jnp.int32)
    grid_row = (number >> 3) + row_step
    grid_col = (number & 7) + column_step
    inside = (grid_row >= 0) & (grid_row < GRID_ROWS) & (grid_col >= 0) & (grid_col < GRID_COLS)
    flag = flags_ref[0, directions.index((row_step, column_step))]
    return jnp.where(inside, flag, 0)


def prepare_kernel(number_ref, flags_ref, tokens_ref, w_ref, query_ref, mask_ref):
    query = contract(w_ref[...], tokens_ref[...], 1, 1).astype(jnp.bfloat16)
    query_ref[:WIDTH, :] = query * jnp.bfloat16(WIDTH**-0.5)
    query_ref[WIDTH : 2 * WIDTH, :] = jnp.zeros((WIDTH, OWN), jnp.bfloat16)
    sublane = lax.broadcasted_iota(jnp.int32, (128, OWN), 0)
    place = lax.broadcasted_iota(jnp.int32, (128, OWN), 1)
    marks = (sublane == (place >> 4)) | (sublane == S + (place & 15)) | (sublane == 2 * S)
    query_ref[2 * WIDTH :, :] = jnp.where(marks, 1.0, 0.0).astype(jnp.bfloat16)
    place = lax.broadcasted_iota(jnp.int32, (COLUMN, 128), 0)
    lane = lax.broadcasted_iota(jnp.int32, (COLUMN, 128), 1)
    key_row = (place >> 4) - HALO
    key_column = place & 15
    far_row = (lane < S) & (jnp.abs(key_row - lane) > HALO)
    column_lane = (lane >= S) & (lane < 2 * S)
    number = number_ref[0]
    for block in range(3):
        offset = key_column + (block - 1) * S - lane + S
        far_column = column_lane & (jnp.abs(offset) > HALO)
        above, beside, below = (usable(flags_ref, number, step, block - 1) for step in (-1, 0, 1))
        flag = jnp.where(key_row < 0, above, jnp.where(key_row >= S, below, beside))
        closed = (lane == 2 * S) & (flag == 0)
        barred = jnp.where(far_row | far_column | closed, BARRED, 0.0)
        mask_ref[block] = barred.astype(jnp.bfloat16)


def prepare(number, flags, tokens, w_qkv):
    whole = lambda shape: pl.BlockSpec(shape, lambda i: (0,) * len(shape))
    return pl.pallas_call(
        prepare_kernel,
        grid=(1,),
        in_specs=[
            pl.BlockSpec(memory_space=pltpu.SMEM),
            pl.BlockSpec(memory_space=pltpu.SMEM),
            whole((OWN, D)),
            whole((WIDTH, D)),
        ],
        out_specs=[whole((256, OWN)), whole((3, COLUMN, 128))],
        out_shape=[
            jax.ShapeDtypeStruct((256, OWN), jnp.bfloat16),
            jax.ShapeDtypeStruct((3, COLUMN, 128), jnp.bfloat16),
        ],
        compiler_params=pltpu.CompilerParams(vmem_limit_bytes=8 << 20),
        name="prepare",
    )(number, flags, tokens, w_qkv)


def attend_kernel(
    query_ref, grad_ref, mask_ref, left_ref, centre_ref, right_ref,
    dquery_ref, dleft_ref, dcentre_ref, dright_ref, scores_ref, low_ref,
):
    pairs = (left_ref, centre_ref, right_ref)
    query = query_ref[...]
    grad = jnp.concatenate([jnp.zeros((WIDTH, OWN), jnp.bfloat16), grad_ref[...]], axis=0)
    highest = None
    for block in range(3):
        rows = pl.ds(block * COLUMN, COLUMN)
        keys = jnp.concatenate([pairs[block][...], mask_ref[block]], axis=1)
        scores = contract(keys, query, 1, 0)
        scores_ref[rows, :] = scores
        top = jnp.max(scores, axis=0, keepdims=True)
        highest = top if highest is None else jnp.maximum(highest, top)
    total = jnp.zeros((1, OWN), jnp.float32)
    for block in range(3):
        rows = pl.ds(block * COLUMN, COLUMN)
        lifted = jnp.exp(scores_ref[rows, :] - highest)
        scores_ref[rows, :] = lifted
        total = total + jnp.sum(lifted, axis=0, keepdims=True)
    inverse = 1.0 / total
    attended = jnp.zeros((128, OWN), jnp.float32)
    for block in range(3):
        rows = pl.ds(block * COLUMN, COLUMN)
        probs = scores_ref[rows, :] * inverse
        scores_ref[rows, :] = probs
        low = probs.astype(jnp.bfloat16)
        low_ref[rows, :] = low
        attended = attended + contract(pairs[block][...], low, 0, 0)
    row_dot = jnp.sum(attended * grad.astype(jnp.float32), axis=0, keepdims=True)
    dquery = jnp.zeros((128, OWN), jnp.float32)
    for block, out_ref in enumerate((dleft_ref, dcentre_ref, dright_ref)):
        rows = pl.ds(block * COLUMN, COLUMN)
        pair = pairs[block][...]
        grad_probs = contract(pair, grad, 1, 0)
        grad_scores = (scores_ref[rows, :] * (grad_probs - row_dot)).astype(jnp.bfloat16)
        dpair = contract(grad_scores, query[:128], 1, 1) + contract(low_ref[rows, :], grad, 1, 1)
        out_ref[...] = dpair.astype(out_ref.dtype)
        dquery = dquery + contract(pair, grad_scores, 0, 0)
    dquery_ref[...] = (dquery[:WIDTH] * WIDTH**-0.5).astype(dquery_ref.dtype)


def attend(query, grad_turned, mask, left, centre, right):
    vmem = pl.BlockSpec(memory_space=pltpu.VMEM)
    return pl.pallas_call(
        attend_kernel,
        in_specs=[vmem] * 6,
        out_specs=[vmem] * 4,
        out_shape=[
            jax.ShapeDtypeStruct((WIDTH, OWN), jnp.bfloat16),
            jax.ShapeDtypeStruct((COLUMN, 128), jnp.bfloat16),
            jax.ShapeDtypeStruct((COLUMN, 128), jnp.float32),
            jax.ShapeDtypeStruct((COLUMN, 128), jnp.bfloat16),
        ],
        scratch_shapes=[
            pltpu.VMEM((3 * COLUMN, OWN), jnp.float32),
            pltpu.VMEM((3 * COLUMN, OWN), jnp.bfloat16),
        ],
        compiler_params=pltpu.CompilerParams(vmem_limit_bytes=16 << 20),
        name="attend",
    )(query, grad_turned, mask, left, centre, right)


def shards(tokens, w_qkv, grad_out, edge_valid):
    number = lax.axis_index("tile")
    pair = contract(tokens, w_qkv[WIDTH:], 1, 1).astype(jnp.bfloat16)
    above = lax.ppermute(pair[OWN - RIM :], "tile", down_pairs)
    below = lax.ppermute(pair[:RIM], "tile", up_pairs)
    query, mask = prepare(number.reshape(1), edge_valid, tokens, w_qkv)
    centre = jnp.concatenate([above, pair, below], axis=0)
    left = lax.ppermute(centre, "tile", right_pairs)
    right = lax.ppermute(centre, "tile", left_pairs)
    dquery, dleft, dcentre, dright = attend(
        query, jnp.transpose(grad_out), mask, left, centre, right
    )
    from_right = lax.ppermute(dleft, "tile", left_pairs)
    from_left = lax.ppermute(dright, "tile", right_pairs)
    column = dcentre + from_right.astype(jnp.float32) + from_left.astype(jnp.float32)
    from_below = lax.ppermute(column[:RIM].astype(jnp.bfloat16), "tile", up_pairs)
    from_above = lax.ppermute(column[OWN + RIM :].astype(jnp.bfloat16), "tile", down_pairs)
    own = (
        column[RIM : RIM + OWN]
        + jnp.pad(from_below.astype(jnp.float32), ((OWN - RIM, 0), (0, 0)))
        + jnp.pad(from_above.astype(jnp.float32), ((0, OWN - RIM), (0, 0)))
    )
    grad_qkv = jnp.concatenate([jnp.transpose(dquery), own.astype(jnp.bfloat16)], axis=1)
    grad_w_term = contract(tokens, grad_qkv, 0, 0).astype(jnp.bfloat16)
    grad_w = summed_exchange(grad_w_term.reshape(TILES, D // TILES, -1), "tile", None)
    rows = OWN // HEADS
    by_owner = grad_qkv.reshape(HIGH, NEAR, rows, -1).transpose(1, 0, 2, 3).reshape(OWN, -1)
    partial_value = contract(by_owner, w_qkv, 1, 0).astype(jnp.bfloat16)
    near_sum = summed_exchange(partial_value.reshape(NEAR, HIGH * rows, D), "head", near_groups)
    grad_x = summed_exchange(
        near_sum.astype(jnp.bfloat16).reshape(HIGH, rows, D), "head", far_groups
    ).astype(jnp.bfloat16)
    return (grad_x, grad_w)


def solution(mesh):
    in_specs = (P("tile", None), P("head", None), P("tile", "head"), P("tile", None))
    out_specs = (P(("tile", "head"), None), P("tile", "head"))
    return jax.shard_map(shards, mesh=mesh, in_specs=in_specs, out_specs=out_specs, check_vma=False)
```

time: 151 us -> 107 us (0.71)
  starting transfers between devices: 69.4 us -> 49.7 us
  local copies, waits for them, and re-layouts: 15.9 us -> 1.8 us
  other arithmetic: 11.6 us -> 2.29 us
  waiting for transfers between devices: 28.6 us -> 34.6 us
  between operations: 6.58 us -> 0.87 us
  Pallas kernels: 0 us -> 4.3 us
  matrix products: 5.11 us -> 2.11 us
    ppermute x16 -> x8, starting transfers between devices: 49.6 us -> 25.6 us  [the longest x1 6.64 us: shards(): right = lax.ppermute(centre, 'tile', left_pairs)]
    another operation x11 -> x1, other arithmetic: 7.93 us -> 0.06 us
    ppermute x16 -> x8, waiting for transfers between devices: 1.91 us -> 6.99 us  [the longest x1 3.71 us: shards(): below = lax.ppermute(pair[:RIM], 'tile', up_pairs)]
    scatter x9 -> x0, local copies, waits for them, and re-layouts: 4.57 us -> none  [the longest x8 4.51 us: shards(): region = region.at[into_top:into_bottom, into_left:into_right].set(moved)]
    pallas_call x0 -> x2, Pallas kernels: none -> 4.3 us  [the longest x1 2.47 us: attend(): pl.pallas_call(attend_kernel, in_specs=[vmem] * 6, out_specs=[vmem] * 4,...]
    all_to_all x2, starting transfers between devices: 19.8 us -> 24 us  [summed_exchange(): received = lax.all_to_all(chunks, axis, 0, 0, axis_index_groups=groups)]
    dot_general x9 -> x3, matrix products: 5.11 us -> 2.11 us  [contract(): lax.dot_general(left, right, (((left_axis,), (right_axis,)), ((), ())), p...]
    and x2 -> x0, local copies, waits for them, and re-layouts: 2.51 us -> none  [window_mask(): (jnp.abs(key_row - query_row - halo) <= halo) & (jnp.abs(key_column - que...]
  transfers between devices with their start and end apart: 18 -> 10, of which waited for: 3 -> 6; matrix products, arithmetic and copies ran while one was open for 15% -> 2% of each run, Pallas kernels for 0% -> 2%
where the time goes in v2:
time: 107 us
  starting transfers between devices  49.7 us (46%)
  waiting for transfers between devices  34.6 us (32%)
  blocking collectives  11.3 us (11%)
  Pallas kernels  4.3 us (4%)
  other arithmetic  2.29 us (2%)
  matrix products  2.11 us (2%)
  local copies, waits for them, and re-layouts  1.8 us (2%)
    all_to_all x2, waiting for transfers between devices, summed_exchange(): received = lax.all_to_all(chunks, axis, 0, 0, axis_index_groups=groups)  27.6 us
    all_to_all x2, starting transfers between devices, summed_exchange(): received = lax.all_to_all(chunks, axis, 0, 0, axis_index_groups=groups)  24 us
    all_to_all x1, blocking collectives, summed_exchange(): received = lax.all_to_all(chunks, axis, 0, 0, axis_index_groups=groups)  11.3 us
    ppermute x1, starting transfers between devices, shards(): right = lax.ppermute(centre, 'tile', left_pairs)  6.64 us
    ppermute x1, starting transfers between devices, shards(): above = lax.ppermute(pair[OWN - RIM:], 'tile', down_pairs)  4.49 us
    ppermute x1, starting transfers between devices, shards(): lax.ppermute(column[OWN + RIM:].astype(jnp.bfloat16), 'tile', down_pairs)  3.99 us
    ppermute x1, waiting for transfers between devices, shards(): below = lax.ppermute(pair[:RIM], 'tile', up_pairs)  3.71 us
    ppermute x1, starting transfers between devices, shards(): from_left = lax.ppermute(dright, 'tile', right_pairs)  3.61 us
  transfers between devices with their start and end apart: 10, of which 6 were waited for; matrix products, arithmetic and copies ran while one was open for 2% of the time, Pallas kernels for 2%

profile of v2, /device:TPU:1, one launch (start us, length us, event | category | flops | bytes accessed | tf_op | source)
XLA Modules:
  0.0 106.9 jit_solution(9250191657796857827)
XLA Ops:
  0.6 1.5 %convolution_convert_fusion.2 = bf16[256,128]{1,0:T(8,128)(2,1)S(1)} fusion(bf16[256,1024]{1,0:T(8,128)(2,1)} %tokens_ref.1, bf16[192,1024]{1,0:T(8,128)(2,1)} %w_ref.1), kind=kOutput, calls=%fused_computation.3 | convolution fusion | flops 67141632 | bytes 851968 | tf_op jit(solution)/shard_map/dot_general | solution.py:39
  2.1 4.5 %collective-permute-start = (bf16[192,128]{1,0:T(8,128)(2,1)S(1)}, bf16[192,128]{1,0:T(8,128)(2,1)S(1)}, u32[]{:S(2)}, u32[]{:S(2)}) collective-permute-start(bf16[192,128]{1,0:T(8,128)(2,1)S(1)} %get-tuple-element.18), channel_id=1, source_target_pairs={{0,128},{16,144},{32,160},{48,176},{64,192},{80,208},{96,224},{112... | collective-permute-start | bytes 147464 | tf_op jit(solution)/shard_map/ppermute | solution.py:167
  6.6 1.3 %collective-permute-start.1 = (bf16[192,128]{1,0:T(8,128)(2,1)S(1)}, bf16[192,128]{1,0:T(8,128)(2,1)S(1)}, u32[]{:S(2)}, u32[]{:S(2)}) collective-permute-start(bf16[192,128]{1,0:T(8,128)(2,1)S(1)} %get-tuple-element.19), channel_id=1, source_target_pairs={{128,0},{144,16},{160,32},{176,48},{192,64},{208,80},{224,96},{240... | collective-permute-start | bytes 147464 | tf_op jit(solution)/shard_map/ppermute | solution.py:168
  8.0 3.7 %collective-permute-done.1 = bf16[192,128]{1,0:T(8,128)(2,1)S(1)} collective-permute-done((bf16[192,128]{1,0:T(8,128)(2,1)S(1)}, bf16[192,128]{1,0:T(8,128)(2,1)S(1)}, u32[]{:S(2)}, u32[]{:S(2)}) %collective-permute-start.1) | collective-permute-done | bytes 49184 | tf_op jit(solution)/shard_map/ppermute | solution.py:168
  11.7 6.6 %collective-permute-start.3 = (bf16[640,128]{1,0:T(8,128)(2,1)S(1)}, bf16[640,128]{1,0:T(8,128)(2,1)S(1)}, u32[]{:S(2)}, u32[]{:S(2)}) collective-permute-start(bf16[640,128]{1,0:T(8,128)(2,1)S(1)} %pad_maximum_fusion.centre_ref), channel_id=1, source_target_pairs={{16,0},{32,16},{48,32},{64,48},{80,64},{96,80},{112,96},{144,128},... | collective-permute-start | bytes 491528 | tf_op jit(solution)/shard_map/ppermute | solution.py:172
  18.3 1.9 %collective-permute-start.2 = (bf16[640,128]{1,0:T(8,128)(2,1)S(1)}, bf16[640,128]{1,0:T(8,128)(2,1)S(1)}, u32[]{:S(2)}, u32[]{:S(2)}) collective-permute-start(bf16[640,128]{1,0:T(8,128)(2,1)S(1)} %pad_maximum_fusion.centre_ref), channel_id=1, source_target_pairs={{0,16},{16,32},{32,48},{48,64},{64,80},{80,96},{96,112},{128,144},... | collective-permute-start | bytes 491528 | tf_op jit(solution)/shard_map/ppermute | solution.py:171
  20.9 1.8 %prepare.1 = (bf16[256,256]{1,0:T(8,128)(2,1)S(1)}, bf16[3,640,128]{2,1,0:T(8,128)(2,1)S(1)}) custom-call(s32[1]{0:T(128)} %bitcast.number_ref, s32[1,8]{1,0:T(1,128)S(1)} %copy-done.3, bf16[256,1024]{1,0:T(8,128)(2,1)S(1)} %copy-done, bf16[192,1024]{1,0:T(8,128)(2,1)S(1)} %copy-done.1), custom_call_target="tpu_custom_call" | custom-call | tf_op jit(solution)/shard_map/prepare/pallas_call | solution.py:81
  22.8 2.5 %attend.1 = (bf16[64,256]{1,0:T(8,128)(2,1)S(1)}, bf16[640,128]{1,0:T(8,128)(2,1)S(1)}, f32[640,128]{1,0:T(8,128)S(1)}, bf16[640,128]{1,0:T(8,128)(2,1)S(1)}) custom-call(bf16[256,256]{1,0:T(8,128)(2,1)S(1)} %get-tuple-element.8.query_ref, bf16[64,256]{1,0:T(8,128)(2,1)S(1)} %bitcast.16, bf16[3,640,128]{2,1,0:T(8,128)(2,1)S(1)} %get-tuple-element.9.mask_ref, ...), custom_call_target="tpu_custom_call" | custom-call | tf_op jit(solution)/shard_map/attend/pallas_call | solution.py:145
  25.3 2.4 %collective-permute-start.4 = (bf16[640,128]{1,0:T(8,128)(2,1)S(1)}, bf16[640,128]{1,0:T(8,128)(2,1)S(1)}, u32[]{:S(2)}, u32[]{:S(2)}) collective-permute-start(bf16[640,128]{1,0:T(8,128)(2,1)S(1)} %get-tuple-element.12), channel_id=1, source_target_pairs={{16,0},{32,16},{48,32},{64,48},{80,64},{96,80},{112,96},{144,128},... | collective-permute-start | bytes 491528 | tf_op jit(solution)/shard_map/ppermute | solution.py:176
  27.7 3.6 %collective-permute-start.5 = (bf16[640,128]{1,0:T(8,128)(2,1)S(1)}, bf16[640,128]{1,0:T(8,128)(2,1)S(1)}, u32[]{:S(2)}, u32[]{:S(2)}) collective-permute-start(bf16[640,128]{1,0:T(8,128)(2,1)S(1)} %get-tuple-element.13), channel_id=1, source_target_pairs={{0,16},{16,32},{32,48},{48,64},{64,80},{80,96},{96,112},{128,144},... | collective-permute-start | bytes 491528 | tf_op jit(solution)/shard_map/ppermute | solution.py:177
  31.3 1.1 collective-permute-done.4
  32.4 1.2 %collective-permute-done.5 = bf16[640,128]{1,0:T(8,128)(2,1)S(1)} collective-permute-done((bf16[640,128]{1,0:T(8,128)(2,1)S(1)}, bf16[640,128]{1,0:T(8,128)(2,1)S(1)}, u32[]{:S(2)}, u32[]{:S(2)}) %collective-permute-start.5) | collective-permute-done | bytes 163872 | tf_op jit(solution)/shard_map/ppermute | solution.py:177
  33.6 1.3 %collective-permute-start.6 = (bf16[192,128]{1,0:T(8,128)(2,1)S(1)}, bf16[192,128]{1,0:T(8,128)(2,1)S(1)}, u32[]{:S(2)}, u32[]{:S(2)}) collective-permute-start(bf16[192,128]{1,0:T(8,128)(2,1)S(1)} %get-tuple-element.16), channel_id=1, source_target_pairs={{128,0},{144,16},{160,32},{176,48},{192,64},{208,80},{224,96},{240... | collective-permute-start | bytes 147464 | tf_op jit(solution)/shard_map/ppermute | solution.py:179
  34.9 4.0 %collective-permute-start.7 = (bf16[192,128]{1,0:T(8,128)(2,1)S(1)}, bf16[192,128]{1,0:T(8,128)(2,1)S(1)}, u32[]{:S(2)}, u32[]{:S(2)}) collective-permute-start(bf16[192,128]{1,0:T(8,128)(2,1)S(1)} %get-tuple-element.17), channel_id=1, source_target_pairs={{0,128},{16,144},{32,160},{48,176},{64,192},{80,208},{96,224},{112... | collective-permute-start | bytes 147464 | tf_op jit(solution)/shard_map/ppermute | solution.py:180
  39.0 1.0 collective-permute-done.7
  40.5 11.3 %all_to_all.15 = bf16[4,64,1024]{2,1,0:T(8,128)(2,1)S(1)} all-to-all(bf16[4,64,1024]{2,1,0:T(8,128)(2,1)S(1)} %bitcast.17), channel_id=1, replica_groups={{0,1,2,3},{4,5,6,7},{8,9,10,11},{12,13,14,15},{16,17,18,19},{20,21,22,2..., dimensions={0} | all-to-all | bytes 1048576 | tf_op jit(solution)/shard_map/all_to_all | solution.py:34
  51.8 0.7 reduce_sum.33
  52.6 13.6 %all-to-all-start.1 = ((bf16[4,16,1024]{2,1,0:T(8,128)(2,1)}), bf16[4,16,1024]{2,1,0:T(8,128)(2,1)S(1)}, u32[]{:S(2)}, u32[]{:S(2)}) async-start(bf16[4,16,1024]{2,1,0:T(8,128)(2,1)} %bitcast.7), calls=%async_computation.1 | async-start | bytes 262144 | tf_op jit(solution)/shard_map/all_to_all | solution.py:34
  66.5 1.0 copy.12
  67.5 11.8 %all-to-all-done.1 = bf16[4,16,1024]{2,1,0:T(8,128)(2,1)S(1)} async-done(((bf16[4,16,1024]{2,1,0:T(8,128)(2,1)}), bf16[4,16,1024]{2,1,0:T(8,128)(2,1)S(1)}, u32[]{:S(2)}, u32[]{:S(2)}) %all-to-all-start.1) | async-done | bytes 131104 | tf_op jit(solution)/shard_map/all_to_all | solution.py:34
  79.3 10.5 %all-to-all-start.2 = ((bf16[32,32,192]{2,1,0:T(8,128)(2,1)}), bf16[32,32,192]{2,1,0:T(8,128)(2,1)S(1)}, u32[]{:S(2)}, u32[]{:S(2)}) async-start(bf16[32,32,192]{2,1,0:T(8,128)(2,1)} %bitcast.9), calls=%async_computation.2 | async-start | bytes 1048576 | tf_op jit(solution)/shard_map/all_to_all | solution.py:34
  89.8 0.6 reduce_sum.34
  90.4 15.8 %all-to-all-done.2 = bf16[32,32,192]{2,1,0:T(8,128)(2,1)S(1)} async-done(((bf16[32,32,192]{2,1,0:T(8,128)(2,1)}), bf16[32,32,192]{2,1,0:T(8,128)(2,1)S(1)}, u32[]{:S(2)}, u32[]{:S(2)}) %all-to-all-start.2) | async-done | bytes 393248 | tf_op jit(solution)/shard_map/all_to_all | solution.py:34
  106.2 0.7 convert_reduce_fusion
  (22 shorter events, 1.6 us)
Async XLA Ops:
  0.6 19.6 %copy-start = (bf16[256,1024]{1,0:T(8,128)(2,1)S(1)}, bf16[256,1024]{1,0:T(8,128)(2,1)}, u32[]{:S(2)}) copy-start(bf16[256,1024]{1,0:T(8,128)(2,1)} %tokens_ref.1) | copy-start | bytes 1572868
  2.1 18.2 %copy-start.1 = (bf16[192,1024]{1,0:T(8,128)(2,1)S(1)}, bf16[192,1024]{1,0:T(8,128)(2,1)}, u32[]{:S(2)}) copy-start(bf16[192,1024]{1,0:T(8,128)(2,1)} %w_ref.1) | copy-start | bytes 1179652
  2.1 5.8 %collective-permute-start = (bf16[192,128]{1,0:T(8,128)(2,1)S(1)}, bf16[192,128]{1,0:T(8,128)(2,1)S(1)}, u32[]{:S(2)}, u32[]{:S(2)}) collective-permute-start(bf16[192,128]{1,0:T(8,128)(2,1)S(1)} %get-tuple-element.18), channel_id=1, source_target_pairs={{0,128},{16,144},{32,160},{48,176},{64,192},{80,208},{96,224},{112... | collective-permute-start | bytes 147464 | tf_op jit(solution)/shard_map/ppermute | solution.py:167
  6.6 5.0 %collective-permute-start.1 = (bf16[192,128]{1,0:T(8,128)(2,1)S(1)}, bf16[192,128]{1,0:T(8,128)(2,1)S(1)}, u32[]{:S(2)}, u32[]{:S(2)}) collective-permute-start(bf16[192,128]{1,0:T(8,128)(2,1)S(1)} %get-tuple-element.19), channel_id=1, source_target_pairs={{128,0},{144,16},{160,32},{176,48},{192,64},{208,80},{224,96},{240... | collective-permute-start | bytes 147464 | tf_op jit(solution)/shard_map/ppermute | solution.py:168
  11.7 11.1 %collective-permute-start.3 = (bf16[640,128]{1,0:T(8,128)(2,1)S(1)}, bf16[640,128]{1,0:T(8,128)(2,1)S(1)}, u32[]{:S(2)}, u32[]{:S(2)}) collective-permute-start(bf16[640,128]{1,0:T(8,128)(2,1)S(1)} %pad_maximum_fusion.centre_ref), channel_id=1, source_target_pairs={{16,0},{32,16},{48,32},{64,48},{80,64},{96,80},{112,96},{144,128},... | collective-permute-start | bytes 491528 | tf_op jit(solution)/shard_map/ppermute | solution.py:172
  18.3 4.4 %collective-permute-start.2 = (bf16[640,128]{1,0:T(8,128)(2,1)S(1)}, bf16[640,128]{1,0:T(8,128)(2,1)S(1)}, u32[]{:S(2)}, u32[]{:S(2)}) collective-permute-start(bf16[640,128]{1,0:T(8,128)(2,1)S(1)} %pad_maximum_fusion.centre_ref), channel_id=1, source_target_pairs={{0,16},{16,32},{32,48},{48,64},{64,80},{80,96},{96,112},{128,144},... | collective-permute-start | bytes 491528 | tf_op jit(solution)/shard_map/ppermute | solution.py:171
  20.3 0.7 copy-start.3
  20.9 1.9 %copy-start.2 = (bf16[256,64]{0,1:T(8,128)(2,1)S(1)}, bf16[256,64]{0,1:T(8,128)(2,1)}, u32[]{:S(2)}) copy-start(bf16[256,64]{0,1:T(8,128)(2,1)} %param.6) | copy-start | bytes 98308
  25.3 7.1 %collective-permute-start.4 = (bf16[640,128]{1,0:T(8,128)(2,1)S(1)}, bf16[640,128]{1,0:T(8,128)(2,1)S(1)}, u32[]{:S(2)}, u32[]{:S(2)}) collective-permute-start(bf16[640,128]{1,0:T(8,128)(2,1)S(1)} %get-tuple-element.12), channel_id=1, source_target_pairs={{16,0},{32,16},{48,32},{64,48},{80,64},{96,80},{112,96},{144,128},... | collective-permute-start | bytes 491528 | tf_op jit(solution)/shard_map/ppermute | solution.py:176
  27.7 5.9 %collective-permute-start.5 = (bf16[640,128]{1,0:T(8,128)(2,1)S(1)}, bf16[640,128]{1,0:T(8,128)(2,1)S(1)}, u32[]{:S(2)}, u32[]{:S(2)}) collective-permute-start(bf16[640,128]{1,0:T(8,128)(2,1)S(1)} %get-tuple-element.13), channel_id=1, source_target_pairs={{0,16},{16,32},{32,48},{48,64},{64,80},{80,96},{96,112},{128,144},... | collective-permute-start | bytes 491528 | tf_op jit(solution)/shard_map/ppermute | solution.py:177
  33.6 5.4 %collective-permute-start.6 = (bf16[192,128]{1,0:T(8,128)(2,1)S(1)}, bf16[192,128]{1,0:T(8,128)(2,1)S(1)}, u32[]{:S(2)}, u32[]{:S(2)}) collective-permute-start(bf16[192,128]{1,0:T(8,128)(2,1)S(1)} %get-tuple-element.16), channel_id=1, source_target_pairs={{128,0},{144,16},{160,32},{176,48},{192,64},{208,80},{224,96},{240... | collective-permute-start | bytes 147464 | tf_op jit(solution)/shard_map/ppermute | solution.py:179
  34.9 5.2 %collective-permute-start.7 = (bf16[192,128]{1,0:T(8,128)(2,1)S(1)}, bf16[192,128]{1,0:T(8,128)(2,1)S(1)}, u32[]{:S(2)}, u32[]{:S(2)}) collective-permute-start(bf16[192,128]{1,0:T(8,128)(2,1)S(1)} %get-tuple-element.17), channel_id=1, source_target_pairs={{0,128},{16,144},{32,160},{48,176},{64,192},{80,208},{96,224},{112... | collective-permute-start | bytes 147464 | tf_op jit(solution)/shard_map/ppermute | solution.py:180
  52.6 26.7 %all-to-all-start.1 = ((bf16[4,16,1024]{2,1,0:T(8,128)(2,1)}), bf16[4,16,1024]{2,1,0:T(8,128)(2,1)S(1)}, u32[]{:S(2)}, u32[]{:S(2)}) async-start(bf16[4,16,1024]{2,1,0:T(8,128)(2,1)} %bitcast.7), calls=%async_computation.1 | async-start | bytes 262144 | tf_op jit(solution)/shard_map/all_to_all | solution.py:34
  79.3 26.9 %all-to-all-start.2 = ((bf16[32,32,192]{2,1,0:T(8,128)(2,1)}), bf16[32,32,192]{2,1,0:T(8,128)(2,1)S(1)}, u32[]{:S(2)}, u32[]{:S(2)}) async-start(bf16[32,32,192]{2,1,0:T(8,128)(2,1)} %bitcast.9), calls=%async_computation.2 | async-start | bytes 1048576 | tf_op jit(solution)/shard_map/all_to_all | solution.py:34

commit v3 on v2

--- a/solution.py
+++ b/solution.py
@@ -21,18 +21,10 @@
 BARRED = -1e30
 
 directions = ((-1, -1), (-1, 0), (-1, 1), (0, -1), (0, 1), (1, -1), (1, 0), (1, 1))
-near_groups = [[high * NEAR + near for near in range(NEAR)] for high in range(HIGH)]
-far_groups = [[high * NEAR + near for high in range(HIGH)] for near in range(NEAR)]
-
 down_pairs = [(tile, tile + GRID_COLS) for tile in range(TILES - GRID_COLS)]
 up_pairs = [(target, source) for source, target in down_pairs]
 right_pairs = [(tile, tile + 1) for tile in range(TILES) if tile % GRID_COLS < GRID_COLS - 1]
 left_pairs = [(target, source) for source, target in right_pairs]
-
-
-def summed_exchange(chunks, axis, groups):
-    received = lax.all_to_all(chunks, axis, 0, 0, axis_index_groups=groups)
-    return jnp.sum(received.astype(jnp.float32), axis=0)
 
 
 def contract(left, right, left_axis, right_axis):
@@ -137,7 +129,7 @@
         dpair = contract(grad_scores, query[:128], 1, 1) + contract(low_ref[rows, :], grad, 1, 1)
         out_ref[...] = dpair.astype(out_ref.dtype)
         dquery = dquery + contract(pair, grad_scores, 0, 0)
-    dquery_ref[...] = (dquery[:WIDTH] * WIDTH**-0.5).astype(dquery_ref.dtype)
+    dquery_ref[...] = jnp.transpose(dquery[:WIDTH] * WIDTH**-0.5).astype(dquery_ref.dtype)
 
 
 def attend(query, grad_turned, mask, left, centre, right):
@@ -147,7 +139,7 @@
         in_specs=[vmem] * 6,
         out_specs=[vmem] * 4,
         out_shape=[
-            jax.ShapeDtypeStruct((WIDTH, OWN), jnp.bfloat16),
+            jax.ShapeDtypeStruct((OWN, WIDTH), jnp.bfloat16),
             jax.ShapeDtypeStruct((COLUMN, 128), jnp.bfloat16),
             jax.ShapeDtypeStruct((COLUMN, 128), jnp.float32),
             jax.ShapeDtypeStruct((COLUMN, 128), jnp.bfloat16),
@@ -161,15 +153,100 @@
     )(query, grad_turned, mask, left, centre, right)
 
 
+def return_kernel(
+    near_ref, column_ref, below_ref, above_ref, dquery_ref, w_ref,
+    dqkv_ref, kept_ref, first_ref, second_ref, third_ref, sum_ref, rows_ref,
+):
+    sum_ref[...] = column_ref[RIM : RIM + OWN]
+    sum_ref[OWN - RIM :] += below_ref[...].astype(jnp.float32)
+    sum_ref[:RIM] += above_ref[...].astype(jnp.float32)
+    dqkv = jnp.concatenate([dquery_ref[...], sum_ref[...].astype(jnp.bfloat16)], axis=1)
+    dqkv_ref[...] = dqkv
+    rows_ref[...] = dqkv.reshape(HEADS, S, 3 * WIDTH)
+    near = near_ref[0]
+    w = w_ref[...]
+    for step, out_ref in enumerate((kept_ref, first_ref, second_ref, third_ref)):
+        target = near ^ step
+        chosen = jnp.concatenate([rows_ref[high * NEAR + target] for high in range(HIGH)], axis=0)
+        out_ref[...] = contract(chosen, w, 1, 0).astype(jnp.bfloat16)
+
+
+def project_back(near, column, from_below, from_above, dquery, w_qkv):
+    vmem = pl.BlockSpec(memory_space=pltpu.VMEM)
+    part = jax.ShapeDtypeStruct((OWN // NEAR, D), jnp.bfloat16)
+    return pl.pallas_call(
+        return_kernel,
+        in_specs=[pl.BlockSpec(memory_space=pltpu.SMEM)] + [vmem] * 5,
+        out_specs=[vmem] * 5,
+        out_shape=[jax.ShapeDtypeStruct((OWN, 3 * WIDTH), jnp.bfloat16)] + [part] * 4,
+        scratch_shapes=[
+            pltpu.VMEM((OWN, 128), jnp.float32),
+            pltpu.VMEM((HEADS, S, 3 * WIDTH), jnp.bfloat16),
+        ],
+        compiler_params=pltpu.CompilerParams(vmem_limit_bytes=8 << 20),
+        name="project_back",
+    )(near, column, from_below, from_above, dquery, w_qkv)
+
+
+def weight_kernel(turned_ref, dqkv_ref, out_ref):
+    out_ref[...] = contract(turned_ref[...], dqkv_ref[...], 1, 0).astype(jnp.bfloat16)
+
+
+def weight_term(turned, dqkv):
+    vmem = pl.BlockSpec(memory_space=pltpu.VMEM)
+    return pl.pallas_call(
+        weight_kernel,
+        in_specs=[vmem] * 2,
+        out_specs=vmem,
+        out_shape=jax.ShapeDtypeStruct((D, 3 * WIDTH), jnp.bfloat16),
+        compiler_params=pltpu.CompilerParams(vmem_limit_bytes=8 << 20),
+        name="weight_term",
+    )(turned, dqkv)
+
+
+def near_kernel(high_ref, *refs):
+    parts, outs, sum_ref = refs[:NEAR], refs[NEAR : NEAR + HIGH], refs[-1]
+    total = sum(part[...].astype(jnp.float32) for part in parts)
+    sum_ref[...] = total.astype(jnp.bfloat16).reshape(HIGH, S, D)
+    for step, out_ref in enumerate(outs):
+        out_ref[...] = sum_ref[high_ref[0] ^ step]
+
+
+def near_total(high, parts):
+    vmem = pl.BlockSpec(memory_space=pltpu.VMEM)
+    return pl.pallas_call(
+        near_kernel,
+        in_specs=[pl.BlockSpec(memory_space=pltpu.SMEM)] + [vmem] * NEAR,
+        out_specs=[vmem] * HIGH,
+        out_shape=[jax.ShapeDtypeStruct((S, D), jnp.bfloat16)] * HIGH,
+        scratch_shapes=[pltpu.VMEM((HIGH, S, D), jnp.bfloat16)],
+        compiler_params=pltpu.CompilerParams(vmem_limit_bytes=8 << 20),
+        name="near_total",
+    )(high, *parts)
+
+
+def near_swap(step):
+    return [(head, head ^ step) for head in range(HEADS)]
+
+
+def far_swap(step):
+    return [(head, head ^ (step * NEAR)) for head in range(HEADS)]
+
+
 def shards(tokens, w_qkv, grad_out, edge_valid):
     number = lax.axis_index("tile")
+    head = lax.axis_index("head")
+    near, high = head & (NEAR - 1), head >> 2
     pair = contract(tokens, w_qkv[WIDTH:], 1, 1).astype(jnp.bfloat16)
     above = lax.ppermute(pair[OWN - RIM :], "tile", down_pairs)
     below = lax.ppermute(pair[:RIM], "tile", up_pairs)
     query, mask = prepare(number.reshape(1), edge_valid, tokens, w_qkv)
+    above, below, query, mask = lax.optimization_barrier((above, below, query, mask))
+    turned = jnp.transpose(tokens)
     centre = jnp.concatenate([above, pair, below], axis=0)
     left = lax.ppermute(centre, "tile", right_pairs)
     right = lax.ppermute(centre, "tile", left_pairs)
+    left, right, turned = lax.optimization_barrier((left, right, turned))
     dquery, dleft, dcentre, dright = attend(
         query, jnp.transpose(grad_out), mask, left, centre, right
     )
@@ -178,21 +255,18 @@
     column = dcentre + from_right.astype(jnp.float32) + from_left.astype(jnp.float32)
     from_below = lax.ppermute(column[:RIM].astype(jnp.bfloat16), "tile", up_pairs)
     from_above = lax.ppermute(column[OWN + RIM :].astype(jnp.bfloat16), "tile", down_pairs)
-    own = (
-        column[RIM : RIM + OWN]
-        + jnp.pad(from_below.astype(jnp.float32), ((OWN - RIM, 0), (0, 0)))
-        + jnp.pad(from_above.astype(jnp.float32), ((0, OWN - RIM), (0, 0)))
+    dqkv, *parts = project_back(
+        near.reshape(1), column, from_below, from_above, dquery, w_qkv
     )
-    grad_qkv = jnp.concatenate([jnp.transpose(dquery), own.astype(jnp.bfloat16)], axis=1)
-    grad_w_term = contract(tokens, grad_qkv, 0, 0).astype(jnp.bfloat16)
-    grad_w = summed_exchange(grad_w_term.reshape(TILES, D // TILES, -1), "tile", None)
-    rows = OWN // HEADS
-    by_owner = grad_qkv.reshape(HIGH, NEAR, rows, -1).transpose(1, 0, 2, 3).reshape(OWN, -1)
-    partial_value = contract(by_owner, w_qkv, 1, 0).astype(jnp.bfloat16)
-    near_sum = summed_exchange(partial_value.reshape(NEAR, HIGH * rows, D), "head", near_groups)
-    grad_x = summed_exchange(
-        near_sum.astype(jnp.bfloat16).reshape(HIGH, rows, D), "head", far_groups
-    ).astype(jnp.bfloat16)
+    for step in (2, 1, 3):
+        parts[step] = lax.ppermute(parts[step], "head", near_swap(step))
+    term = weight_term(turned, dqkv)
+    terms = lax.all_to_all(term.reshape(TILES, D // TILES, -1), "tile", 0, 0)
+    chunks = list(near_total(high.reshape(1), parts))
+    for step in (3, 2, 1):
+        chunks[step] = lax.ppermute(chunks[step], "head", far_swap(step))
+    grad_x = sum(chunk.astype(jnp.float32) for chunk in chunks).astype(jnp.bfloat16)
+    grad_w = jnp.sum(terms.astype(jnp.float32), axis=0)
     return (grad_x, grad_w)
 
 

time: 107 us -> 97.1 us (0.907)
  the two profiles are of different devices: /device:TPU:1 before, /device:TPU:10 now
where the time goes in v3:
time: 97.1 us; the launch traced here: 96.4 us
  starting transfers between devices  60.2 us (62%)
  waiting for transfers between devices  25.5 us (26%)
  Pallas kernels  6.06 us (6%)
  matrix products  1.49 us (2%)
  other arithmetic  1.42 us (1%)
    ppermute x3, starting transfers between devices, shards(): chunks[step] = lax.ppermute(chunks[step], 'head', far_swap(step))  19.2 us
    all_to_all x1, starting transfers between devices, shards(): terms = lax.all_to_all(term.reshape(TILES, D // TILES, -1), 'tile', 0, 0)  9.47 us
    ppermute x3, starting transfers between devices, shards(): parts[step] = lax.ppermute(parts[step], 'head', near_swap(step))  9.21 us
    ppermute x3, waiting for transfers between devices, shards(): chunks[step] = lax.ppermute(chunks[step], 'head', far_swap(step))  7.89 us
    ppermute x3, waiting for transfers between devices, shards(): parts[step] = lax.ppermute(parts[step], 'head', near_swap(step))  6.41 us
    ppermute x1, starting transfers between devices, shards(): lax.ppermute(column[OWN + RIM:].astype(jnp.bfloat16), 'tile', down_pairs)  4.55 us
    ppermute x1, starting transfers between devices, shards(): above = lax.ppermute(pair[OWN - RIM:], 'tile', down_pairs)  3.82 us
    ppermute x1, waiting for transfers between devices, shards(): from_left = lax.ppermute(dright, 'tile', right_pairs)  3.82 us
  transfers between devices with their start and end apart: 15, of which 11 were waited for; matrix products, arithmetic and copies ran while one was open for 1% of the time, Pallas kernels for 2%

profile of v3, /device:TPU:10, one launch (start us, length us, event | category | flops | bytes accessed | tf_op | source)
XLA Modules:
  0.0 96.4 jit_solution(11718052445001606557)
XLA Ops:
  0.6 1.5 %convolution_convert_fusion = bf16[256,128]{1,0:T(8,128)(2,1)S(1)} fusion(bf16[256,1024]{1,0:T(8,128)(2,1)} %tokens_ref.1, bf16[192,1024]{1,0:T(8,128)(2,1)} %w_ref.3), kind=kOutput, calls=%fused_computation | convolution fusion | flops 67141632 | bytes 851968 | tf_op jit(solution)/shard_map/dot_general | solution.py:31
  2.2 3.8 %collective-permute-start = (bf16[192,128]{1,0:T(8,128)(2,1)S(1)}, bf16[192,128]{1,0:T(8,128)(2,1)S(1)}, u32[]{:S(2)}, u32[]{:S(2)}) collective-permute-start(bf16[192,128]{1,0:T(8,128)(2,1)S(1)} %get-tuple-element.51), channel_id=1, source_target_pairs={{0,128},{16,144},{32,160},{48,176},{64,192},{80,208},{96,224},{112... | collective-permute-start | bytes 147464 | tf_op jit(solution)/shard_map/ppermute | solution.py:241
  8.0 1.8 %prepare.1 = (bf16[256,256]{1,0:T(8,128)(2,1)S(1)}, bf16[3,640,128]{2,1,0:T(8,128)(2,1)S(1)}) custom-call(s32[1]{0:T(128)} %bitcast.2.number_ref, s32[1,8]{1,0:T(1,128)S(1)} %copy-done.3, bf16[256,1024]{1,0:T(8,128)(2,1)S(1)} %copy-done, bf16[192,1024]{1,0:T(8,128)(2,1)S(1)} %copy-done.1), custom_call_target="tpu_custom_call" | custom-call | tf_op jit(solution)/shard_map/prepare/pallas_call | solution.py:73
  9.8 2.2 %collective-permute-done.1 = bf16[192,128]{1,0:T(8,128)(2,1)S(1)} collective-permute-done((bf16[192,128]{1,0:T(8,128)(2,1)S(1)}, bf16[192,128]{1,0:T(8,128)(2,1)S(1)}, u32[]{:S(2)}, u32[]{:S(2)}) %collective-permute-start.1) | collective-permute-done | bytes 49184 | tf_op jit(solution)/shard_map/ppermute | solution.py:242
  12.0 1.9 %collective-permute-start.2 = (bf16[640,128]{1,0:T(8,128)(2,1)S(1)}, bf16[640,128]{1,0:T(8,128)(2,1)S(1)}, u32[]{:S(2)}, u32[]{:S(2)}) collective-permute-start(bf16[640,128]{1,0:T(8,128)(2,1)S(1)} %pad_maximum_fusion.centre_ref), channel_id=1, source_target_pairs={{0,16},{16,32},{32,48},{48,64},{64,80},{80,96},{96,112},{128,144},... | collective-permute-start | bytes 491528 | tf_op jit(solution)/shard_map/ppermute | solution.py:247
  13.9 3.6 %collective-permute-start.3 = (bf16[640,128]{1,0:T(8,128)(2,1)S(1)}, bf16[640,128]{1,0:T(8,128)(2,1)S(1)}, u32[]{:S(2)}, u32[]{:S(2)}) collective-permute-start(bf16[640,128]{1,0:T(8,128)(2,1)S(1)} %pad_maximum_fusion.centre_ref), channel_id=1, source_target_pairs={{16,0},{32,16},{48,32},{64,48},{80,64},{96,80},{112,96},{144,128},... | collective-permute-start | bytes 491528 | tf_op jit(solution)/shard_map/ppermute | solution.py:248
  18.6 1.8 %collective-permute-done.3.right_ref = bf16[640,128]{1,0:T(8,128)(2,1)S(1)} collective-permute-done((bf16[640,128]{1,0:T(8,128)(2,1)S(1)}, bf16[640,128]{1,0:T(8,128)(2,1)S(1)}, u32[]{:S(2)}, u32[]{:S(2)}) %collective-permute-start.3) | collective-permute-done | bytes 163872 | tf_op jit(solution)/shard_map/ppermute | solution.py:248
  20.4 2.5 %attend.1 = (bf16[256,64]{1,0:T(8,128)(2,1)S(1)}, bf16[640,128]{1,0:T(8,128)(2,1)S(1)}, f32[640,128]{1,0:T(8,128)S(1)}, bf16[640,128]{1,0:T(8,128)(2,1)S(1)}) custom-call(bf16[256,256]{1,0:T(8,128)(2,1)S(1)} %get-tuple-element.26.query_ref, bf16[64,256]{1,0:T(8,128)(2,1)S(1)} %bitcast.8, bf16[3,640,128]{2,1,0:T(8,128)(2,1)S(1)} %get-tuple-element.27.mask_ref, ...), custom_call_target="tpu_custom_call" | custom-call | tf_op jit(solution)/shard_map/attend/pallas_call | solution.py:137
  23.0 3.8 %collective-permute-start.4 = (bf16[640,128]{1,0:T(8,128)(2,1)S(1)}, bf16[640,128]{1,0:T(8,128)(2,1)S(1)}, u32[]{:S(2)}, u32[]{:S(2)}) collective-permute-start(bf16[640,128]{1,0:T(8,128)(2,1)S(1)} %get-tuple-element.33), channel_id=1, source_target_pairs={{16,0},{32,16},{48,32},{64,48},{80,64},{96,80},{112,96},{144,128},... | collective-permute-start | bytes 491528 | tf_op jit(solution)/shard_map/ppermute | solution.py:253
  26.8 1.9 %collective-permute-start.5 = (bf16[640,128]{1,0:T(8,128)(2,1)S(1)}, bf16[640,128]{1,0:T(8,128)(2,1)S(1)}, u32[]{:S(2)}, u32[]{:S(2)}) collective-permute-start(bf16[640,128]{1,0:T(8,128)(2,1)S(1)} %get-tuple-element.34), channel_id=1, source_target_pairs={{0,16},{16,32},{32,48},{48,64},{64,80},{80,96},{96,112},{128,144},... | collective-permute-start | bytes 491528 | tf_op jit(solution)/shard_map/ppermute | solution.py:254
  29.6 3.8 %collective-permute-done.5 = bf16[640,128]{1,0:T(8,128)(2,1)S(1)} collective-permute-done((bf16[640,128]{1,0:T(8,128)(2,1)S(1)}, bf16[640,128]{1,0:T(8,128)(2,1)S(1)}, u32[]{:S(2)}, u32[]{:S(2)}) %collective-permute-start.5) | collective-permute-done | bytes 163872 | tf_op jit(solution)/shard_map/ppermute | solution.py:254
  34.8 4.5 %collective-permute-start.7 = (bf16[192,128]{1,0:T(8,128)(2,1)S(1)}, bf16[192,128]{1,0:T(8,128)(2,1)S(1)}, u32[]{:S(2)}, u32[]{:S(2)}) collective-permute-start(bf16[192,128]{1,0:T(8,128)(2,1)S(1)} %get-tuple-element.48), channel_id=1, source_target_pairs={{0,128},{16,144},{32,160},{48,176},{64,192},{80,208},{96,224},{112... | collective-permute-start | bytes 147464 | tf_op jit(solution)/shard_map/ppermute | solution.py:257
  39.5 1.6 %collective-permute-done.7.above_ref = bf16[192,128]{1,0:T(8,128)(2,1)S(1)} collective-permute-done((bf16[192,128]{1,0:T(8,128)(2,1)S(1)}, bf16[192,128]{1,0:T(8,128)(2,1)S(1)}, u32[]{:S(2)}, u32[]{:S(2)}) %collective-permute-start.7) | collective-permute-done | bytes 49184 | tf_op jit(solution)/shard_map/ppermute | solution.py:257
  42.7 9.5 %all-to-all-start = ((bf16[32,32,192]{2,1,0:T(8,128)(2,1)}), bf16[32,32,192]{2,1,0:T(8,128)(2,1)S(1)}, u32[]{:S(2)}, u32[]{:S(2)}) async-start(bf16[32,32,192]{2,1,0:T(8,128)(2,1)} %bitcast.5), calls=%async_computation | async-start | bytes 1048576 | tf_op jit(solution)/shard_map/all_to_all | solution.py:264
  52.1 3.5 %collective-permute-start.10 = (bf16[64,1024]{1,0:T(8,128)(2,1)S(1)}, bf16[64,1024]{1,0:T(8,128)(2,1)S(1)}, u32[]{:S(2)}, u32[]{:S(2)}) collective-permute-start(bf16[64,1024]{1,0:T(8,128)(2,1)S(1)} %get-tuple-element.39), channel_id=1, source_target_pairs={{0,3},{1,2},{2,1},{3,0},{4,7},{5,6},{6,5},{7,4},{8,11},{9,10},{10,... | collective-permute-start | bytes 393224 | tf_op jit(solution)/shard_map/ppermute | solution.py:262
  55.6 3.8 %collective-permute-start.8 = (bf16[64,1024]{1,0:T(8,128)(2,1)S(1)}, bf16[64,1024]{1,0:T(8,128)(2,1)S(1)}, u32[]{:S(2)}, u32[]{:S(2)}) collective-permute-start(bf16[64,1024]{1,0:T(8,128)(2,1)S(1)} %get-tuple-element.37), channel_id=1, source_target_pairs={{0,1},{1,0},{2,3},{3,2},{4,5},{5,4},{6,7},{7,6},{8,9},{9,8},{10,11... | collective-permute-start | bytes 393224 | tf_op jit(solution)/shard_map/ppermute | solution.py:262
  59.4 1.9 %collective-permute-start.9 = (bf16[64,1024]{1,0:T(8,128)(2,1)S(1)}, bf16[64,1024]{1,0:T(8,128)(2,1)S(1)}, u32[]{:S(2)}, u32[]{:S(2)}) collective-permute-start(bf16[64,1024]{1,0:T(8,128)(2,1)S(1)} %get-tuple-element.38), channel_id=1, source_target_pairs={{0,2},{1,3},{2,0},{3,1},{4,6},{5,7},{6,4},{7,5},{8,10},{9,11},{10,... | collective-permute-start | bytes 393224 | tf_op jit(solution)/shard_map/ppermute | solution.py:262
  61.4 1.7 %collective-permute-done.8.refs_1_ = bf16[64,1024]{1,0:T(8,128)(2,1)S(1)} collective-permute-done((bf16[64,1024]{1,0:T(8,128)(2,1)S(1)}, bf16[64,1024]{1,0:T(8,128)(2,1)S(1)}, u32[]{:S(2)}, u32[]{:S(2)}) %collective-permute-start.8) | collective-permute-done | bytes 131104 | tf_op jit(solution)/shard_map/ppermute | solution.py:262
  63.1 4.8 %collective-permute-done.9.refs_2_ = bf16[64,1024]{1,0:T(8,128)(2,1)S(1)} collective-permute-done((bf16[64,1024]{1,0:T(8,128)(2,1)S(1)}, bf16[64,1024]{1,0:T(8,128)(2,1)S(1)}, u32[]{:S(2)}, u32[]{:S(2)}) %collective-permute-start.9) | collective-permute-done | bytes 131104 | tf_op jit(solution)/shard_map/ppermute | solution.py:262
  67.9 9.1 %collective-permute-start.11 = (bf16[16,1024]{1,0:T(8,128)(2,1)S(1)}, bf16[16,1024]{1,0:T(8,128)(2,1)S(1)}, u32[]{:S(2)}, u32[]{:S(2)}) collective-permute-start(bf16[16,1024]{1,0:T(8,128)(2,1)S(1)} %get-tuple-element.41), channel_id=1, source_target_pairs={{0,4},{1,5},{2,6},{3,7},{4,0},{5,1},{6,2},{7,3},{8,12},{9,13},{10,... | collective-permute-start | bytes 98312 | tf_op jit(solution)/shard_map/ppermute | solution.py:267
  77.0 8.2 %collective-permute-start.12 = (bf16[16,1024]{1,0:T(8,128)(2,1)S(1)}, bf16[16,1024]{1,0:T(8,128)(2,1)S(1)}, u32[]{:S(2)}, u32[]{:S(2)}) collective-permute-start(bf16[16,1024]{1,0:T(8,128)(2,1)S(1)} %get-tuple-element.42), channel_id=1, source_target_pairs={{0,8},{1,9},{2,10},{3,11},{4,12},{5,13},{6,14},{7,15},{8,0},{9,1},... | collective-permute-start | bytes 98312 | tf_op jit(solution)/shard_map/ppermute | solution.py:267
  85.2 1.9 %collective-permute-start.13 = (bf16[16,1024]{1,0:T(8,128)(2,1)S(1)}, bf16[16,1024]{1,0:T(8,128)(2,1)S(1)}, u32[]{:S(2)}, u32[]{:S(2)}) collective-permute-start(bf16[16,1024]{1,0:T(8,128)(2,1)S(1)} %get-tuple-element.43), channel_id=1, source_target_pairs={{0,12},{1,13},{2,14},{3,15},{4,8},{5,9},{6,10},{7,11},{8,4},{9,5},... | collective-permute-start | bytes 98312 | tf_op jit(solution)/shard_map/ppermute | solution.py:267
  87.2 4.4 %collective-permute-done.12 = bf16[16,1024]{1,0:T(8,128)(2,1)S(1)} collective-permute-done((bf16[16,1024]{1,0:T(8,128)(2,1)S(1)}, bf16[16,1024]{1,0:T(8,128)(2,1)S(1)}, u32[]{:S(2)}, u32[]{:S(2)}) %collective-permute-start.12) | collective-permute-done | bytes 32800 | tf_op jit(solution)/shard_map/ppermute | solution.py:267
  91.6 3.5 %collective-permute-done.13 = bf16[16,1024]{1,0:T(8,128)(2,1)S(1)} collective-permute-done((bf16[16,1024]{1,0:T(8,128)(2,1)S(1)}, bf16[16,1024]{1,0:T(8,128)(2,1)S(1)}, u32[]{:S(2)}, u32[]{:S(2)}) %collective-permute-start.13) | collective-permute-done | bytes 32800 | tf_op jit(solution)/shard_map/ppermute | solution.py:267
  (27 shorter events, 8.4 us)
Async XLA Ops:
  0.6 6.7 %copy-start = (bf16[256,1024]{1,0:T(8,128)(2,1)S(1)}, bf16[256,1024]{1,0:T(8,128)(2,1)}, u32[]{:S(2)}) copy-start(bf16[256,1024]{1,0:T(8,128)(2,1)} %tokens_ref.1) | copy-start | bytes 1572868
  0.6 6.7 %copy-start.1 = (bf16[192,1024]{1,0:T(8,128)(2,1)S(1)}, bf16[192,1024]{1,0:T(8,128)(2,1)}, u32[]{:S(2)}) copy-start(bf16[192,1024]{1,0:T(8,128)(2,1)} %w_ref.3) | copy-start | bytes 1179652
  2.2 7.6 %collective-permute-start = (bf16[192,128]{1,0:T(8,128)(2,1)S(1)}, bf16[192,128]{1,0:T(8,128)(2,1)S(1)}, u32[]{:S(2)}, u32[]{:S(2)}) collective-permute-start(bf16[192,128]{1,0:T(8,128)(2,1)S(1)} %get-tuple-element.51), channel_id=1, source_target_pairs={{0,128},{16,144},{32,160},{48,176},{64,192},{80,208},{96,224},{112... | collective-permute-start | bytes 147464 | tf_op jit(solution)/shard_map/ppermute | solution.py:241
  6.0 6.0 %collective-permute-start.1 = (bf16[192,128]{1,0:T(8,128)(2,1)S(1)}, bf16[192,128]{1,0:T(8,128)(2,1)S(1)}, u32[]{:S(2)}, u32[]{:S(2)}) collective-permute-start(bf16[192,128]{1,0:T(8,128)(2,1)S(1)} %get-tuple-element.50), channel_id=1, source_target_pairs={{128,0},{144,16},{160,32},{176,48},{192,64},{208,80},{224,96},{240... | collective-permute-start | bytes 147464 | tf_op jit(solution)/shard_map/ppermute | solution.py:242
  7.3 0.7 copy-start.3
  12.0 8.4 %copy-start.2 = (bf16[256,64]{0,1:T(8,128)(2,1)S(1)}, bf16[256,64]{0,1:T(8,128)(2,1)}, u32[]{:S(2)}) copy-start(bf16[256,64]{0,1:T(8,128)(2,1)} %param.6) | copy-start | bytes 98308
  12.0 6.6 %collective-permute-start.2 = (bf16[640,128]{1,0:T(8,128)(2,1)S(1)}, bf16[640,128]{1,0:T(8,128)(2,1)S(1)}, u32[]{:S(2)}, u32[]{:S(2)}) collective-permute-start(bf16[640,128]{1,0:T(8,128)(2,1)S(1)} %pad_maximum_fusion.centre_ref), channel_id=1, source_target_pairs={{0,16},{16,32},{32,48},{48,64},{64,80},{80,96},{96,112},{128,144},... | collective-permute-start | bytes 491528 | tf_op jit(solution)/shard_map/ppermute | solution.py:247
  13.9 6.5 %collective-permute-start.3 = (bf16[640,128]{1,0:T(8,128)(2,1)S(1)}, bf16[640,128]{1,0:T(8,128)(2,1)S(1)}, u32[]{:S(2)}, u32[]{:S(2)}) collective-permute-start(bf16[640,128]{1,0:T(8,128)(2,1)S(1)} %pad_maximum_fusion.centre_ref), channel_id=1, source_target_pairs={{16,0},{32,16},{48,32},{64,48},{80,64},{96,80},{112,96},{144,128},... | collective-permute-start | bytes 491528 | tf_op jit(solution)/shard_map/ppermute | solution.py:248
  23.0 6.6 %collective-permute-start.4 = (bf16[640,128]{1,0:T(8,128)(2,1)S(1)}, bf16[640,128]{1,0:T(8,128)(2,1)S(1)}, u32[]{:S(2)}, u32[]{:S(2)}) collective-permute-start(bf16[640,128]{1,0:T(8,128)(2,1)S(1)} %get-tuple-element.33), channel_id=1, source_target_pairs={{16,0},{32,16},{48,32},{64,48},{80,64},{96,80},{112,96},{144,128},... | collective-permute-start | bytes 491528 | tf_op jit(solution)/shard_map/ppermute | solution.py:253
  26.8 6.6 %collective-permute-start.5 = (bf16[640,128]{1,0:T(8,128)(2,1)S(1)}, bf16[640,128]{1,0:T(8,128)(2,1)S(1)}, u32[]{:S(2)}, u32[]{:S(2)}) collective-permute-start(bf16[640,128]{1,0:T(8,128)(2,1)S(1)} %get-tuple-element.34), channel_id=1, source_target_pairs={{0,16},{16,32},{32,48},{48,64},{64,80},{80,96},{96,112},{128,144},... | collective-permute-start | bytes 491528 | tf_op jit(solution)/shard_map/ppermute | solution.py:254
  33.5 6.0 %collective-permute-start.6 = (bf16[192,128]{1,0:T(8,128)(2,1)S(1)}, bf16[192,128]{1,0:T(8,128)(2,1)S(1)}, u32[]{:S(2)}, u32[]{:S(2)}) collective-permute-start(bf16[192,128]{1,0:T(8,128)(2,1)S(1)} %get-tuple-element.49), channel_id=1, source_target_pairs={{128,0},{144,16},{160,32},{176,48},{192,64},{208,80},{224,96},{240... | collective-permute-start | bytes 147464 | tf_op jit(solution)/shard_map/ppermute | solution.py:256
  34.8 6.3 %collective-permute-start.7 = (bf16[192,128]{1,0:T(8,128)(2,1)S(1)}, bf16[192,128]{1,0:T(8,128)(2,1)S(1)}, u32[]{:S(2)}, u32[]{:S(2)}) collective-permute-start(bf16[192,128]{1,0:T(8,128)(2,1)S(1)} %get-tuple-element.48), channel_id=1, source_target_pairs={{0,128},{16,144},{32,160},{48,176},{64,192},{80,208},{96,224},{112... | collective-permute-start | bytes 147464 | tf_op jit(solution)/shard_map/ppermute | solution.py:257
  42.7 53.0 %all-to-all-start = ((bf16[32,32,192]{2,1,0:T(8,128)(2,1)}), bf16[32,32,192]{2,1,0:T(8,128)(2,1)S(1)}, u32[]{:S(2)}, u32[]{:S(2)}) async-start(bf16[32,32,192]{2,1,0:T(8,128)(2,1)} %bitcast.5), calls=%async_computation | async-start | bytes 1048576 | tf_op jit(solution)/shard_map/all_to_all | solution.py:264
  52.1 9.2 %collective-permute-start.10 = (bf16[64,1024]{1,0:T(8,128)(2,1)S(1)}, bf16[64,1024]{1,0:T(8,128)(2,1)S(1)}, u32[]{:S(2)}, u32[]{:S(2)}) collective-permute-start(bf16[64,1024]{1,0:T(8,128)(2,1)S(1)} %get-tuple-element.39), channel_id=1, source_target_pairs={{0,3},{1,2},{2,1},{3,0},{4,7},{5,6},{6,5},{7,4},{8,11},{9,10},{10,... | collective-permute-start | bytes 393224 | tf_op jit(solution)/shard_map/ppermute | solution.py:262
  55.6 7.4 %collective-permute-start.8 = (bf16[64,1024]{1,0:T(8,128)(2,1)S(1)}, bf16[64,1024]{1,0:T(8,128)(2,1)S(1)}, u32[]{:S(2)}, u32[]{:S(2)}) collective-permute-start(bf16[64,1024]{1,0:T(8,128)(2,1)S(1)} %get-tuple-element.37), channel_id=1, source_target_pairs={{0,1},{1,0},{2,3},{3,2},{4,5},{5,4},{6,7},{7,6},{8,9},{9,8},{10,11... | collective-permute-start | bytes 393224 | tf_op jit(solution)/shard_map/ppermute | solution.py:262
  59.4 8.4 %collective-permute-start.9 = (bf16[64,1024]{1,0:T(8,128)(2,1)S(1)}, bf16[64,1024]{1,0:T(8,128)(2,1)S(1)}, u32[]{:S(2)}, u32[]{:S(2)}) collective-permute-start(bf16[64,1024]{1,0:T(8,128)(2,1)S(1)} %get-tuple-element.38), channel_id=1, source_target_pairs={{0,2},{1,3},{2,0},{3,1},{4,6},{5,7},{6,4},{7,5},{8,10},{9,11},{10,... | collective-permute-start | bytes 393224 | tf_op jit(solution)/shard_map/ppermute | solution.py:262
  67.9 19.3 %collective-permute-start.11 = (bf16[16,1024]{1,0:T(8,128)(2,1)S(1)}, bf16[16,1024]{1,0:T(8,128)(2,1)S(1)}, u32[]{:S(2)}, u32[]{:S(2)}) collective-permute-start(bf16[16,1024]{1,0:T(8,128)(2,1)S(1)} %get-tuple-element.41), channel_id=1, source_target_pairs={{0,4},{1,5},{2,6},{3,7},{4,0},{5,1},{6,2},{7,3},{8,12},{9,13},{10,... | collective-permute-start | bytes 98312 | tf_op jit(solution)/shard_map/ppermute | solution.py:267
  77.0 14.6 %collective-permute-start.12 = (bf16[16,1024]{1,0:T(8,128)(2,1)S(1)}, bf16[16,1024]{1,0:T(8,128)(2,1)S(1)}, u32[]{:S(2)}, u32[]{:S(2)}) collective-permute-start(bf16[16,1024]{1,0:T(8,128)(2,1)S(1)} %get-tuple-element.42), channel_id=1, source_target_pairs={{0,8},{1,9},{2,10},{3,11},{4,12},{5,13},{6,14},{7,15},{8,0},{9,1},... | collective-permute-start | bytes 98312 | tf_op jit(solution)/shard_map/ppermute | solution.py:267
  85.2 9.8 %collective-permute-start.13 = (bf16[16,1024]{1,0:T(8,128)(2,1)S(1)}, bf16[16,1024]{1,0:T(8,128)(2,1)S(1)}, u32[]{:S(2)}, u32[]{:S(2)}) collective-permute-start(bf16[16,1024]{1,0:T(8,128)(2,1)S(1)} %get-tuple-element.43), channel_id=1, source_target_pairs={{0,12},{1,13},{2,14},{3,15},{4,8},{5,9},{6,10},{7,11},{8,4},{9,5},... | collective-permute-start | bytes 98312 | tf_op jit(solution)/shard_map/ppermute | solution.py:267

commit v4 on v3

--- a/solution.py
+++ b/solution.py
@@ -23,8 +23,12 @@
 directions = ((-1, -1), (-1, 0), (-1, 1), (0, -1), (0, 1), (1, -1), (1, 0), (1, 1))
 down_pairs = [(tile, tile + GRID_COLS) for tile in range(TILES - GRID_COLS)]
 up_pairs = [(target, source) for source, target in down_pairs]
-right_pairs = [(tile, tile + 1) for tile in range(TILES) if tile % GRID_COLS < GRID_COLS - 1]
-left_pairs = [(target, source) for source, target in right_pairs]
+twin_pairs = [(tile, tile ^ 1) for tile in range(TILES)]
+next_pairs = [
+    (tile, tile + 2 * (tile & 1) - 1)
+    for tile in range(TILES)
+    if 0 <= tile % GRID_COLS + 2 * (tile & 1) - 1 < GRID_COLS
+]
 
 
 def contract(left, right, left_axis, right_axis):
@@ -58,10 +62,19 @@
     far_row = (lane < S) & (jnp.abs(key_row - lane) > HALO)
     column_lane = (lane >= S) & (lane < 2 * S)
     number = number_ref[0]
-    for block in range(3):
-        offset = key_column + (block - 1) * S - lane + S
+    odd = number & 1
+    for block in range(3):
+        column_step = (block - 1) * (1 - 2 * odd)
+        offset = key_column + column_step * S - lane + S
         far_column = column_lane & (jnp.abs(offset) > HALO)
-        above, beside, below = (usable(flags_ref, number, step, block - 1) for step in (-1, 0, 1))
+        above, beside, below = (
+            jnp.where(
+                odd == 1,
+                usable(flags_ref, number, step, 1 - block),
+                usable(flags_ref, number, step, block - 1),
+            )
+            for step in (-1, 0, 1)
+        )
         flag = jnp.where(key_row < 0, above, jnp.where(key_row >= S, below, beside))
         closed = (lane == 2 * S) & (flag == 0)
         barred = jnp.where(far_row | far_column | closed, BARRED, 0.0)
@@ -233,7 +246,7 @@
     return [(head, head ^ (step * NEAR)) for head in range(HEADS)]
 
 
-def shards(tokens, w_qkv, grad_out, edge_valid):
+def local_step(tokens, w_qkv, grad_out, edge_valid):
     number = lax.axis_index("tile")
     head = lax.axis_index("head")
     near, high = head & (NEAR - 1), head >> 2
@@ -244,33 +257,31 @@
     above, below, query, mask = lax.optimization_barrier((above, below, query, mask))
     turned = jnp.transpose(tokens)
     centre = jnp.concatenate([above, pair, below], axis=0)
-    left = lax.ppermute(centre, "tile", right_pairs)
-    right = lax.ppermute(centre, "tile", left_pairs)
-    left, right, turned = lax.optimization_barrier((left, right, turned))
-    dquery, dleft, dcentre, dright = attend(
-        query, jnp.transpose(grad_out), mask, left, centre, right
+    beyond = lax.ppermute(centre, "tile", next_pairs)
+    twin = lax.ppermute(centre, "tile", twin_pairs)
+    beyond, twin, turned = lax.optimization_barrier((beyond, twin, turned))
+    dquery, dbeyond, dcentre, dtwin = attend(
+        query, jnp.transpose(grad_out), mask, beyond, centre, twin
     )
-    from_right = lax.ppermute(dleft, "tile", left_pairs)
-    from_left = lax.ppermute(dright, "tile", right_pairs)
-    column = dcentre + from_right.astype(jnp.float32) + from_left.astype(jnp.float32)
+    from_beyond = lax.ppermute(dbeyond, "tile", next_pairs)
+    from_twin = lax.ppermute(dtwin, "tile", twin_pairs)
+    column = dcentre + from_beyond.astype(jnp.float32) + from_twin.astype(jnp.float32)
     from_below = lax.ppermute(column[:RIM].astype(jnp.bfloat16), "tile", up_pairs)
     from_above = lax.ppermute(column[OWN + RIM :].astype(jnp.bfloat16), "tile", down_pairs)
-    dqkv, *parts = project_back(
-        near.reshape(1), column, from_below, from_above, dquery, w_qkv
-    )
+    dqkv, *parts = project_back(near.reshape(1), column, from_below, from_above, dquery, w_qkv)
     for step in (2, 1, 3):
         parts[step] = lax.ppermute(parts[step], "head", near_swap(step))
     term = weight_term(turned, dqkv)
     terms = lax.all_to_all(term.reshape(TILES, D // TILES, -1), "tile", 0, 0)
     chunks = list(near_total(high.reshape(1), parts))
-    for step in (3, 2, 1):
+    for step in (2, 1, 3):
         chunks[step] = lax.ppermute(chunks[step], "head", far_swap(step))
+    grad_w = jnp.sum(terms.astype(jnp.float32), axis=0)
     grad_x = sum(chunk.astype(jnp.float32) for chunk in chunks).astype(jnp.bfloat16)
-    grad_w = jnp.sum(terms.astype(jnp.float32), axis=0)
     return (grad_x, grad_w)
 
 
 def solution(mesh):
     in_specs = (P("tile", None), P("head", None), P("tile", "head"), P("tile", None))
     out_specs = (P(("tile", "head"), None), P("tile", "head"))
-    return jax.shard_map(shards, mesh=mesh, in_specs=in_specs, out_specs=out_specs, check_vma=False)
+    return jax.shard_map(local_step, mesh=mesh, in_specs=in_specs, out_specs=out_specs, check_vma=False)

time: 97.1 us -> 91.5 us (0.942)
  waiting for transfers between devices: 25.5 us -> 20.4 us
    ppermute x14, waiting for transfers between devices: 25.5 us -> 20.4 us  [the longest x3 7.89 us: local_step(): chunks[step] = lax.ppermute(chunks[step], 'head', far_swap(step))]
  transfers between devices with their start and end apart: 15 -> 15, of which waited for: 11 -> 9; matrix products, arithmetic and copies ran while one was open for 1% -> 1% of each run, Pallas kernels for 2% -> 2%
where the time goes in v4:
time: 91.5 us; the launch traced here: 90.9 us
  starting transfers between devices  59.7 us (65%)
  waiting for transfers between devices  20.4 us (22%)
  Pallas kernels  6.04 us (7%)
  matrix products  1.49 us (2%)
  other arithmetic  1.42 us (2%)
    ppermute x3, starting transfers between devices, local_step(): chunks[step] = lax.ppermute(chunks[step], 'head', far_swap(step))  19.2 us
    all_to_all x1, starting transfers between devices, local_step(): terms = lax.all_to_all(term.reshape(TILES, D // TILES, -1), 'tile', 0, 0)  9.47 us
    ppermute x3, starting transfers between devices, local_step(): parts[step] = lax.ppermute(parts[step], 'head', near_swap(step))  9.21 us
    ppermute x3, waiting for transfers between devices, local_step(): chunks[step] = lax.ppermute(chunks[step], 'head', far_swap(step))  7.89 us
    ppermute x3, waiting for transfers between devices, local_step(): parts[step] = lax.ppermute(parts[step], 'head', near_swap(step))  6.41 us
    ppermute x1, starting transfers between devices, local_step(): lax.ppermute(column[OWN + RIM:].astype(jnp.bfloat16), 'tile', down_pairs)  4.55 us
    ppermute x1, starting transfers between devices, local_step(): above = lax.ppermute(pair[OWN - RIM:], 'tile', down_pairs)  3.82 us
    ppermute x1, starting transfers between devices, local_step(): twin = lax.ppermute(centre, 'tile', twin_pairs)  3.5 us
  transfers between devices with their start and end apart: 15, of which 9 were waited for; matrix products, arithmetic and copies ran while one was open for 1% of the time, Pallas kernels for 2%

profile of v4, /device:TPU:10, one launch (start us, length us, event | category | flops | bytes accessed | tf_op | source)
XLA Modules:
  0.0 90.9 jit_solution(17229706801623825922)
XLA Ops:
  0.6 1.5 %convolution_convert_fusion = bf16[256,128]{1,0:T(8,128)(2,1)S(1)} fusion(bf16[256,1024]{1,0:T(8,128)(2,1)} %tokens_ref.1, bf16[192,1024]{1,0:T(8,128)(2,1)} %w_ref.3), kind=kOutput, calls=%fused_computation | convolution fusion | flops 67141632 | bytes 851968 | tf_op jit(solution)/shard_map/dot_general | solution.py:35
  2.2 3.8 %collective-permute-start = (bf16[192,128]{1,0:T(8,128)(2,1)S(1)}, bf16[192,128]{1,0:T(8,128)(2,1)S(1)}, u32[]{:S(2)}, u32[]{:S(2)}) collective-permute-start(bf16[192,128]{1,0:T(8,128)(2,1)S(1)} %get-tuple-element.51), channel_id=1, source_target_pairs={{0,128},{16,144},{32,160},{48,176},{64,192},{80,208},{96,224},{112... | collective-permute-start | bytes 147464 | tf_op jit(solution)/shard_map/ppermute | solution.py:254
  6.0 1.3 %collective-permute-start.1 = (bf16[192,128]{1,0:T(8,128)(2,1)S(1)}, bf16[192,128]{1,0:T(8,128)(2,1)S(1)}, u32[]{:S(2)}, u32[]{:S(2)}) collective-permute-start(bf16[192,128]{1,0:T(8,128)(2,1)S(1)} %get-tuple-element.50), channel_id=1, source_target_pairs={{128,0},{144,16},{160,32},{176,48},{192,64},{208,80},{224,96},{240... | collective-permute-start | bytes 147464 | tf_op jit(solution)/shard_map/ppermute | solution.py:255
  8.0 1.8 %prepare.1 = (bf16[256,256]{1,0:T(8,128)(2,1)S(1)}, bf16[3,640,128]{2,1,0:T(8,128)(2,1)S(1)}) custom-call(s32[1]{0:T(128)} %bitcast.2.number_ref, s32[1,8]{1,0:T(1,128)S(1)} %copy-done.3, bf16[256,1024]{1,0:T(8,128)(2,1)S(1)} %copy-done, bf16[192,1024]{1,0:T(8,128)(2,1)S(1)} %copy-done.1), custom_call_target="tpu_custom_call" | custom-call | tf_op jit(solution)/shard_map/prepare/pallas_call | solution.py:86
  9.8 2.2 %collective-permute-done.1 = bf16[192,128]{1,0:T(8,128)(2,1)S(1)} collective-permute-done((bf16[192,128]{1,0:T(8,128)(2,1)S(1)}, bf16[192,128]{1,0:T(8,128)(2,1)S(1)}, u32[]{:S(2)}, u32[]{:S(2)}) %collective-permute-start.1) | collective-permute-done | bytes 49184 | tf_op jit(solution)/shard_map/ppermute | solution.py:255
  12.0 1.9 %collective-permute-start.2 = (bf16[640,128]{1,0:T(8,128)(2,1)S(1)}, bf16[640,128]{1,0:T(8,128)(2,1)S(1)}, u32[]{:S(2)}, u32[]{:S(2)}) collective-permute-start(bf16[640,128]{1,0:T(8,128)(2,1)S(1)} %pad_maximum_fusion.centre_ref), channel_id=1, source_target_pairs={{16,32},{32,16},{48,64},{64,48},{80,96},{96,80},{144,160},{160,144... | collective-permute-start | bytes 491528 | tf_op jit(solution)/shard_map/ppermute | solution.py:260
  13.9 3.5 %collective-permute-start.3 = (bf16[640,128]{1,0:T(8,128)(2,1)S(1)}, bf16[640,128]{1,0:T(8,128)(2,1)S(1)}, u32[]{:S(2)}, u32[]{:S(2)}) collective-permute-start(bf16[640,128]{1,0:T(8,128)(2,1)S(1)} %pad_maximum_fusion.centre_ref), channel_id=1, source_target_pairs={{0,16},{16,0},{32,48},{48,32},{64,80},{80,64},{96,112},{112,96},{1... | collective-permute-start | bytes 491528 | tf_op jit(solution)/shard_map/ppermute | solution.py:261
  18.6 2.5 %attend.1 = (bf16[256,64]{1,0:T(8,128)(2,1)S(1)}, bf16[640,128]{1,0:T(8,128)(2,1)S(1)}, f32[640,128]{1,0:T(8,128)S(1)}, bf16[640,128]{1,0:T(8,128)(2,1)S(1)}) custom-call(bf16[256,256]{1,0:T(8,128)(2,1)S(1)} %get-tuple-element.26.query_ref, bf16[64,256]{1,0:T(8,128)(2,1)S(1)} %bitcast.8, bf16[3,640,128]{2,1,0:T(8,128)(2,1)S(1)} %get-tuple-element.27.mask_ref, ...), custom_call_target="tpu_custom_call" | custom-call | tf_op jit(solution)/shard_map/attend/pallas_call | solution.py:150
  21.2 2.2 %collective-permute-start.4 = (bf16[640,128]{1,0:T(8,128)(2,1)S(1)}, bf16[640,128]{1,0:T(8,128)(2,1)S(1)}, u32[]{:S(2)}, u32[]{:S(2)}) collective-permute-start(bf16[640,128]{1,0:T(8,128)(2,1)S(1)} %get-tuple-element.33), channel_id=1, source_target_pairs={{16,32},{32,16},{48,64},{64,48},{80,96},{96,80},{144,160},{160,144... | collective-permute-start | bytes 491528 | tf_op jit(solution)/shard_map/ppermute | solution.py:266
  23.4 3.2 %collective-permute-start.5 = (bf16[640,128]{1,0:T(8,128)(2,1)S(1)}, bf16[640,128]{1,0:T(8,128)(2,1)S(1)}, u32[]{:S(2)}, u32[]{:S(2)}) collective-permute-start(bf16[640,128]{1,0:T(8,128)(2,1)S(1)} %get-tuple-element.34), channel_id=1, source_target_pairs={{0,16},{16,0},{32,48},{48,32},{64,80},{80,64},{96,112},{112,96},{1... | collective-permute-start | bytes 491528 | tf_op jit(solution)/shard_map/ppermute | solution.py:267
  27.9 1.3 %collective-permute-start.6 = (bf16[192,128]{1,0:T(8,128)(2,1)S(1)}, bf16[192,128]{1,0:T(8,128)(2,1)S(1)}, u32[]{:S(2)}, u32[]{:S(2)}) collective-permute-start(bf16[192,128]{1,0:T(8,128)(2,1)S(1)} %get-tuple-element.49), channel_id=1, source_target_pairs={{128,0},{144,16},{160,32},{176,48},{192,64},{208,80},{224,96},{240... | collective-permute-start | bytes 147464 | tf_op jit(solution)/shard_map/ppermute | solution.py:269
  29.2 4.5 %collective-permute-start.7 = (bf16[192,128]{1,0:T(8,128)(2,1)S(1)}, bf16[192,128]{1,0:T(8,128)(2,1)S(1)}, u32[]{:S(2)}, u32[]{:S(2)}) collective-permute-start(bf16[192,128]{1,0:T(8,128)(2,1)S(1)} %get-tuple-element.48), channel_id=1, source_target_pairs={{0,128},{16,144},{32,160},{48,176},{64,192},{80,208},{96,224},{112... | collective-permute-start | bytes 147464 | tf_op jit(solution)/shard_map/ppermute | solution.py:270
  33.9 1.6 %collective-permute-done.7.above_ref = bf16[192,128]{1,0:T(8,128)(2,1)S(1)} collective-permute-done((bf16[192,128]{1,0:T(8,128)(2,1)S(1)}, bf16[192,128]{1,0:T(8,128)(2,1)S(1)}, u32[]{:S(2)}, u32[]{:S(2)}) %collective-permute-start.7) | collective-permute-done | bytes 49184 | tf_op jit(solution)/shard_map/ppermute | solution.py:270
  37.1 9.5 %all-to-all-start = ((bf16[32,32,192]{2,1,0:T(8,128)(2,1)}), bf16[32,32,192]{2,1,0:T(8,128)(2,1)S(1)}, u32[]{:S(2)}, u32[]{:S(2)}) async-start(bf16[32,32,192]{2,1,0:T(8,128)(2,1)} %bitcast.5), calls=%async_computation | async-start | bytes 1048576 | tf_op jit(solution)/shard_map/all_to_all | solution.py:275
  46.6 3.5 %collective-permute-start.10 = (bf16[64,1024]{1,0:T(8,128)(2,1)S(1)}, bf16[64,1024]{1,0:T(8,128)(2,1)S(1)}, u32[]{:S(2)}, u32[]{:S(2)}) collective-permute-start(bf16[64,1024]{1,0:T(8,128)(2,1)S(1)} %get-tuple-element.39), channel_id=1, source_target_pairs={{0,3},{1,2},{2,1},{3,0},{4,7},{5,6},{6,5},{7,4},{8,11},{9,10},{10,... | collective-permute-start | bytes 393224 | tf_op jit(solution)/shard_map/ppermute | solution.py:273
  50.1 3.8 %collective-permute-start.8 = (bf16[64,1024]{1,0:T(8,128)(2,1)S(1)}, bf16[64,1024]{1,0:T(8,128)(2,1)S(1)}, u32[]{:S(2)}, u32[]{:S(2)}) collective-permute-start(bf16[64,1024]{1,0:T(8,128)(2,1)S(1)} %get-tuple-element.37), channel_id=1, source_target_pairs={{0,1},{1,0},{2,3},{3,2},{4,5},{5,4},{6,7},{7,6},{8,9},{9,8},{10,11... | collective-permute-start | bytes 393224 | tf_op jit(solution)/shard_map/ppermute | solution.py:273
  53.9 1.9 %collective-permute-start.9 = (bf16[64,1024]{1,0:T(8,128)(2,1)S(1)}, bf16[64,1024]{1,0:T(8,128)(2,1)S(1)}, u32[]{:S(2)}, u32[]{:S(2)}) collective-permute-start(bf16[64,1024]{1,0:T(8,128)(2,1)S(1)} %get-tuple-element.38), channel_id=1, source_target_pairs={{0,2},{1,3},{2,0},{3,1},{4,6},{5,7},{6,4},{7,5},{8,10},{9,11},{10,... | collective-permute-start | bytes 393224 | tf_op jit(solution)/shard_map/ppermute | solution.py:273
  55.8 1.7 %collective-permute-done.8.refs_1_ = bf16[64,1024]{1,0:T(8,128)(2,1)S(1)} collective-permute-done((bf16[64,1024]{1,0:T(8,128)(2,1)S(1)}, bf16[64,1024]{1,0:T(8,128)(2,1)S(1)}, u32[]{:S(2)}, u32[]{:S(2)}) %collective-permute-start.8) | collective-permute-done | bytes 131104 | tf_op jit(solution)/shard_map/ppermute | solution.py:273
  57.5 4.8 %collective-permute-done.9.refs_2_ = bf16[64,1024]{1,0:T(8,128)(2,1)S(1)} collective-permute-done((bf16[64,1024]{1,0:T(8,128)(2,1)S(1)}, bf16[64,1024]{1,0:T(8,128)(2,1)S(1)}, u32[]{:S(2)}, u32[]{:S(2)}) %collective-permute-start.9) | collective-permute-done | bytes 131104 | tf_op jit(solution)/shard_map/ppermute | solution.py:273
  62.3 9.1 %collective-permute-start.11 = (bf16[16,1024]{1,0:T(8,128)(2,1)S(1)}, bf16[16,1024]{1,0:T(8,128)(2,1)S(1)}, u32[]{:S(2)}, u32[]{:S(2)}) collective-permute-start(bf16[16,1024]{1,0:T(8,128)(2,1)S(1)} %get-tuple-element.41), channel_id=1, source_target_pairs={{0,4},{1,5},{2,6},{3,7},{4,0},{5,1},{6,2},{7,3},{8,12},{9,13},{10,... | collective-permute-start | bytes 98312 | tf_op jit(solution)/shard_map/ppermute | solution.py:278
  71.5 8.2 %collective-permute-start.12 = (bf16[16,1024]{1,0:T(8,128)(2,1)S(1)}, bf16[16,1024]{1,0:T(8,128)(2,1)S(1)}, u32[]{:S(2)}, u32[]{:S(2)}) collective-permute-start(bf16[16,1024]{1,0:T(8,128)(2,1)S(1)} %get-tuple-element.42), channel_id=1, source_target_pairs={{0,8},{1,9},{2,10},{3,11},{4,12},{5,13},{6,14},{7,15},{8,0},{9,1},... | collective-permute-start | bytes 98312 | tf_op jit(solution)/shard_map/ppermute | solution.py:278
  79.7 1.9 %collective-permute-start.13 = (bf16[16,1024]{1,0:T(8,128)(2,1)S(1)}, bf16[16,1024]{1,0:T(8,128)(2,1)S(1)}, u32[]{:S(2)}, u32[]{:S(2)}) collective-permute-start(bf16[16,1024]{1,0:T(8,128)(2,1)S(1)} %get-tuple-element.43), channel_id=1, source_target_pairs={{0,12},{1,13},{2,14},{3,15},{4,8},{5,9},{6,10},{7,11},{8,4},{9,5},... | collective-permute-start | bytes 98312 | tf_op jit(solution)/shard_map/ppermute | solution.py:278
  81.6 4.4 %collective-permute-done.12 = bf16[16,1024]{1,0:T(8,128)(2,1)S(1)} collective-permute-done((bf16[16,1024]{1,0:T(8,128)(2,1)S(1)}, bf16[16,1024]{1,0:T(8,128)(2,1)S(1)}, u32[]{:S(2)}, u32[]{:S(2)}) %collective-permute-start.12) | collective-permute-done | bytes 32800 | tf_op jit(solution)/shard_map/ppermute | solution.py:278
  86.0 3.5 %collective-permute-done.13 = bf16[16,1024]{1,0:T(8,128)(2,1)S(1)} collective-permute-done((bf16[16,1024]{1,0:T(8,128)(2,1)S(1)}, bf16[16,1024]{1,0:T(8,128)(2,1)S(1)}, u32[]{:S(2)}, u32[]{:S(2)}) %collective-permute-start.13) | collective-permute-done | bytes 32800 | tf_op jit(solution)/shard_map/ppermute | solution.py:278
  (27 shorter events, 6.3 us)
Async XLA Ops:
  0.6 6.7 %copy-start = (bf16[256,1024]{1,0:T(8,128)(2,1)S(1)}, bf16[256,1024]{1,0:T(8,128)(2,1)}, u32[]{:S(2)}) copy-start(bf16[256,1024]{1,0:T(8,128)(2,1)} %tokens_ref.1) | copy-start | bytes 1572868
  0.6 6.7 %copy-start.1 = (bf16[192,1024]{1,0:T(8,128)(2,1)S(1)}, bf16[192,1024]{1,0:T(8,128)(2,1)}, u32[]{:S(2)}) copy-start(bf16[192,1024]{1,0:T(8,128)(2,1)} %w_ref.3) | copy-start | bytes 1179652
  2.2 7.6 %collective-permute-start = (bf16[192,128]{1,0:T(8,128)(2,1)S(1)}, bf16[192,128]{1,0:T(8,128)(2,1)S(1)}, u32[]{:S(2)}, u32[]{:S(2)}) collective-permute-start(bf16[192,128]{1,0:T(8,128)(2,1)S(1)} %get-tuple-element.51), channel_id=1, source_target_pairs={{0,128},{16,144},{32,160},{48,176},{64,192},{80,208},{96,224},{112... | collective-permute-start | bytes 147464 | tf_op jit(solution)/shard_map/ppermute | solution.py:254
  6.0 6.0 %collective-permute-start.1 = (bf16[192,128]{1,0:T(8,128)(2,1)S(1)}, bf16[192,128]{1,0:T(8,128)(2,1)S(1)}, u32[]{:S(2)}, u32[]{:S(2)}) collective-permute-start(bf16[192,128]{1,0:T(8,128)(2,1)S(1)} %get-tuple-element.50), channel_id=1, source_target_pairs={{128,0},{144,16},{160,32},{176,48},{192,64},{208,80},{224,96},{240... | collective-permute-start | bytes 147464 | tf_op jit(solution)/shard_map/ppermute | solution.py:255
  7.3 0.7 copy-start.3
  12.0 6.7 %copy-start.2 = (bf16[256,64]{0,1:T(8,128)(2,1)S(1)}, bf16[256,64]{0,1:T(8,128)(2,1)}, u32[]{:S(2)}) copy-start(bf16[256,64]{0,1:T(8,128)(2,1)} %param.6) | copy-start | bytes 98308
  12.0 6.6 %collective-permute-start.2 = (bf16[640,128]{1,0:T(8,128)(2,1)S(1)}, bf16[640,128]{1,0:T(8,128)(2,1)S(1)}, u32[]{:S(2)}, u32[]{:S(2)}) collective-permute-start(bf16[640,128]{1,0:T(8,128)(2,1)S(1)} %pad_maximum_fusion.centre_ref), channel_id=1, source_target_pairs={{16,32},{32,16},{48,64},{64,48},{80,96},{96,80},{144,160},{160,144... | collective-permute-start | bytes 491528 | tf_op jit(solution)/shard_map/ppermute | solution.py:260
  13.9 4.7 %collective-permute-start.3 = (bf16[640,128]{1,0:T(8,128)(2,1)S(1)}, bf16[640,128]{1,0:T(8,128)(2,1)S(1)}, u32[]{:S(2)}, u32[]{:S(2)}) collective-permute-start(bf16[640,128]{1,0:T(8,128)(2,1)S(1)} %pad_maximum_fusion.centre_ref), channel_id=1, source_target_pairs={{0,16},{16,0},{32,48},{48,32},{64,80},{80,64},{96,112},{112,96},{1... | collective-permute-start | bytes 491528 | tf_op jit(solution)/shard_map/ppermute | solution.py:261
  21.2 6.6 %collective-permute-start.4 = (bf16[640,128]{1,0:T(8,128)(2,1)S(1)}, bf16[640,128]{1,0:T(8,128)(2,1)S(1)}, u32[]{:S(2)}, u32[]{:S(2)}) collective-permute-start(bf16[640,128]{1,0:T(8,128)(2,1)S(1)} %get-tuple-element.33), channel_id=1, source_target_pairs={{16,32},{32,16},{48,64},{64,48},{80,96},{96,80},{144,160},{160,144... | collective-permute-start | bytes 491528 | tf_op jit(solution)/shard_map/ppermute | solution.py:266
  23.4 4.4 %collective-permute-start.5 = (bf16[640,128]{1,0:T(8,128)(2,1)S(1)}, bf16[640,128]{1,0:T(8,128)(2,1)S(1)}, u32[]{:S(2)}, u32[]{:S(2)}) collective-permute-start(bf16[640,128]{1,0:T(8,128)(2,1)S(1)} %get-tuple-element.34), channel_id=1, source_target_pairs={{0,16},{16,0},{32,48},{48,32},{64,80},{80,64},{96,112},{112,96},{1... | collective-permute-start | bytes 491528 | tf_op jit(solution)/shard_map/ppermute | solution.py:267
  27.9 6.0 %collective-permute-start.6 = (bf16[192,128]{1,0:T(8,128)(2,1)S(1)}, bf16[192,128]{1,0:T(8,128)(2,1)S(1)}, u32[]{:S(2)}, u32[]{:S(2)}) collective-permute-start(bf16[192,128]{1,0:T(8,128)(2,1)S(1)} %get-tuple-element.49), channel_id=1, source_target_pairs={{128,0},{144,16},{160,32},{176,48},{192,64},{208,80},{224,96},{240... | collective-permute-start | bytes 147464 | tf_op jit(solution)/shard_map/ppermute | solution.py:269
  29.2 6.3 %collective-permute-start.7 = (bf16[192,128]{1,0:T(8,128)(2,1)S(1)}, bf16[192,128]{1,0:T(8,128)(2,1)S(1)}, u32[]{:S(2)}, u32[]{:S(2)}) collective-permute-start(bf16[192,128]{1,0:T(8,128)(2,1)S(1)} %get-tuple-element.48), channel_id=1, source_target_pairs={{0,128},{16,144},{32,160},{48,176},{64,192},{80,208},{96,224},{112... | collective-permute-start | bytes 147464 | tf_op jit(solution)/shard_map/ppermute | solution.py:270
  37.1 53.0 %all-to-all-start = ((bf16[32,32,192]{2,1,0:T(8,128)(2,1)}), bf16[32,32,192]{2,1,0:T(8,128)(2,1)S(1)}, u32[]{:S(2)}, u32[]{:S(2)}) async-start(bf16[32,32,192]{2,1,0:T(8,128)(2,1)} %bitcast.5), calls=%async_computation | async-start | bytes 1048576 | tf_op jit(solution)/shard_map/all_to_all | solution.py:275
  46.6 9.2 %collective-permute-start.10 = (bf16[64,1024]{1,0:T(8,128)(2,1)S(1)}, bf16[64,1024]{1,0:T(8,128)(2,1)S(1)}, u32[]{:S(2)}, u32[]{:S(2)}) collective-permute-start(bf16[64,1024]{1,0:T(8,128)(2,1)S(1)} %get-tuple-element.39), channel_id=1, source_target_pairs={{0,3},{1,2},{2,1},{3,0},{4,7},{5,6},{6,5},{7,4},{8,11},{9,10},{10,... | collective-permute-start | bytes 393224 | tf_op jit(solution)/shard_map/ppermute | solution.py:273
  50.1 7.4 %collective-permute-start.8 = (bf16[64,1024]{1,0:T(8,128)(2,1)S(1)}, bf16[64,1024]{1,0:T(8,128)(2,1)S(1)}, u32[]{:S(2)}, u32[]{:S(2)}) collective-permute-start(bf16[64,1024]{1,0:T(8,128)(2,1)S(1)} %get-tuple-element.37), channel_id=1, source_target_pairs={{0,1},{1,0},{2,3},{3,2},{4,5},{5,4},{6,7},{7,6},{8,9},{9,8},{10,11... | collective-permute-start | bytes 393224 | tf_op jit(solution)/shard_map/ppermute | solution.py:273
  53.9 8.4 %collective-permute-start.9 = (bf16[64,1024]{1,0:T(8,128)(2,1)S(1)}, bf16[64,1024]{1,0:T(8,128)(2,1)S(1)}, u32[]{:S(2)}, u32[]{:S(2)}) collective-permute-start(bf16[64,1024]{1,0:T(8,128)(2,1)S(1)} %get-tuple-element.38), channel_id=1, source_target_pairs={{0,2},{1,3},{2,0},{3,1},{4,6},{5,7},{6,4},{7,5},{8,10},{9,11},{10,... | collective-permute-start | bytes 393224 | tf_op jit(solution)/shard_map/ppermute | solution.py:273
  62.3 19.3 %collective-permute-start.11 = (bf16[16,1024]{1,0:T(8,128)(2,1)S(1)}, bf16[16,1024]{1,0:T(8,128)(2,1)S(1)}, u32[]{:S(2)}, u32[]{:S(2)}) collective-permute-start(bf16[16,1024]{1,0:T(8,128)(2,1)S(1)} %get-tuple-element.41), channel_id=1, source_target_pairs={{0,4},{1,5},{2,6},{3,7},{4,0},{5,1},{6,2},{7,3},{8,12},{9,13},{10,... | collective-permute-start | bytes 98312 | tf_op jit(solution)/shard_map/ppermute | solution.py:278
  71.5 14.6 %collective-permute-start.12 = (bf16[16,1024]{1,0:T(8,128)(2,1)S(1)}, bf16[16,1024]{1,0:T(8,128)(2,1)S(1)}, u32[]{:S(2)}, u32[]{:S(2)}) collective-permute-start(bf16[16,1024]{1,0:T(8,128)(2,1)S(1)} %get-tuple-element.42), channel_id=1, source_target_pairs={{0,8},{1,9},{2,10},{3,11},{4,12},{5,13},{6,14},{7,15},{8,0},{9,1},... | collective-permute-start | bytes 98312 | tf_op jit(solution)/shard_map/ppermute | solution.py:278
  79.7 9.8 %collective-permute-start.13 = (bf16[16,1024]{1,0:T(8,128)(2,1)S(1)}, bf16[16,1024]{1,0:T(8,128)(2,1)S(1)}, u32[]{:S(2)}, u32[]{:S(2)}) collective-permute-start(bf16[16,1024]{1,0:T(8,128)(2,1)S(1)} %get-tuple-element.43), channel_id=1, source_target_pairs={{0,12},{1,13},{2,14},{3,15},{4,8},{5,9},{6,10},{7,11},{8,4},{9,5},... | collective-permute-start | bytes 98312 | tf_op jit(solution)/shard_map/ppermute | solution.py:278

commit v5 on v4

--- a/solution.py
+++ b/solution.py
@@ -218,11 +218,11 @@
 
 
 def near_kernel(high_ref, *refs):
-    parts, outs, sum_ref = refs[:NEAR], refs[NEAR : NEAR + HIGH], refs[-1]
+    parts, outs, sum_ref = refs[:NEAR], refs[NEAR:-1], refs[-1]
     total = sum(part[...].astype(jnp.float32) for part in parts)
     sum_ref[...] = total.astype(jnp.bfloat16).reshape(HIGH, S, D)
-    for step, out_ref in enumerate(outs):
-        out_ref[...] = sum_ref[high_ref[0] ^ step]
+    for step, out_ref in zip((0, -1, 1, 2), outs):
+        out_ref[...] = sum_ref[(high_ref[0] + step) & (HIGH - 1)]
 
 
 def near_total(high, parts):
@@ -238,12 +238,28 @@
     )(high, *parts)
 
 
+def tile_kernel(terms_ref, out_ref):
+    out_ref[...] = jnp.sum(terms_ref[...].astype(jnp.float32), axis=0)
+
+
+def tile_total(terms):
+    vmem = pl.BlockSpec(memory_space=pltpu.VMEM)
+    return pl.pallas_call(
+        tile_kernel,
+        in_specs=[vmem],
+        out_specs=vmem,
+        out_shape=jax.ShapeDtypeStruct((D // TILES, 3 * WIDTH), jnp.float32),
+        compiler_params=pltpu.CompilerParams(vmem_limit_bytes=8 << 20),
+        name="tile_total",
+    )(terms)
+
+
 def near_swap(step):
     return [(head, head ^ step) for head in range(HEADS)]
 
 
-def far_swap(step):
-    return [(head, head ^ (step * NEAR)) for head in range(HEADS)]
+def far_moves(*blocks):
+    return [(a * NEAR + near, b * NEAR + near) for a, b in blocks for near in range(NEAR)]
 
 
 def local_step(tokens, w_qkv, grad_out, edge_valid):
@@ -273,10 +289,16 @@
         parts[step] = lax.ppermute(parts[step], "head", near_swap(step))
     term = weight_term(turned, dqkv)
     terms = lax.all_to_all(term.reshape(TILES, D // TILES, -1), "tile", 0, 0)
-    chunks = list(near_total(high.reshape(1), parts))
-    for step in (2, 1, 3):
-        chunks[step] = lax.ppermute(chunks[step], "head", far_swap(step))
-    grad_w = jnp.sum(terms.astype(jnp.float32), axis=0)
+    kept, before, after, across = near_total(high.reshape(1), parts)
+    chunks = [
+        kept,
+        lax.ppermute(before, "head", far_moves((1, 0), (2, 1))),
+        lax.ppermute(after, "head", far_moves((3, 0))),
+        lax.ppermute(across, "head", far_moves((0, 2), (1, 3), (2, 0), (3, 1))),
+        lax.ppermute(after, "head", far_moves((0, 1), (1, 2), (2, 3))),
+        lax.ppermute(before, "head", far_moves((3, 2), (0, 3))),
+    ]
+    grad_w = tile_total(terms)
     grad_x = sum(chunk.astype(jnp.float32) for chunk in chunks).astype(jnp.bfloat16)
     return (grad_x, grad_w)
 

time: 91.5 us -> 87.4 us (0.955)
  the two profiles are of different devices: /device:TPU:10 before, /device:TPU:1 now
where the time goes in v5:
time: 87.4 us; the launch traced here: 86.7 us
  starting transfers between devices  63.4 us (73%)
  waiting for transfers between devices  12.6 us (14%)
  Pallas kernels  6.75 us (8%)
  matrix products  1.49 us (2%)
  between operations  0.94 us (1%)
    ppermute x1, starting transfers between devices, local_step(): lax.ppermute(across, 'head', far_moves((0, 2), (1, 3), (2, 0), (3, 1)))  13.9 us
    all_to_all x1, starting transfers between devices, local_step(): terms = lax.all_to_all(term.reshape(TILES, D // TILES, -1), 'tile', 0, 0)  10.2 us
    ppermute x3, starting transfers between devices, local_step(): parts[step] = lax.ppermute(parts[step], 'head', near_swap(step))  9.66 us
    ppermute x1, starting transfers between devices, local_step(): beyond = lax.ppermute(centre, 'tile', next_pairs)  4.92 us
    ppermute x3, waiting for transfers between devices, local_step(): parts[step] = lax.ppermute(parts[step], 'head', near_swap(step))  4.7 us
    ppermute x1, starting transfers between devices, local_step(): above = lax.ppermute(pair[OWN - RIM:], 'tile', down_pairs)  4.36 us
    ppermute x1, starting transfers between devices, local_step(): lax.ppermute(column[OWN + RIM:].astype(jnp.bfloat16), 'tile', down_pairs)  4.06 us
    ppermute x1, starting transfers between devices, local_step(): from_beyond = lax.ppermute(dbeyond, 'tile', next_pairs)  3.23 us
  transfers between devices with their start and end apart: 17, of which 9 were waited for; matrix products, arithmetic and copies ran while one was open for 1% of the time, Pallas kernels for 2%

profile of v5, /device:TPU:1, one launch (start us, length us, event | category | flops | bytes accessed | tf_op | source)
XLA Modules:
  0.0 86.7 jit_solution(2107863318291922268)
XLA Ops:
  0.6 1.5 %convolution_convert_fusion = bf16[256,128]{1,0:T(8,128)(2,1)S(1)} fusion(bf16[256,1024]{1,0:T(8,128)(2,1)} %tokens_ref.1, bf16[192,1024]{1,0:T(8,128)(2,1)} %w_ref.3), kind=kOutput, calls=%fused_computation | convolution fusion | flops 67141632 | bytes 851968 | tf_op jit(solution)/shard_map/dot_general | solution.py:35
  2.2 4.4 %collective-permute-start = (bf16[192,128]{1,0:T(8,128)(2,1)S(1)}, bf16[192,128]{1,0:T(8,128)(2,1)S(1)}, u32[]{:S(2)}, u32[]{:S(2)}) collective-permute-start(bf16[192,128]{1,0:T(8,128)(2,1)S(1)} %get-tuple-element.51), channel_id=1, source_target_pairs={{0,128},{16,144},{32,160},{48,176},{64,192},{80,208},{96,224},{112... | collective-permute-start | bytes 147464 | tf_op jit(solution)/shard_map/ppermute | solution.py:270
  6.5 1.3 %collective-permute-start.1 = (bf16[192,128]{1,0:T(8,128)(2,1)S(1)}, bf16[192,128]{1,0:T(8,128)(2,1)S(1)}, u32[]{:S(2)}, u32[]{:S(2)}) collective-permute-start(bf16[192,128]{1,0:T(8,128)(2,1)S(1)} %get-tuple-element.50), channel_id=1, source_target_pairs={{128,0},{144,16},{160,32},{176,48},{192,64},{208,80},{224,96},{240... | collective-permute-start | bytes 147464 | tf_op jit(solution)/shard_map/ppermute | solution.py:271
  8.5 1.8 %prepare.1 = (bf16[256,256]{1,0:T(8,128)(2,1)S(1)}, bf16[3,640,128]{2,1,0:T(8,128)(2,1)S(1)}) custom-call(s32[1]{0:T(128)} %bitcast.2.number_ref, s32[1,8]{1,0:T(1,128)S(1)} %copy-done.3, bf16[256,1024]{1,0:T(8,128)(2,1)S(1)} %copy-done, bf16[192,1024]{1,0:T(8,128)(2,1)S(1)} %copy-done.1), custom_call_target="tpu_custom_call" | custom-call | tf_op jit(solution)/shard_map/prepare/pallas_call | solution.py:86
  11.6 4.9 %collective-permute-start.2 = (bf16[640,128]{1,0:T(8,128)(2,1)S(1)}, bf16[640,128]{1,0:T(8,128)(2,1)S(1)}, u32[]{:S(2)}, u32[]{:S(2)}) collective-permute-start(bf16[640,128]{1,0:T(8,128)(2,1)S(1)} %pad_maximum_fusion.centre_ref), channel_id=1, source_target_pairs={{16,32},{32,16},{48,64},{64,48},{80,96},{96,80},{144,160},{160,144... | collective-permute-start | bytes 491528 | tf_op jit(solution)/shard_map/ppermute | solution.py:276
  16.5 2.4 %collective-permute-start.3 = (bf16[640,128]{1,0:T(8,128)(2,1)S(1)}, bf16[640,128]{1,0:T(8,128)(2,1)S(1)}, u32[]{:S(2)}, u32[]{:S(2)}) collective-permute-start(bf16[640,128]{1,0:T(8,128)(2,1)S(1)} %pad_maximum_fusion.centre_ref), channel_id=1, source_target_pairs={{0,16},{16,0},{32,48},{48,32},{64,80},{80,64},{96,112},{112,96},{1... | collective-permute-start | bytes 491528 | tf_op jit(solution)/shard_map/ppermute | solution.py:277
  19.9 2.5 %attend.1 = (bf16[256,64]{1,0:T(8,128)(2,1)S(1)}, bf16[640,128]{1,0:T(8,128)(2,1)S(1)}, f32[640,128]{1,0:T(8,128)S(1)}, bf16[640,128]{1,0:T(8,128)(2,1)S(1)}) custom-call(bf16[256,256]{1,0:T(8,128)(2,1)S(1)} %get-tuple-element.26.query_ref, bf16[64,256]{1,0:T(8,128)(2,1)S(1)} %bitcast.8, bf16[3,640,128]{2,1,0:T(8,128)(2,1)S(1)} %get-tuple-element.27.mask_ref, ...), custom_call_target="tpu_custom_call" | custom-call | tf_op jit(solution)/shard_map/attend/pallas_call | solution.py:150
  22.5 3.2 %collective-permute-start.4 = (bf16[640,128]{1,0:T(8,128)(2,1)S(1)}, bf16[640,128]{1,0:T(8,128)(2,1)S(1)}, u32[]{:S(2)}, u32[]{:S(2)}) collective-permute-start(bf16[640,128]{1,0:T(8,128)(2,1)S(1)} %get-tuple-element.33), channel_id=1, source_target_pairs={{16,32},{32,16},{48,64},{64,48},{80,96},{96,80},{144,160},{160,144... | collective-permute-start | bytes 491528 | tf_op jit(solution)/shard_map/ppermute | solution.py:282
  25.7 1.9 %collective-permute-start.5 = (bf16[640,128]{1,0:T(8,128)(2,1)S(1)}, bf16[640,128]{1,0:T(8,128)(2,1)S(1)}, u32[]{:S(2)}, u32[]{:S(2)}) collective-permute-start(bf16[640,128]{1,0:T(8,128)(2,1)S(1)} %get-tuple-element.34), channel_id=1, source_target_pairs={{0,16},{16,0},{32,48},{48,32},{64,80},{80,64},{96,112},{112,96},{1... | collective-permute-start | bytes 491528 | tf_op jit(solution)/shard_map/ppermute | solution.py:283
  27.6 1.5 %collective-permute-done.4 = bf16[640,128]{1,0:T(8,128)(2,1)S(1)} collective-permute-done((bf16[640,128]{1,0:T(8,128)(2,1)S(1)}, bf16[640,128]{1,0:T(8,128)(2,1)S(1)}, u32[]{:S(2)}, u32[]{:S(2)}) %collective-permute-start.4) | collective-permute-done | bytes 163872 | tf_op jit(solution)/shard_map/ppermute | solution.py:282
  29.2 1.3 %collective-permute-start.6 = (bf16[192,128]{1,0:T(8,128)(2,1)S(1)}, bf16[192,128]{1,0:T(8,128)(2,1)S(1)}, u32[]{:S(2)}, u32[]{:S(2)}) collective-permute-start(bf16[192,128]{1,0:T(8,128)(2,1)S(1)} %get-tuple-element.49), channel_id=1, source_target_pairs={{128,0},{144,16},{160,32},{176,48},{192,64},{208,80},{224,96},{240... | collective-permute-start | bytes 147464 | tf_op jit(solution)/shard_map/ppermute | solution.py:285
  30.5 4.1 %collective-permute-start.7 = (bf16[192,128]{1,0:T(8,128)(2,1)S(1)}, bf16[192,128]{1,0:T(8,128)(2,1)S(1)}, u32[]{:S(2)}, u32[]{:S(2)}) collective-permute-start(bf16[192,128]{1,0:T(8,128)(2,1)S(1)} %get-tuple-element.48), channel_id=1, source_target_pairs={{0,128},{16,144},{32,160},{48,176},{64,192},{80,208},{96,224},{112... | collective-permute-start | bytes 147464 | tf_op jit(solution)/shard_map/ppermute | solution.py:286
  37.3 10.2 %all-to-all-start = ((bf16[32,32,192]{2,1,0:T(8,128)(2,1)}), bf16[32,32,192]{2,1,0:T(8,128)(2,1)S(1)}, u32[]{:S(2)}, u32[]{:S(2)}) async-start(bf16[32,32,192]{2,1,0:T(8,128)(2,1)} %bitcast.5), calls=%async_computation | async-start | bytes 1048576 | tf_op jit(solution)/shard_map/all_to_all | solution.py:291
  47.5 4.6 %collective-permute-start.10 = (bf16[64,1024]{1,0:T(8,128)(2,1)S(1)}, bf16[64,1024]{1,0:T(8,128)(2,1)S(1)}, u32[]{:S(2)}, u32[]{:S(2)}) collective-permute-start(bf16[64,1024]{1,0:T(8,128)(2,1)S(1)} %get-tuple-element.39), channel_id=1, source_target_pairs={{0,3},{1,2},{2,1},{3,0},{4,7},{5,6},{6,5},{7,4},{8,11},{9,10},{10,... | collective-permute-start | bytes 393224 | tf_op jit(solution)/shard_map/ppermute | solution.py:289
  52.2 1.9 %collective-permute-start.8 = (bf16[64,1024]{1,0:T(8,128)(2,1)S(1)}, bf16[64,1024]{1,0:T(8,128)(2,1)S(1)}, u32[]{:S(2)}, u32[]{:S(2)}) collective-permute-start(bf16[64,1024]{1,0:T(8,128)(2,1)S(1)} %get-tuple-element.37), channel_id=1, source_target_pairs={{0,1},{1,0},{2,3},{3,2},{4,5},{5,4},{6,7},{7,6},{8,9},{9,8},{10,11... | collective-permute-start | bytes 393224 | tf_op jit(solution)/shard_map/ppermute | solution.py:289
  54.1 3.1 %collective-permute-start.9 = (bf16[64,1024]{1,0:T(8,128)(2,1)S(1)}, bf16[64,1024]{1,0:T(8,128)(2,1)S(1)}, u32[]{:S(2)}, u32[]{:S(2)}) collective-permute-start(bf16[64,1024]{1,0:T(8,128)(2,1)S(1)} %get-tuple-element.38), channel_id=1, source_target_pairs={{0,2},{1,3},{2,0},{3,1},{4,6},{5,7},{6,4},{7,5},{8,10},{9,11},{10,... | collective-permute-start | bytes 393224 | tf_op jit(solution)/shard_map/ppermute | solution.py:289
  57.2 1.4 %collective-permute-done.8.refs_1_ = bf16[64,1024]{1,0:T(8,128)(2,1)S(1)} collective-permute-done((bf16[64,1024]{1,0:T(8,128)(2,1)S(1)}, bf16[64,1024]{1,0:T(8,128)(2,1)S(1)}, u32[]{:S(2)}, u32[]{:S(2)}) %collective-permute-start.8) | collective-permute-done | bytes 131104 | tf_op jit(solution)/shard_map/ppermute | solution.py:289
  58.6 3.3 %collective-permute-done.9.refs_2_ = bf16[64,1024]{1,0:T(8,128)(2,1)S(1)} collective-permute-done((bf16[64,1024]{1,0:T(8,128)(2,1)S(1)}, bf16[64,1024]{1,0:T(8,128)(2,1)S(1)}, u32[]{:S(2)}, u32[]{:S(2)}) %collective-permute-start.9) | collective-permute-done | bytes 131104 | tf_op jit(solution)/shard_map/ppermute | solution.py:289
  62.0 1.3 %collective-permute-start.11 = (bf16[16,1024]{1,0:T(8,128)(2,1)S(1)}, bf16[16,1024]{1,0:T(8,128)(2,1)S(1)}, u32[]{:S(2)}, u32[]{:S(2)}) collective-permute-start(bf16[16,1024]{1,0:T(8,128)(2,1)S(1)} %get-tuple-element.41), channel_id=1, source_target_pairs={{4,0},{5,1},{6,2},{7,3},{8,4},{9,5},{10,6},{11,7},{20,16},{21,17},... | collective-permute-start | bytes 98312 | tf_op jit(solution)/shard_map/ppermute | solution.py:295
  63.3 1.3 %collective-permute-start.12 = (bf16[16,1024]{1,0:T(8,128)(2,1)S(1)}, bf16[16,1024]{1,0:T(8,128)(2,1)S(1)}, u32[]{:S(2)}, u32[]{:S(2)}) collective-permute-start(bf16[16,1024]{1,0:T(8,128)(2,1)S(1)} %get-tuple-element.42), channel_id=1, source_target_pairs={{12,0},{13,1},{14,2},{15,3},{28,16},{29,17},{30,18},{31,19},{44,32... | collective-permute-start | bytes 98312 | tf_op jit(solution)/shard_map/ppermute | solution.py:296
  64.6 13.9 %collective-permute-start.13 = (bf16[16,1024]{1,0:T(8,128)(2,1)S(1)}, bf16[16,1024]{1,0:T(8,128)(2,1)S(1)}, u32[]{:S(2)}, u32[]{:S(2)}) collective-permute-start(bf16[16,1024]{1,0:T(8,128)(2,1)S(1)} %get-tuple-element.43), channel_id=1, source_target_pairs={{0,8},{1,9},{2,10},{3,11},{4,12},{5,13},{6,14},{7,15},{8,0},{9,1},... | collective-permute-start | bytes 98312 | tf_op jit(solution)/shard_map/ppermute | solution.py:297
  78.5 2.2 %collective-permute-start.14 = (bf16[16,1024]{1,0:T(8,128)(2,1)S(1)}, bf16[16,1024]{1,0:T(8,128)(2,1)S(1)}, u32[]{:S(2)}, u32[]{:S(2)}) collective-permute-start(bf16[16,1024]{1,0:T(8,128)(2,1)S(1)} %get-tuple-element.42), channel_id=1, source_target_pairs={{0,4},{1,5},{2,6},{3,7},{4,8},{5,9},{6,10},{7,11},{8,12},{9,13},{1... | collective-permute-start | bytes 98312 | tf_op jit(solution)/shard_map/ppermute | solution.py:298
  80.8 1.3 %collective-permute-start.15 = (bf16[16,1024]{1,0:T(8,128)(2,1)S(1)}, bf16[16,1024]{1,0:T(8,128)(2,1)S(1)}, u32[]{:S(2)}, u32[]{:S(2)}) collective-permute-start(bf16[16,1024]{1,0:T(8,128)(2,1)S(1)} %get-tuple-element.41), channel_id=1, source_target_pairs={{12,8},{13,9},{14,10},{15,11},{0,12},{1,13},{2,14},{3,15},{28,24},... | collective-permute-start | bytes 98312 | tf_op jit(solution)/shard_map/ppermute | solution.py:299
  82.8 2.6 %collective-permute-done.15 = bf16[16,1024]{1,0:T(8,128)(2,1)S(1)} collective-permute-done((bf16[16,1024]{1,0:T(8,128)(2,1)S(1)}, bf16[16,1024]{1,0:T(8,128)(2,1)S(1)}, u32[]{:S(2)}, u32[]{:S(2)}) %collective-permute-start.15) | collective-permute-done | bytes 32800 | tf_op jit(solution)/shard_map/ppermute | solution.py:299
  (31 shorter events, 7.9 us)
Async XLA Ops:
  0.6 7.2 %copy-start = (bf16[256,1024]{1,0:T(8,128)(2,1)S(1)}, bf16[256,1024]{1,0:T(8,128)(2,1)}, u32[]{:S(2)}) copy-start(bf16[256,1024]{1,0:T(8,128)(2,1)} %tokens_ref.1) | copy-start | bytes 1572868
  0.6 7.2 %copy-start.1 = (bf16[192,1024]{1,0:T(8,128)(2,1)S(1)}, bf16[192,1024]{1,0:T(8,128)(2,1)}, u32[]{:S(2)}) copy-start(bf16[192,1024]{1,0:T(8,128)(2,1)} %w_ref.3) | copy-start | bytes 1179652
  2.2 8.2 %collective-permute-start = (bf16[192,128]{1,0:T(8,128)(2,1)S(1)}, bf16[192,128]{1,0:T(8,128)(2,1)S(1)}, u32[]{:S(2)}, u32[]{:S(2)}) collective-permute-start(bf16[192,128]{1,0:T(8,128)(2,1)S(1)} %get-tuple-element.51), channel_id=1, source_target_pairs={{0,128},{16,144},{32,160},{48,176},{64,192},{80,208},{96,224},{112... | collective-permute-start | bytes 147464 | tf_op jit(solution)/shard_map/ppermute | solution.py:270
  6.5 5.0 %collective-permute-start.1 = (bf16[192,128]{1,0:T(8,128)(2,1)S(1)}, bf16[192,128]{1,0:T(8,128)(2,1)S(1)}, u32[]{:S(2)}, u32[]{:S(2)}) collective-permute-start(bf16[192,128]{1,0:T(8,128)(2,1)S(1)} %get-tuple-element.50), channel_id=1, source_target_pairs={{128,0},{144,16},{160,32},{176,48},{192,64},{208,80},{224,96},{240... | collective-permute-start | bytes 147464 | tf_op jit(solution)/shard_map/ppermute | solution.py:271
  7.8 0.7 copy-start.3
  11.6 8.3 %copy-start.2 = (bf16[256,64]{0,1:T(8,128)(2,1)S(1)}, bf16[256,64]{0,1:T(8,128)(2,1)}, u32[]{:S(2)}) copy-start(bf16[256,64]{0,1:T(8,128)(2,1)} %param.6) | copy-start | bytes 98308
  11.6 7.9 %collective-permute-start.2 = (bf16[640,128]{1,0:T(8,128)(2,1)S(1)}, bf16[640,128]{1,0:T(8,128)(2,1)S(1)}, u32[]{:S(2)}, u32[]{:S(2)}) collective-permute-start(bf16[640,128]{1,0:T(8,128)(2,1)S(1)} %pad_maximum_fusion.centre_ref), channel_id=1, source_target_pairs={{16,32},{32,16},{48,64},{64,48},{80,96},{96,80},{144,160},{160,144... | collective-permute-start | bytes 491528 | tf_op jit(solution)/shard_map/ppermute | solution.py:276
  16.5 3.4 %collective-permute-start.3 = (bf16[640,128]{1,0:T(8,128)(2,1)S(1)}, bf16[640,128]{1,0:T(8,128)(2,1)S(1)}, u32[]{:S(2)}, u32[]{:S(2)}) collective-permute-start(bf16[640,128]{1,0:T(8,128)(2,1)S(1)} %pad_maximum_fusion.centre_ref), channel_id=1, source_target_pairs={{0,16},{16,0},{32,48},{48,32},{64,80},{80,64},{96,112},{112,96},{1... | collective-permute-start | bytes 491528 | tf_op jit(solution)/shard_map/ppermute | solution.py:277
  22.5 6.6 %collective-permute-start.4 = (bf16[640,128]{1,0:T(8,128)(2,1)S(1)}, bf16[640,128]{1,0:T(8,128)(2,1)S(1)}, u32[]{:S(2)}, u32[]{:S(2)}) collective-permute-start(bf16[640,128]{1,0:T(8,128)(2,1)S(1)} %get-tuple-element.33), channel_id=1, source_target_pairs={{16,32},{32,16},{48,64},{64,48},{80,96},{96,80},{144,160},{160,144... | collective-permute-start | bytes 491528 | tf_op jit(solution)/shard_map/ppermute | solution.py:282
  25.7 3.4 %collective-permute-start.5 = (bf16[640,128]{1,0:T(8,128)(2,1)S(1)}, bf16[640,128]{1,0:T(8,128)(2,1)S(1)}, u32[]{:S(2)}, u32[]{:S(2)}) collective-permute-start(bf16[640,128]{1,0:T(8,128)(2,1)S(1)} %get-tuple-element.34), channel_id=1, source_target_pairs={{0,16},{16,0},{32,48},{48,32},{64,80},{80,64},{96,112},{112,96},{1... | collective-permute-start | bytes 491528 | tf_op jit(solution)/shard_map/ppermute | solution.py:283
  29.2 5.4 %collective-permute-start.6 = (bf16[192,128]{1,0:T(8,128)(2,1)S(1)}, bf16[192,128]{1,0:T(8,128)(2,1)S(1)}, u32[]{:S(2)}, u32[]{:S(2)}) collective-permute-start(bf16[192,128]{1,0:T(8,128)(2,1)S(1)} %get-tuple-element.49), channel_id=1, source_target_pairs={{128,0},{144,16},{160,32},{176,48},{192,64},{208,80},{224,96},{240... | collective-permute-start | bytes 147464 | tf_op jit(solution)/shard_map/ppermute | solution.py:285
  30.5 5.2 %collective-permute-start.7 = (bf16[192,128]{1,0:T(8,128)(2,1)S(1)}, bf16[192,128]{1,0:T(8,128)(2,1)S(1)}, u32[]{:S(2)}, u32[]{:S(2)}) collective-permute-start(bf16[192,128]{1,0:T(8,128)(2,1)S(1)} %get-tuple-element.48), channel_id=1, source_target_pairs={{0,128},{16,144},{32,160},{48,176},{64,192},{80,208},{96,224},{112... | collective-permute-start | bytes 147464 | tf_op jit(solution)/shard_map/ppermute | solution.py:286
  37.3 48.7 %all-to-all-start = ((bf16[32,32,192]{2,1,0:T(8,128)(2,1)}), bf16[32,32,192]{2,1,0:T(8,128)(2,1)S(1)}, u32[]{:S(2)}, u32[]{:S(2)}) async-start(bf16[32,32,192]{2,1,0:T(8,128)(2,1)} %bitcast.5), calls=%async_computation | async-start | bytes 1048576 | tf_op jit(solution)/shard_map/all_to_all | solution.py:291
  47.5 9.7 %collective-permute-start.10 = (bf16[64,1024]{1,0:T(8,128)(2,1)S(1)}, bf16[64,1024]{1,0:T(8,128)(2,1)S(1)}, u32[]{:S(2)}, u32[]{:S(2)}) collective-permute-start(bf16[64,1024]{1,0:T(8,128)(2,1)S(1)} %get-tuple-element.39), channel_id=1, source_target_pairs={{0,3},{1,2},{2,1},{3,0},{4,7},{5,6},{6,5},{7,4},{8,11},{9,10},{10,... | collective-permute-start | bytes 393224 | tf_op jit(solution)/shard_map/ppermute | solution.py:289
  52.2 6.4 %collective-permute-start.8 = (bf16[64,1024]{1,0:T(8,128)(2,1)S(1)}, bf16[64,1024]{1,0:T(8,128)(2,1)S(1)}, u32[]{:S(2)}, u32[]{:S(2)}) collective-permute-start(bf16[64,1024]{1,0:T(8,128)(2,1)S(1)} %get-tuple-element.37), channel_id=1, source_target_pairs={{0,1},{1,0},{2,3},{3,2},{4,5},{5,4},{6,7},{7,6},{8,9},{9,8},{10,11... | collective-permute-start | bytes 393224 | tf_op jit(solution)/shard_map/ppermute | solution.py:289
  54.1 7.8 %collective-permute-start.9 = (bf16[64,1024]{1,0:T(8,128)(2,1)S(1)}, bf16[64,1024]{1,0:T(8,128)(2,1)S(1)}, u32[]{:S(2)}, u32[]{:S(2)}) collective-permute-start(bf16[64,1024]{1,0:T(8,128)(2,1)S(1)} %get-tuple-element.38), channel_id=1, source_target_pairs={{0,2},{1,3},{2,0},{3,1},{4,6},{5,7},{6,4},{7,5},{8,10},{9,11},{10,... | collective-permute-start | bytes 393224 | tf_op jit(solution)/shard_map/ppermute | solution.py:289
  62.0 20.0 %collective-permute-start.11 = (bf16[16,1024]{1,0:T(8,128)(2,1)S(1)}, bf16[16,1024]{1,0:T(8,128)(2,1)S(1)}, u32[]{:S(2)}, u32[]{:S(2)}) collective-permute-start(bf16[16,1024]{1,0:T(8,128)(2,1)S(1)} %get-tuple-element.41), channel_id=1, source_target_pairs={{4,0},{5,1},{6,2},{7,3},{8,4},{9,5},{10,6},{11,7},{20,16},{21,17},... | collective-permute-start | bytes 98312 | tf_op jit(solution)/shard_map/ppermute | solution.py:295
  63.3 18.8 %collective-permute-start.12 = (bf16[16,1024]{1,0:T(8,128)(2,1)S(1)}, bf16[16,1024]{1,0:T(8,128)(2,1)S(1)}, u32[]{:S(2)}, u32[]{:S(2)}) collective-permute-start(bf16[16,1024]{1,0:T(8,128)(2,1)S(1)} %get-tuple-element.42), channel_id=1, source_target_pairs={{12,0},{13,1},{14,2},{15,3},{28,16},{29,17},{30,18},{31,19},{44,32... | collective-permute-start | bytes 98312 | tf_op jit(solution)/shard_map/ppermute | solution.py:296
  64.6 17.5 %collective-permute-start.13 = (bf16[16,1024]{1,0:T(8,128)(2,1)S(1)}, bf16[16,1024]{1,0:T(8,128)(2,1)S(1)}, u32[]{:S(2)}, u32[]{:S(2)}) collective-permute-start(bf16[16,1024]{1,0:T(8,128)(2,1)S(1)} %get-tuple-element.43), channel_id=1, source_target_pairs={{0,8},{1,9},{2,10},{3,11},{4,12},{5,13},{6,14},{7,15},{8,0},{9,1},... | collective-permute-start | bytes 98312 | tf_op jit(solution)/shard_map/ppermute | solution.py:297
  78.5 4.3 %collective-permute-start.14 = (bf16[16,1024]{1,0:T(8,128)(2,1)S(1)}, bf16[16,1024]{1,0:T(8,128)(2,1)S(1)}, u32[]{:S(2)}, u32[]{:S(2)}) collective-permute-start(bf16[16,1024]{1,0:T(8,128)(2,1)S(1)} %get-tuple-element.42), channel_id=1, source_target_pairs={{0,4},{1,5},{2,6},{3,7},{4,8},{5,9},{6,10},{7,11},{8,12},{9,13},{1... | collective-permute-start | bytes 98312 | tf_op jit(solution)/shard_map/ppermute | solution.py:298
  80.8 4.6 %collective-permute-start.15 = (bf16[16,1024]{1,0:T(8,128)(2,1)S(1)}, bf16[16,1024]{1,0:T(8,128)(2,1)S(1)}, u32[]{:S(2)}, u32[]{:S(2)}) collective-permute-start(bf16[16,1024]{1,0:T(8,128)(2,1)S(1)} %get-tuple-element.41), channel_id=1, source_target_pairs={{12,8},{13,9},{14,10},{15,11},{0,12},{1,13},{2,14},{3,15},{28,24},... | collective-permute-start | bytes 98312 | tf_op jit(solution)/shard_map/ppermute | solution.py:299

commit v6 on v5

--- a/solution.py
+++ b/solution.py
@@ -21,8 +21,10 @@
 BARRED = -1e30
 
 directions = ((-1, -1), (-1, 0), (-1, 1), (0, -1), (0, 1), (1, -1), (1, 0), (1, 1))
-down_pairs = [(tile, tile + GRID_COLS) for tile in range(TILES - GRID_COLS)]
-up_pairs = [(target, source) for source, target in down_pairs]
+fold_pairs = [(tile, tile ^ GRID_COLS) for tile in range(TILES)]
+middle_pairs = [
+    (tile, tile ^ (3 * GRID_COLS)) for tile in range(TILES) if 0 < tile // GRID_COLS < GRID_ROWS - 1
+]
 twin_pairs = [(tile, tile ^ 1) for tile in range(TILES)]
 next_pairs = [
     (tile, tile + 2 * (tile & 1) - 1)
@@ -103,10 +105,11 @@
 
 
 def attend_kernel(
-    query_ref, grad_ref, mask_ref, left_ref, centre_ref, right_ref,
-    dquery_ref, dleft_ref, dcentre_ref, dright_ref, scores_ref, low_ref,
+    query_ref, grad_ref, mask_ref, beyond_ref, centre_ref, twin_ref,
+    dbeyond_ref, dtwin_ref, probs_ref, probs_low_ref, row_dot_ref, dquery_ref,
+    scores_ref, low_ref,
 ):
-    pairs = (left_ref, centre_ref, right_ref)
+    pairs = (beyond_ref, centre_ref, twin_ref)
     query = query_ref[...]
     grad = jnp.concatenate([jnp.zeros((WIDTH, OWN), jnp.bfloat16), grad_ref[...]], axis=0)
     highest = None
@@ -134,28 +137,38 @@
         attended = attended + contract(pairs[block][...], low, 0, 0)
     row_dot = jnp.sum(attended * grad.astype(jnp.float32), axis=0, keepdims=True)
     dquery = jnp.zeros((128, OWN), jnp.float32)
-    for block, out_ref in enumerate((dleft_ref, dcentre_ref, dright_ref)):
+    for block, out_ref in ((0, dbeyond_ref), (2, dtwin_ref)):
         rows = pl.ds(block * COLUMN, COLUMN)
-        pair = pairs[block][...]
-        grad_probs = contract(pair, grad, 1, 0)
-        grad_scores = (scores_ref[rows, :] * (grad_probs - row_dot)).astype(jnp.bfloat16)
-        dpair = contract(grad_scores, query[:128], 1, 1) + contract(low_ref[rows, :], grad, 1, 1)
-        out_ref[...] = dpair.astype(out_ref.dtype)
-        dquery = dquery + contract(pair, grad_scores, 0, 0)
-    dquery_ref[...] = jnp.transpose(dquery[:WIDTH] * WIDTH**-0.5).astype(dquery_ref.dtype)
-
-
-def attend(query, grad_turned, mask, left, centre, right):
+        dpair, dquery = block_backward(
+            pairs[block][...], query, grad, scores_ref[rows, :], low_ref[rows, :], row_dot, dquery
+        )
+        out_ref[...] = dpair.astype(jnp.bfloat16)
+    probs_ref[...] = scores_ref[COLUMN : 2 * COLUMN, :]
+    probs_low_ref[...] = low_ref[COLUMN : 2 * COLUMN, :]
+    row_dot_ref[...] = row_dot
+    dquery_ref[...] = dquery
+
+
+def block_backward(pair, query, grad, probs, low, row_dot, dquery):
+    grad_probs = contract(pair, grad, 1, 0)
+    grad_scores = (probs * (grad_probs - row_dot)).astype(jnp.bfloat16)
+    dpair = contract(grad_scores, query[:128], 1, 1) + contract(low, grad, 1, 1)
+    return dpair, dquery + contract(pair, grad_scores, 0, 0)
+
+
+def attend(query, grad_turned, mask, beyond, centre, twin):
     vmem = pl.BlockSpec(memory_space=pltpu.VMEM)
     return pl.pallas_call(
         attend_kernel,
         in_specs=[vmem] * 6,
-        out_specs=[vmem] * 4,
+        out_specs=[vmem] * 6,
         out_shape=[
-            jax.ShapeDtypeStruct((OWN, WIDTH), jnp.bfloat16),
             jax.ShapeDtypeStruct((COLUMN, 128), jnp.bfloat16),
-            jax.ShapeDtypeStruct((COLUMN, 128), jnp.float32),
             jax.ShapeDtypeStruct((COLUMN, 128), jnp.bfloat16),
+            jax.ShapeDtypeStruct((COLUMN, OWN), jnp.float32),
+            jax.ShapeDtypeStruct((COLUMN, OWN), jnp.bfloat16),
+            jax.ShapeDtypeStruct((1, OWN), jnp.float32),
+            jax.ShapeDtypeStruct((128, OWN), jnp.float32),
         ],
         scratch_shapes=[
             pltpu.VMEM((3 * COLUMN, OWN), jnp.float32),
@@ -163,16 +176,47 @@
         ],
         compiler_params=pltpu.CompilerParams(vmem_limit_bytes=16 << 20),
         name="attend",
-    )(query, grad_turned, mask, left, centre, right)
+    )(query, grad_turned, mask, beyond, centre, twin)
+
+
+def finish_kernel(
+    query_ref, grad_ref, centre_ref, probs_ref, low_ref, row_dot_ref, dquery_ref,
+    out_query_ref, out_pair_ref,
+):
+    grad = jnp.concatenate([jnp.zeros((WIDTH, OWN), jnp.bfloat16), grad_ref[...]], axis=0)
+    dpair, dquery = block_backward(
+        centre_ref[...], query_ref[...], grad, probs_ref[...], low_ref[...], row_dot_ref[...],
+        dquery_ref[...],
+    )
+    out_pair_ref[...] = dpair
+    out_query_ref[...] = jnp.transpose(dquery[:WIDTH] * WIDTH**-0.5).astype(jnp.bfloat16)
+
+
+def finish(query, grad_turned, centre, probs, low, row_dot, dquery):
+    vmem = pl.BlockSpec(memory_space=pltpu.VMEM)
+    return pl.pallas_call(
+        finish_kernel,
+        in_specs=[vmem] * 7,
+        out_specs=[vmem] * 2,
+        out_shape=[
+            jax.ShapeDtypeStruct((OWN, WIDTH), jnp.bfloat16),
+            jax.ShapeDtypeStruct((COLUMN, 128), jnp.float32),
+        ],
+        compiler_params=pltpu.CompilerParams(vmem_limit_bytes=16 << 20),
+        name="finish",
+    )(query, grad_turned, centre, probs, low, row_dot, dquery)
 
 
 def return_kernel(
-    near_ref, column_ref, below_ref, above_ref, dquery_ref, w_ref,
+    near_ref, odd_ref, column_ref, fold_ref, middle_ref, dquery_ref, w_ref,
     dqkv_ref, kept_ref, first_ref, second_ref, third_ref, sum_ref, rows_ref,
 ):
     sum_ref[...] = column_ref[RIM : RIM + OWN]
-    sum_ref[OWN - RIM :] += below_ref[...].astype(jnp.float32)
-    sum_ref[:RIM] += above_ref[...].astype(jnp.float32)
+    odd = odd_ref[0] == 1
+    fold = fold_ref[...].astype(jnp.float32)
+    middle = middle_ref[...].astype(jnp.float32)
+    sum_ref[OWN - RIM :] += jnp.where(odd, middle, fold)
+    sum_ref[:RIM] += jnp.where(odd, fold, middle)
     dqkv = jnp.concatenate([dquery_ref[...], sum_ref[...].astype(jnp.bfloat16)], axis=1)
     dqkv_ref[...] = dqkv
     rows_ref[...] = dqkv.reshape(HEADS, S, 3 * WIDTH)
@@ -184,12 +228,12 @@
         out_ref[...] = contract(chosen, w, 1, 0).astype(jnp.bfloat16)
 
 
-def project_back(near, column, from_below, from_above, dquery, w_qkv):
+def project_back(near, odd, column, from_fold, from_middle, dquery, w_qkv):
     vmem = pl.BlockSpec(memory_space=pltpu.VMEM)
     part = jax.ShapeDtypeStruct((OWN // NEAR, D), jnp.bfloat16)
     return pl.pallas_call(
         return_kernel,
-        in_specs=[pl.BlockSpec(memory_space=pltpu.SMEM)] + [vmem] * 5,
+        in_specs=[pl.BlockSpec(memory_space=pltpu.SMEM)] * 2 + [vmem] * 5,
         out_specs=[vmem] * 5,
         out_shape=[jax.ShapeDtypeStruct((OWN, 3 * WIDTH), jnp.bfloat16)] + [part] * 4,
         scratch_shapes=[
@@ -198,7 +242,7 @@
         ],
         compiler_params=pltpu.CompilerParams(vmem_limit_bytes=8 << 20),
         name="project_back",
-    )(near, column, from_below, from_above, dquery, w_qkv)
+    )(near, odd, column, from_fold, from_middle, dquery, w_qkv)
 
 
 def weight_kernel(turned_ref, dqkv_ref, out_ref):
@@ -267,24 +311,33 @@
     head = lax.axis_index("head")
     near, high = head & (NEAR - 1), head >> 2
     pair = contract(tokens, w_qkv[WIDTH:], 1, 1).astype(jnp.bfloat16)
-    above = lax.ppermute(pair[OWN - RIM :], "tile", down_pairs)
-    below = lax.ppermute(pair[:RIM], "tile", up_pairs)
+    odd = (number // GRID_COLS) & 1
+    fold = jnp.where(odd == 1, pair[:RIM], pair[OWN - RIM :])
+    middle = jnp.where(odd == 1, pair[OWN - RIM :], pair[:RIM])
+    fold = lax.ppermute(fold, "tile", fold_pairs)
+    middle = lax.ppermute(middle, "tile", middle_pairs)
     query, mask = prepare(number.reshape(1), edge_valid, tokens, w_qkv)
-    above, below, query, mask = lax.optimization_barrier((above, below, query, mask))
+    fold, middle, query, mask = lax.optimization_barrier((fold, middle, query, mask))
+    above = jnp.where(odd == 1, fold, middle)
+    below = jnp.where(odd == 1, middle, fold)
     turned = jnp.transpose(tokens)
     centre = jnp.concatenate([above, pair, below], axis=0)
     beyond = lax.ppermute(centre, "tile", next_pairs)
     twin = lax.ppermute(centre, "tile", twin_pairs)
     beyond, twin, turned = lax.optimization_barrier((beyond, twin, turned))
-    dquery, dbeyond, dcentre, dtwin = attend(
-        query, jnp.transpose(grad_out), mask, beyond, centre, twin
-    )
+    grad_turned = jnp.transpose(grad_out)
+    dbeyond, dtwin, *saved = attend(query, grad_turned, mask, beyond, centre, twin)
     from_beyond = lax.ppermute(dbeyond, "tile", next_pairs)
     from_twin = lax.ppermute(dtwin, "tile", twin_pairs)
+    dquery, dcentre = finish(query, grad_turned, centre, *saved)
     column = dcentre + from_beyond.astype(jnp.float32) + from_twin.astype(jnp.float32)
-    from_below = lax.ppermute(column[:RIM].astype(jnp.bfloat16), "tile", up_pairs)
-    from_above = lax.ppermute(column[OWN + RIM :].astype(jnp.bfloat16), "tile", down_pairs)
-    dqkv, *parts = project_back(near.reshape(1), column, from_below, from_above, dquery, w_qkv)
+    upper = column[:RIM].astype(jnp.bfloat16)
+    lower = column[OWN + RIM :].astype(jnp.bfloat16)
+    from_fold = lax.ppermute(jnp.where(odd == 1, upper, lower), "tile", fold_pairs)
+    from_middle = lax.ppermute(jnp.where(odd == 1, lower, upper), "tile", middle_pairs)
+    dqkv, *parts = project_back(
+        near.reshape(1), odd.reshape(1), column, from_fold, from_middle, dquery, w_qkv
+    )
     for step in (2, 1, 3):
         parts[step] = lax.ppermute(parts[step], "head", near_swap(step))
     term = weight_term(turned, dqkv)

time: 87.4 us -> 85.5 us (0.978)
    ppermute x1, starting transfers between devices: 2.39 us -> 4.51 us  [local_step(): twin = lax.ppermute(centre, 'tile', twin_pairs)]
    ppermute x4, waiting for transfers between devices: 2.38 us -> 0.8 us  [the longest x1 0.79 us: local_step(): lax.ppermute(jnp.where(odd == 1, upper, lower), 'tile', fold_pairs)]
    ppermute x1, starting transfers between devices: 3.23 us -> 1.92 us  [local_step(): from_beyond = lax.ppermute(dbeyond, 'tile', next_pairs)]
    ppermute x1, starting transfers between devices: 4.92 us -> 3.96 us  [local_step(): beyond = lax.ppermute(centre, 'tile', next_pairs)]
    pallas_call x1 -> x2, Pallas kernels: 2.54 us -> 2.56 us  [the longest x1 2.03 us: attend(): pl.pallas_call(attend_kernel, in_specs=[vmem] * 6, out_specs=[vmem] * 6,...]
  transfers between devices with their start and end apart: 17 -> 17, of which waited for: 9 -> 7; matrix products, arithmetic and copies ran while one was open for 1% -> 1% of each run, Pallas kernels for 2% -> 3%
where the time goes in v6:
time: 85.5 us; the launch traced here: 84.8 us
  starting transfers between devices  62.8 us (73%)
  waiting for transfers between devices  11.8 us (14%)
  Pallas kernels  6.79 us (8%)
  matrix products  1.49 us (2%)
  between operations  0.99 us (1%)
    ppermute x1, starting transfers between devices, local_step(): lax.ppermute(across, 'head', far_moves((0, 2), (1, 3), (2, 0), (3, 1)))  13.9 us
    ppermute x3, starting transfers between devices, local_step(): parts[step] = lax.ppermute(parts[step], 'head', near_swap(step))  9.65 us
    all_to_all x1, starting transfers between devices, local_step(): terms = lax.all_to_all(term.reshape(TILES, D // TILES, -1), 'tile', 0, 0)  9.55 us
    ppermute x1, starting transfers between devices, local_step(): lax.ppermute(jnp.where(odd == 1, upper, lower), 'tile', fold_pairs)  5.58 us
    ppermute x3, waiting for transfers between devices, local_step(): parts[step] = lax.ppermute(parts[step], 'head', near_swap(step))  4.69 us
    ppermute x1, starting transfers between devices, local_step(): twin = lax.ppermute(centre, 'tile', twin_pairs)  4.51 us
    ppermute x1, starting transfers between devices, local_step(): fold = lax.ppermute(fold, 'tile', fold_pairs)  4.36 us
    ppermute x1, starting transfers between devices, local_step(): beyond = lax.ppermute(centre, 'tile', next_pairs)  3.96 us
  transfers between devices with their start and end apart: 17, of which 7 were waited for; matrix products, arithmetic and copies ran while one was open for 1% of the time, Pallas kernels for 3%

profile of v6, /device:TPU:1, one launch (start us, length us, event | category | flops | bytes accessed | tf_op | source)
XLA Modules:
  0.0 84.8 jit_solution(14088516884786983291)
XLA Ops:
  0.7 1.5 %convolution_convert_fusion = bf16[256,128]{1,0:T(8,128)(2,1)S(1)} fusion(bf16[256,1024]{1,0:T(8,128)(2,1)} %tokens_ref.1, bf16[192,1024]{1,0:T(8,128)(2,1)} %w_ref.3), kind=kOutput, calls=%fused_computation | convolution fusion | flops 67141632 | bytes 851968 | tf_op jit(solution)/shard_map/dot_general | solution.py:37
  2.2 4.4 %collective-permute-start = (bf16[192,128]{1,0:T(8,128)(2,1)S(1)}, bf16[192,128]{1,0:T(8,128)(2,1)S(1)}, u32[]{:S(2)}, u32[]{:S(2)}) collective-permute-start(bf16[192,128]{1,0:T(8,128)(2,1)S(1)} %get-tuple-element.61), channel_id=1, source_target_pairs={{0,128},{16,144},{32,160},{48,176},{64,192},{80,208},{96,224},{112... | collective-permute-start | bytes 147464 | tf_op jit(solution)/shard_map/ppermute | solution.py:317
  7.3 1.8 %prepare.1 = (bf16[256,256]{1,0:T(8,128)(2,1)S(1)}, bf16[3,640,128]{2,1,0:T(8,128)(2,1)S(1)}) custom-call(s32[1]{0:T(128)} %bitcast.3.number_ref, s32[1,8]{1,0:T(1,128)S(1)} %copy-done.3, bf16[256,1024]{1,0:T(8,128)(2,1)S(1)} %copy-done, bf16[192,1024]{1,0:T(8,128)(2,1)S(1)} %copy-done.1), custom_call_target="tpu_custom_call" | custom-call | tf_op jit(solution)/shard_map/prepare/pallas_call | solution.py:88
  9.2 4.0 %collective-permute-start.2 = (bf16[640,128]{1,0:T(8,128)(2,1)S(1)}, bf16[640,128]{1,0:T(8,128)(2,1)S(1)}, u32[]{:S(2)}, u32[]{:S(2)}) collective-permute-start(bf16[640,128]{1,0:T(8,128)(2,1)S(1)} %pad_maximum_fusion.centre_ref), channel_id=1, source_target_pairs={{16,32},{32,16},{48,64},{64,48},{80,96},{96,80},{144,160},{160,144... | collective-permute-start | bytes 491528 | tf_op jit(solution)/shard_map/ppermute | solution.py:325
  13.1 4.5 %collective-permute-start.3 = (bf16[640,128]{1,0:T(8,128)(2,1)S(1)}, bf16[640,128]{1,0:T(8,128)(2,1)S(1)}, u32[]{:S(2)}, u32[]{:S(2)}) collective-permute-start(bf16[640,128]{1,0:T(8,128)(2,1)S(1)} %pad_maximum_fusion.centre_ref), channel_id=1, source_target_pairs={{0,16},{16,0},{32,48},{48,32},{64,80},{80,64},{96,112},{112,96},{1... | collective-permute-start | bytes 491528 | tf_op jit(solution)/shard_map/ppermute | solution.py:326
  18.7 2.0 %attend.1 = (bf16[640,128]{1,0:T(8,128)(2,1)S(1)}, bf16[640,128]{1,0:T(8,128)(2,1)S(1)}, f32[640,256]{1,0:T(8,128)S(1)}, bf16[640,256]{1,0:T(8,128)(2,1)S(1)}, f...) custom-call(bf16[256,256]{1,0:T(8,128)(2,1)S(1)} %get-tuple-element.30.query_ref, bf16[64,256]{1,0:T(8,128)(2,1)S(1)} %bitcast.9, ...), custom_call_target="tpu_custom_call" | custom-call | tf_op jit(solution)/shard_map/attend/pallas_call | solution.py:161
  20.7 1.9 %collective-permute-start.4 = (bf16[640,128]{1,0:T(8,128)(2,1)S(1)}, bf16[640,128]{1,0:T(8,128)(2,1)S(1)}, u32[]{:S(2)}, u32[]{:S(2)}) collective-permute-start(bf16[640,128]{1,0:T(8,128)(2,1)S(1)} %get-tuple-element.41), channel_id=1, source_target_pairs={{16,32},{32,16},{48,64},{64,48},{80,96},{96,80},{144,160},{160,144... | collective-permute-start | bytes 491528 | tf_op jit(solution)/shard_map/ppermute | solution.py:330
  22.6 1.9 %collective-permute-start.5 = (bf16[640,128]{1,0:T(8,128)(2,1)S(1)}, bf16[640,128]{1,0:T(8,128)(2,1)S(1)}, u32[]{:S(2)}, u32[]{:S(2)}) collective-permute-start(bf16[640,128]{1,0:T(8,128)(2,1)S(1)} %get-tuple-element.42), channel_id=1, source_target_pairs={{0,16},{16,0},{32,48},{48,32},{64,80},{80,64},{96,112},{112,96},{1... | collective-permute-start | bytes 491528 | tf_op jit(solution)/shard_map/ppermute | solution.py:331
  25.1 2.2 %collective-permute-done.4 = bf16[640,128]{1,0:T(8,128)(2,1)S(1)} collective-permute-done((bf16[640,128]{1,0:T(8,128)(2,1)S(1)}, bf16[640,128]{1,0:T(8,128)(2,1)S(1)}, u32[]{:S(2)}, u32[]{:S(2)}) %collective-permute-start.4) | collective-permute-done | bytes 163872 | tf_op jit(solution)/shard_map/ppermute | solution.py:330
  27.4 5.6 %collective-permute-start.6 = (bf16[192,128]{1,0:T(8,128)(2,1)S(1)}, bf16[192,128]{1,0:T(8,128)(2,1)S(1)}, u32[]{:S(2)}, u32[]{:S(2)}) collective-permute-start(bf16[192,128]{1,0:T(8,128)(2,1)S(1)} %get-tuple-element.57), channel_id=1, source_target_pairs={{0,128},{16,144},{32,160},{48,176},{64,192},{80,208},{96,224},{112... | collective-permute-start | bytes 147464 | tf_op jit(solution)/shard_map/ppermute | solution.py:336
  33.7 0.8 collective-permute-done.6.fold_ref
  35.0 1.1 %weight_term.1 = bf16[1024,192]{1,0:T(8,128)(2,1)} custom-call(bf16[1024,256]{1,0:T(8,128)(2,1)S(1)} %bitcast.8, bf16[256,192]{1,0:T(8,128)(2,1)S(1)} %get-tuple-element.53.dqkv_ref), custom_call_target="tpu_custom_call" | custom-call | tf_op jit(solution)/shard_map/weight_term/pallas_call | solution.py:254
  36.1 9.6 %all-to-all-start = ((bf16[32,32,192]{2,1,0:T(8,128)(2,1)}), bf16[32,32,192]{2,1,0:T(8,128)(2,1)S(1)}, u32[]{:S(2)}, u32[]{:S(2)}) async-start(bf16[32,32,192]{2,1,0:T(8,128)(2,1)} %bitcast.6), calls=%async_computation | async-start | bytes 1048576 | tf_op jit(solution)/shard_map/all_to_all | solution.py:344
  45.7 4.6 %collective-permute-start.10 = (bf16[64,1024]{1,0:T(8,128)(2,1)S(1)}, bf16[64,1024]{1,0:T(8,128)(2,1)S(1)}, u32[]{:S(2)}, u32[]{:S(2)}) collective-permute-start(bf16[64,1024]{1,0:T(8,128)(2,1)S(1)} %get-tuple-element.47), channel_id=1, source_target_pairs={{0,3},{1,2},{2,1},{3,0},{4,7},{5,6},{6,5},{7,4},{8,11},{9,10},{10,... | collective-permute-start | bytes 393224 | tf_op jit(solution)/shard_map/ppermute | solution.py:342
  50.3 1.9 %collective-permute-start.8 = (bf16[64,1024]{1,0:T(8,128)(2,1)S(1)}, bf16[64,1024]{1,0:T(8,128)(2,1)S(1)}, u32[]{:S(2)}, u32[]{:S(2)}) collective-permute-start(bf16[64,1024]{1,0:T(8,128)(2,1)S(1)} %get-tuple-element.45), channel_id=1, source_target_pairs={{0,1},{1,0},{2,3},{3,2},{4,5},{5,4},{6,7},{7,6},{8,9},{9,8},{10,11... | collective-permute-start | bytes 393224 | tf_op jit(solution)/shard_map/ppermute | solution.py:342
  52.2 3.1 %collective-permute-start.9 = (bf16[64,1024]{1,0:T(8,128)(2,1)S(1)}, bf16[64,1024]{1,0:T(8,128)(2,1)S(1)}, u32[]{:S(2)}, u32[]{:S(2)}) collective-permute-start(bf16[64,1024]{1,0:T(8,128)(2,1)S(1)} %get-tuple-element.46), channel_id=1, source_target_pairs={{0,2},{1,3},{2,0},{3,1},{4,6},{5,7},{6,4},{7,5},{8,10},{9,11},{10,... | collective-permute-start | bytes 393224 | tf_op jit(solution)/shard_map/ppermute | solution.py:342
  55.3 1.4 %collective-permute-done.8.refs_1_ = bf16[64,1024]{1,0:T(8,128)(2,1)S(1)} collective-permute-done((bf16[64,1024]{1,0:T(8,128)(2,1)S(1)}, bf16[64,1024]{1,0:T(8,128)(2,1)S(1)}, u32[]{:S(2)}, u32[]{:S(2)}) %collective-permute-start.8) | collective-permute-done | bytes 131104 | tf_op jit(solution)/shard_map/ppermute | solution.py:342
  56.7 3.3 %collective-permute-done.9.refs_2_ = bf16[64,1024]{1,0:T(8,128)(2,1)S(1)} collective-permute-done((bf16[64,1024]{1,0:T(8,128)(2,1)S(1)}, bf16[64,1024]{1,0:T(8,128)(2,1)S(1)}, u32[]{:S(2)}, u32[]{:S(2)}) %collective-permute-start.9) | collective-permute-done | bytes 131104 | tf_op jit(solution)/shard_map/ppermute | solution.py:342
  60.1 1.3 %collective-permute-start.11 = (bf16[16,1024]{1,0:T(8,128)(2,1)S(1)}, bf16[16,1024]{1,0:T(8,128)(2,1)S(1)}, u32[]{:S(2)}, u32[]{:S(2)}) collective-permute-start(bf16[16,1024]{1,0:T(8,128)(2,1)S(1)} %get-tuple-element.49), channel_id=1, source_target_pairs={{4,0},{5,1},{6,2},{7,3},{8,4},{9,5},{10,6},{11,7},{20,16},{21,17},... | collective-permute-start | bytes 98312 | tf_op jit(solution)/shard_map/ppermute | solution.py:348
  61.4 1.3 %collective-permute-start.12 = (bf16[16,1024]{1,0:T(8,128)(2,1)S(1)}, bf16[16,1024]{1,0:T(8,128)(2,1)S(1)}, u32[]{:S(2)}, u32[]{:S(2)}) collective-permute-start(bf16[16,1024]{1,0:T(8,128)(2,1)S(1)} %get-tuple-element.50), channel_id=1, source_target_pairs={{12,0},{13,1},{14,2},{15,3},{28,16},{29,17},{30,18},{31,19},{44,32... | collective-permute-start | bytes 98312 | tf_op jit(solution)/shard_map/ppermute | solution.py:349
  62.7 13.9 %collective-permute-start.13 = (bf16[16,1024]{1,0:T(8,128)(2,1)S(1)}, bf16[16,1024]{1,0:T(8,128)(2,1)S(1)}, u32[]{:S(2)}, u32[]{:S(2)}) collective-permute-start(bf16[16,1024]{1,0:T(8,128)(2,1)S(1)} %get-tuple-element.51), channel_id=1, source_target_pairs={{0,8},{1,9},{2,10},{3,11},{4,12},{5,13},{6,14},{7,15},{8,0},{9,1},... | collective-permute-start | bytes 98312 | tf_op jit(solution)/shard_map/ppermute | solution.py:350
  76.6 2.2 %collective-permute-start.14 = (bf16[16,1024]{1,0:T(8,128)(2,1)S(1)}, bf16[16,1024]{1,0:T(8,128)(2,1)S(1)}, u32[]{:S(2)}, u32[]{:S(2)}) collective-permute-start(bf16[16,1024]{1,0:T(8,128)(2,1)S(1)} %get-tuple-element.50), channel_id=1, source_target_pairs={{0,4},{1,5},{2,6},{3,7},{4,8},{5,9},{6,10},{7,11},{8,12},{9,13},{1... | collective-permute-start | bytes 98312 | tf_op jit(solution)/shard_map/ppermute | solution.py:351
  78.9 1.3 %collective-permute-start.15 = (bf16[16,1024]{1,0:T(8,128)(2,1)S(1)}, bf16[16,1024]{1,0:T(8,128)(2,1)S(1)}, u32[]{:S(2)}, u32[]{:S(2)}) collective-permute-start(bf16[16,1024]{1,0:T(8,128)(2,1)S(1)} %get-tuple-element.49), channel_id=1, source_target_pairs={{12,8},{13,9},{14,10},{15,11},{0,12},{1,13},{2,14},{3,15},{28,24},... | collective-permute-start | bytes 98312 | tf_op jit(solution)/shard_map/ppermute | solution.py:352
  80.9 2.6 %collective-permute-done.15 = bf16[16,1024]{1,0:T(8,128)(2,1)S(1)} collective-permute-done((bf16[16,1024]{1,0:T(8,128)(2,1)S(1)}, bf16[16,1024]{1,0:T(8,128)(2,1)S(1)}, u32[]{:S(2)}, u32[]{:S(2)}) %collective-permute-start.15) | collective-permute-done | bytes 32800 | tf_op jit(solution)/shard_map/ppermute | solution.py:352
  (33 shorter events, 5.6 us)
Async XLA Ops:
  0.6 6.6 %copy-start = (bf16[256,1024]{1,0:T(8,128)(2,1)S(1)}, bf16[256,1024]{1,0:T(8,128)(2,1)}, u32[]{:S(2)}) copy-start(bf16[256,1024]{1,0:T(8,128)(2,1)} %tokens_ref.1) | copy-start | bytes 1572868
  0.7 6.6 %copy-start.1 = (bf16[192,1024]{1,0:T(8,128)(2,1)S(1)}, bf16[192,1024]{1,0:T(8,128)(2,1)}, u32[]{:S(2)}) copy-start(bf16[192,1024]{1,0:T(8,128)(2,1)} %w_ref.3) | copy-start | bytes 1179652
  2.2 6.9 %collective-permute-start = (bf16[192,128]{1,0:T(8,128)(2,1)S(1)}, bf16[192,128]{1,0:T(8,128)(2,1)S(1)}, u32[]{:S(2)}, u32[]{:S(2)}) collective-permute-start(bf16[192,128]{1,0:T(8,128)(2,1)S(1)} %get-tuple-element.61), channel_id=1, source_target_pairs={{0,128},{16,144},{32,160},{48,176},{64,192},{80,208},{96,224},{112... | collective-permute-start | bytes 147464 | tf_op jit(solution)/shard_map/ppermute | solution.py:317
  6.6 0.7 copy-start.3
  6.6 2.5 %collective-permute-start.1 = (bf16[192,128]{1,0:T(8,128)(2,1)S(1)}, bf16[192,128]{1,0:T(8,128)(2,1)S(1)}, u32[]{:S(2)}, u32[]{:S(2)}) collective-permute-start(bf16[192,128]{1,0:T(8,128)(2,1)S(1)} %get-tuple-element.60), channel_id=1, source_target_pairs={{128,256},{144,272},{160,288},{176,304},{192,320},{208,336},{224,3... | collective-permute-start | bytes 147464 | tf_op jit(solution)/shard_map/ppermute | solution.py:318
  9.2 9.5 %copy-start.2 = (bf16[256,64]{0,1:T(8,128)(2,1)S(1)}, bf16[256,64]{0,1:T(8,128)(2,1)}, u32[]{:S(2)}) copy-start(bf16[256,64]{0,1:T(8,128)(2,1)} %param.6) | copy-start | bytes 98308
  9.2 8.7 %collective-permute-start.2 = (bf16[640,128]{1,0:T(8,128)(2,1)S(1)}, bf16[640,128]{1,0:T(8,128)(2,1)S(1)}, u32[]{:S(2)}, u32[]{:S(2)}) collective-permute-start(bf16[640,128]{1,0:T(8,128)(2,1)S(1)} %pad_maximum_fusion.centre_ref), channel_id=1, source_target_pairs={{16,32},{32,16},{48,64},{64,48},{80,96},{96,80},{144,160},{160,144... | collective-permute-start | bytes 491528 | tf_op jit(solution)/shard_map/ppermute | solution.py:325
  13.1 5.5 %collective-permute-start.3 = (bf16[640,128]{1,0:T(8,128)(2,1)S(1)}, bf16[640,128]{1,0:T(8,128)(2,1)S(1)}, u32[]{:S(2)}, u32[]{:S(2)}) collective-permute-start(bf16[640,128]{1,0:T(8,128)(2,1)S(1)} %pad_maximum_fusion.centre_ref), channel_id=1, source_target_pairs={{0,16},{16,0},{32,48},{48,32},{64,80},{80,64},{96,112},{112,96},{1... | collective-permute-start | bytes 491528 | tf_op jit(solution)/shard_map/ppermute | solution.py:326
  20.7 6.6 %collective-permute-start.4 = (bf16[640,128]{1,0:T(8,128)(2,1)S(1)}, bf16[640,128]{1,0:T(8,128)(2,1)S(1)}, u32[]{:S(2)}, u32[]{:S(2)}) collective-permute-start(bf16[640,128]{1,0:T(8,128)(2,1)S(1)} %get-tuple-element.41), channel_id=1, source_target_pairs={{16,32},{32,16},{48,64},{64,48},{80,96},{96,80},{144,160},{160,144... | collective-permute-start | bytes 491528 | tf_op jit(solution)/shard_map/ppermute | solution.py:330
  22.6 4.7 %collective-permute-start.5 = (bf16[640,128]{1,0:T(8,128)(2,1)S(1)}, bf16[640,128]{1,0:T(8,128)(2,1)S(1)}, u32[]{:S(2)}, u32[]{:S(2)}) collective-permute-start(bf16[640,128]{1,0:T(8,128)(2,1)S(1)} %get-tuple-element.42), channel_id=1, source_target_pairs={{0,16},{16,0},{32,48},{48,32},{64,80},{80,64},{96,112},{112,96},{1... | collective-permute-start | bytes 491528 | tf_op jit(solution)/shard_map/ppermute | solution.py:331
  27.4 7.0 %collective-permute-start.6 = (bf16[192,128]{1,0:T(8,128)(2,1)S(1)}, bf16[192,128]{1,0:T(8,128)(2,1)S(1)}, u32[]{:S(2)}, u32[]{:S(2)}) collective-permute-start(bf16[192,128]{1,0:T(8,128)(2,1)S(1)} %get-tuple-element.57), channel_id=1, source_target_pairs={{0,128},{16,144},{32,160},{48,176},{64,192},{80,208},{96,224},{112... | collective-permute-start | bytes 147464 | tf_op jit(solution)/shard_map/ppermute | solution.py:336
  33.0 1.5 %collective-permute-start.7 = (bf16[192,128]{1,0:T(8,128)(2,1)S(1)}, bf16[192,128]{1,0:T(8,128)(2,1)S(1)}, u32[]{:S(2)}, u32[]{:S(2)}) collective-permute-start(bf16[192,128]{1,0:T(8,128)(2,1)S(1)} %get-tuple-element.56), channel_id=1, source_target_pairs={{128,256},{144,272},{160,288},{176,304},{192,320},{208,336},{224,3... | collective-permute-start | bytes 147464 | tf_op jit(solution)/shard_map/ppermute | solution.py:337
  36.1 48.0 %all-to-all-start = ((bf16[32,32,192]{2,1,0:T(8,128)(2,1)}), bf16[32,32,192]{2,1,0:T(8,128)(2,1)S(1)}, u32[]{:S(2)}, u32[]{:S(2)}) async-start(bf16[32,32,192]{2,1,0:T(8,128)(2,1)} %bitcast.6), calls=%async_computation | async-start | bytes 1048576 | tf_op jit(solution)/shard_map/all_to_all | solution.py:344
  45.7 9.7 %collective-permute-start.10 = (bf16[64,1024]{1,0:T(8,128)(2,1)S(1)}, bf16[64,1024]{1,0:T(8,128)(2,1)S(1)}, u32[]{:S(2)}, u32[]{:S(2)}) collective-permute-start(bf16[64,1024]{1,0:T(8,128)(2,1)S(1)} %get-tuple-element.47), channel_id=1, source_target_pairs={{0,3},{1,2},{2,1},{3,0},{4,7},{5,6},{6,5},{7,4},{8,11},{9,10},{10,... | collective-permute-start | bytes 393224 | tf_op jit(solution)/shard_map/ppermute | solution.py:342
  50.3 6.4 %collective-permute-start.8 = (bf16[64,1024]{1,0:T(8,128)(2,1)S(1)}, bf16[64,1024]{1,0:T(8,128)(2,1)S(1)}, u32[]{:S(2)}, u32[]{:S(2)}) collective-permute-start(bf16[64,1024]{1,0:T(8,128)(2,1)S(1)} %get-tuple-element.45), channel_id=1, source_target_pairs={{0,1},{1,0},{2,3},{3,2},{4,5},{5,4},{6,7},{7,6},{8,9},{9,8},{10,11... | collective-permute-start | bytes 393224 | tf_op jit(solution)/shard_map/ppermute | solution.py:342
  52.2 7.8 %collective-permute-start.9 = (bf16[64,1024]{1,0:T(8,128)(2,1)S(1)}, bf16[64,1024]{1,0:T(8,128)(2,1)S(1)}, u32[]{:S(2)}, u32[]{:S(2)}) collective-permute-start(bf16[64,1024]{1,0:T(8,128)(2,1)S(1)} %get-tuple-element.46), channel_id=1, source_target_pairs={{0,2},{1,3},{2,0},{3,1},{4,6},{5,7},{6,4},{7,5},{8,10},{9,11},{10,... | collective-permute-start | bytes 393224 | tf_op jit(solution)/shard_map/ppermute | solution.py:342
  60.1 20.1 %collective-permute-start.11 = (bf16[16,1024]{1,0:T(8,128)(2,1)S(1)}, bf16[16,1024]{1,0:T(8,128)(2,1)S(1)}, u32[]{:S(2)}, u32[]{:S(2)}) collective-permute-start(bf16[16,1024]{1,0:T(8,128)(2,1)S(1)} %get-tuple-element.49), channel_id=1, source_target_pairs={{4,0},{5,1},{6,2},{7,3},{8,4},{9,5},{10,6},{11,7},{20,16},{21,17},... | collective-permute-start | bytes 98312 | tf_op jit(solution)/shard_map/ppermute | solution.py:348
  61.4 18.8 %collective-permute-start.12 = (bf16[16,1024]{1,0:T(8,128)(2,1)S(1)}, bf16[16,1024]{1,0:T(8,128)(2,1)S(1)}, u32[]{:S(2)}, u32[]{:S(2)}) collective-permute-start(bf16[16,1024]{1,0:T(8,128)(2,1)S(1)} %get-tuple-element.50), channel_id=1, source_target_pairs={{12,0},{13,1},{14,2},{15,3},{28,16},{29,17},{30,18},{31,19},{44,32... | collective-permute-start | bytes 98312 | tf_op jit(solution)/shard_map/ppermute | solution.py:349
  62.7 17.5 %collective-permute-start.13 = (bf16[16,1024]{1,0:T(8,128)(2,1)S(1)}, bf16[16,1024]{1,0:T(8,128)(2,1)S(1)}, u32[]{:S(2)}, u32[]{:S(2)}) collective-permute-start(bf16[16,1024]{1,0:T(8,128)(2,1)S(1)} %get-tuple-element.51), channel_id=1, source_target_pairs={{0,8},{1,9},{2,10},{3,11},{4,12},{5,13},{6,14},{7,15},{8,0},{9,1},... | collective-permute-start | bytes 98312 | tf_op jit(solution)/shard_map/ppermute | solution.py:350
  76.6 4.3 %collective-permute-start.14 = (bf16[16,1024]{1,0:T(8,128)(2,1)S(1)}, bf16[16,1024]{1,0:T(8,128)(2,1)S(1)}, u32[]{:S(2)}, u32[]{:S(2)}) collective-permute-start(bf16[16,1024]{1,0:T(8,128)(2,1)S(1)} %get-tuple-element.50), channel_id=1, source_target_pairs={{0,4},{1,5},{2,6},{3,7},{4,8},{5,9},{6,10},{7,11},{8,12},{9,13},{1... | collective-permute-start | bytes 98312 | tf_op jit(solution)/shard_map/ppermute | solution.py:351
  78.9 4.6 %collective-permute-start.15 = (bf16[16,1024]{1,0:T(8,128)(2,1)S(1)}, bf16[16,1024]{1,0:T(8,128)(2,1)S(1)}, u32[]{:S(2)}, u32[]{:S(2)}) collective-permute-start(bf16[16,1024]{1,0:T(8,128)(2,1)S(1)} %get-tuple-element.49), channel_id=1, source_target_pairs={{12,8},{13,9},{14,10},{15,11},{0,12},{1,13},{2,14},{3,15},{28,24},... | collective-permute-start | bytes 98312 | tf_op jit(solution)/shard_map/ppermute | solution.py:352

commit v7 on v6

--- a/solution.py
+++ b/solution.py
@@ -4,6 +4,7 @@
 from jax.experimental import pallas as pl
 from jax.experimental.pallas import tpu as pltpu
 from jax.sharding import PartitionSpec as P
+
 
 D = 1024
 HEADS = 16
@@ -37,6 +38,19 @@
     return lax.dot_general(
         left, right, (((left_axis,), (right_axis,)), ((), ())), preferred_element_type=jnp.float32
     )
+
+
+far_rounds = (
+    ((1, 0),),
+    ((1, 3), (2, 0), (3, 1)),
+    ((0, 2), (3, 0)),
+    ((0, 1), (1, 2)),
+    ((0, 3), (3, 2), (2, 1)),
+    ((2, 3),),
+)
+
+
+core_groups = [[2 * place + core for place in range(TILES // 2)] for core in range(2)]
 
 
 def usable(flags_ref, number, row_step, column_step):
@@ -104,47 +118,77 @@
     )(number, flags, tokens, w_qkv)
 
 
+def early_kernel(query_ref, mask_ref, centre_ref, lifted_ref, top_ref, total_ref):
+    keys = jnp.concatenate([centre_ref[...], mask_ref[1]], axis=1)
+    scores = contract(keys, query_ref[...], 1, 0)
+    top = jnp.max(scores, axis=0, keepdims=True)
+    lifted = jnp.exp(scores - top)
+    lifted_ref[...] = lifted
+    top_ref[...] = top
+    total_ref[...] = jnp.sum(lifted, axis=0, keepdims=True)
+
+
+def centre_scores(query, mask, centre):
+    vmem = pl.BlockSpec(memory_space=pltpu.VMEM)
+    return pl.pallas_call(
+        early_kernel,
+        in_specs=[vmem] * 3,
+        out_specs=[vmem] * 3,
+        out_shape=[
+            jax.ShapeDtypeStruct((COLUMN, OWN), jnp.float32),
+            jax.ShapeDtypeStruct((1, OWN), jnp.float32),
+            jax.ShapeDtypeStruct((1, OWN), jnp.float32),
+        ],
+        compiler_params=pltpu.CompilerParams(vmem_limit_bytes=8 << 20),
+        name="centre_scores",
+    )(query, mask, centre)
+
+
 def attend_kernel(
     query_ref, grad_ref, mask_ref, beyond_ref, centre_ref, twin_ref,
+    lifted_ref, top_ref, total_ref,
     dbeyond_ref, dtwin_ref, probs_ref, probs_low_ref, row_dot_ref, dquery_ref,
     scores_ref, low_ref,
 ):
-    pairs = (beyond_ref, centre_ref, twin_ref)
     query = query_ref[...]
     grad = jnp.concatenate([jnp.zeros((WIDTH, OWN), jnp.bfloat16), grad_ref[...]], axis=0)
-    highest = None
-    for block in range(3):
-        rows = pl.ds(block * COLUMN, COLUMN)
-        keys = jnp.concatenate([pairs[block][...], mask_ref[block]], axis=1)
+    sides = ((beyond_ref, 0, dbeyond_ref), (twin_ref, 2, dtwin_ref))
+    own_top = top_ref[...]
+    highest = own_top
+    for place, (pair_ref, block, _) in enumerate(sides):
+        rows = pl.ds(place * COLUMN, COLUMN)
+        keys = jnp.concatenate([pair_ref[...], mask_ref[block]], axis=1)
         scores = contract(keys, query, 1, 0)
         scores_ref[rows, :] = scores
-        top = jnp.max(scores, axis=0, keepdims=True)
-        highest = top if highest is None else jnp.maximum(highest, top)
-    total = jnp.zeros((1, OWN), jnp.float32)
-    for block in range(3):
-        rows = pl.ds(block * COLUMN, COLUMN)
+        highest = jnp.maximum(highest, jnp.max(scores, axis=0, keepdims=True))
+    own_scale = jnp.exp(own_top - highest)
+    total = total_ref[...] * own_scale
+    for place in range(2):
+        rows = pl.ds(place * COLUMN, COLUMN)
         lifted = jnp.exp(scores_ref[rows, :] - highest)
         scores_ref[rows, :] = lifted
         total = total + jnp.sum(lifted, axis=0, keepdims=True)
     inverse = 1.0 / total
-    attended = jnp.zeros((128, OWN), jnp.float32)
-    for block in range(3):
-        rows = pl.ds(block * COLUMN, COLUMN)
+    probs = lifted_ref[...] * (own_scale * inverse)
+    low = probs.astype(jnp.bfloat16)
+    probs_ref[...] = probs
+    probs_low_ref[...] = low
+    attended = contract(centre_ref[...], low, 0, 0)
+    for place, (pair_ref, _, _) in enumerate(sides):
+        rows = pl.ds(place * COLUMN, COLUMN)
         probs = scores_ref[rows, :] * inverse
         scores_ref[rows, :] = probs
         low = probs.astype(jnp.bfloat16)
         low_ref[rows, :] = low
-        attended = attended + contract(pairs[block][...], low, 0, 0)
+        attended = attended + contract(pair_ref[...], low, 0, 0)
     row_dot = jnp.sum(attended * grad.astype(jnp.float32), axis=0, keepdims=True)
     dquery = jnp.zeros((128, OWN), jnp.float32)
-    for block, out_ref in ((0, dbeyond_ref), (2, dtwin_ref)):
-        rows = pl.ds(block * COLUMN, COLUMN)
+    for place, (pair_ref, _, out_ref) in enumerate(sides):
+        rows = pl.ds(place * COLUMN, COLUMN)
         dpair, dquery = block_backward(
-            pairs[block][...], query, grad, scores_ref[rows, :], low_ref[rows, :], row_dot, dquery
+            pair_ref[...], query, grad, scores_ref[rows, :], low_ref[rows, :], row_dot, dquery
         )
         out_ref[...] = dpair.astype(jnp.bfloat16)
-    probs_ref[...] = scores_ref[COLUMN : 2 * COLUMN, :]
-    probs_low_ref[...] = low_ref[COLUMN : 2 * COLUMN, :]
     row_dot_ref[...] = row_dot
     dquery_ref[...] = dquery
 
@@ -156,11 +200,11 @@
     return dpair, dquery + contract(pair, grad_scores, 0, 0)
 
 
-def attend(query, grad_turned, mask, beyond, centre, twin):
+def attend(query, grad_turned, mask, beyond, centre, twin, early):
     vmem = pl.BlockSpec(memory_space=pltpu.VMEM)
     return pl.pallas_call(
         attend_kernel,
-        in_specs=[vmem] * 6,
+        in_specs=[vmem] * 9,
         out_specs=[vmem] * 6,
         out_shape=[
             jax.ShapeDtypeStruct((COLUMN, 128), jnp.bfloat16),
@@ -171,12 +215,12 @@
             jax.ShapeDtypeStruct((128, OWN), jnp.float32),
         ],
         scratch_shapes=[
-            pltpu.VMEM((3 * COLUMN, OWN), jnp.float32),
-            pltpu.VMEM((3 * COLUMN, OWN), jnp.bfloat16),
+            pltpu.VMEM((2 * COLUMN, OWN), jnp.float32),
+            pltpu.VMEM((2 * COLUMN, OWN), jnp.bfloat16),
         ],
         compiler_params=pltpu.CompilerParams(vmem_limit_bytes=16 << 20),
         name="attend",
-    )(query, grad_turned, mask, beyond, centre, twin)
+    )(query, grad_turned, mask, beyond, centre, twin, *early)
 
 
 def finish_kernel(
@@ -245,37 +289,44 @@
     )(near, odd, column, from_fold, from_middle, dquery, w_qkv)
 
 
-def weight_kernel(turned_ref, dqkv_ref, out_ref):
-    out_ref[...] = contract(turned_ref[...], dqkv_ref[...], 1, 0).astype(jnp.bfloat16)
-
-
-def weight_term(turned, dqkv):
+def weight_kernel(turned_ref, lent_ref, dqkv_ref, twin_ref, out_ref):
+    term = contract(turned_ref[...], dqkv_ref[...], 1, 0)
+    out_ref[...] = (term + contract(lent_ref[...], twin_ref[...], 1, 0)).astype(jnp.bfloat16)
+
+
+def weight_term(turned, lent, dqkv, twin):
     vmem = pl.BlockSpec(memory_space=pltpu.VMEM)
     return pl.pallas_call(
         weight_kernel,
-        in_specs=[vmem] * 2,
+        in_specs=[vmem] * 4,
         out_specs=vmem,
-        out_shape=jax.ShapeDtypeStruct((D, 3 * WIDTH), jnp.bfloat16),
+        out_shape=jax.ShapeDtypeStruct((D // 2, 3 * WIDTH), jnp.bfloat16),
         compiler_params=pltpu.CompilerParams(vmem_limit_bytes=8 << 20),
         name="weight_term",
-    )(turned, dqkv)
+    )(turned, lent, dqkv, twin)
 
 
 def near_kernel(high_ref, *refs):
     parts, outs, sum_ref = refs[:NEAR], refs[NEAR:-1], refs[-1]
     total = sum(part[...].astype(jnp.float32) for part in parts)
     sum_ref[...] = total.astype(jnp.bfloat16).reshape(HIGH, S, D)
-    for step, out_ref in zip((0, -1, 1, 2), outs):
-        out_ref[...] = sum_ref[(high_ref[0] + step) & (HIGH - 1)]
+    high = high_ref[0]
+    outs[0][...] = sum_ref[high]
+    for moves, out_ref in zip(far_rounds, outs[1:]):
+        target = 0
+        for source, sent in moves:
+            target = jnp.where(high == source, sent, target)
+        out_ref[...] = sum_ref[target]
 
 
 def near_total(high, parts):
     vmem = pl.BlockSpec(memory_space=pltpu.VMEM)
+    outs = 1 + len(far_rounds)
     return pl.pallas_call(
         near_kernel,
         in_specs=[pl.BlockSpec(memory_space=pltpu.SMEM)] + [vmem] * NEAR,
-        out_specs=[vmem] * HIGH,
-        out_shape=[jax.ShapeDtypeStruct((S, D), jnp.bfloat16)] * HIGH,
+        out_specs=[vmem] * outs,
+        out_shape=[jax.ShapeDtypeStruct((S, D), jnp.bfloat16)] * outs,
         scratch_shapes=[pltpu.VMEM((HIGH, S, D), jnp.bfloat16)],
         compiler_params=pltpu.CompilerParams(vmem_limit_bytes=8 << 20),
         name="near_total",
@@ -320,13 +371,19 @@
     fold, middle, query, mask = lax.optimization_barrier((fold, middle, query, mask))
     above = jnp.where(odd == 1, fold, middle)
     below = jnp.where(odd == 1, middle, fold)
-    turned = jnp.transpose(tokens)
+    core = number & 1
+    turned = jnp.transpose(tokens).reshape(TILES // 2, 2, D // TILES, OWN)
+    kept_rows = lax.dynamic_index_in_dim(turned, core, 1, False).reshape(D // 2, OWN)
+    lent_rows = lax.dynamic_index_in_dim(turned, 1 - core, 1, False).reshape(D // 2, OWN)
     centre = jnp.concatenate([above, pair, below], axis=0)
     beyond = lax.ppermute(centre, "tile", next_pairs)
     twin = lax.ppermute(centre, "tile", twin_pairs)
-    beyond, twin, turned = lax.optimization_barrier((beyond, twin, turned))
+    early = centre_scores(query, mask, centre)
+    beyond, twin, kept_rows, lent_rows = lax.optimization_barrier(
+        (beyond, twin, kept_rows, lent_rows)
+    )
     grad_turned = jnp.transpose(grad_out)
-    dbeyond, dtwin, *saved = attend(query, grad_turned, mask, beyond, centre, twin)
+    dbeyond, dtwin, *saved = attend(query, grad_turned, mask, beyond, centre, twin, early)
     from_beyond = lax.ppermute(dbeyond, "tile", next_pairs)
     from_twin = lax.ppermute(dtwin, "tile", twin_pairs)
     dquery, dcentre = finish(query, grad_turned, centre, *saved)
@@ -335,22 +392,21 @@
     lower = column[OWN + RIM :].astype(jnp.bfloat16)
     from_fold = lax.ppermute(jnp.where(odd == 1, upper, lower), "tile", fold_pairs)
     from_middle = lax.ppermute(jnp.where(odd == 1, lower, upper), "tile", middle_pairs)
+    lent_rows = lax.ppermute(lent_rows, "tile", twin_pairs)
     dqkv, *parts = project_back(
         near.reshape(1), odd.reshape(1), column, from_fold, from_middle, dquery, w_qkv
     )
+    twin_dqkv = lax.ppermute(dqkv, "tile", twin_pairs)
     for step in (2, 1, 3):
         parts[step] = lax.ppermute(parts[step], "head", near_swap(step))
-    term = weight_term(turned, dqkv)
-    terms = lax.all_to_all(term.reshape(TILES, D // TILES, -1), "tile", 0, 0)
-    kept, before, after, across = near_total(high.reshape(1), parts)
-    chunks = [
-        kept,
-        lax.ppermute(before, "head", far_moves((1, 0), (2, 1))),
-        lax.ppermute(after, "head", far_moves((3, 0))),
-        lax.ppermute(across, "head", far_moves((0, 2), (1, 3), (2, 0), (3, 1))),
-        lax.ppermute(after, "head", far_moves((0, 1), (1, 2), (2, 3))),
-        lax.ppermute(before, "head", far_moves((3, 2), (0, 3))),
-    ]
+    term = weight_term(kept_rows, lent_rows, dqkv, twin_dqkv)
+    terms = lax.all_to_all(
+        term.reshape(TILES // 2, D // TILES, -1),
+        "tile", 0, 0, axis_index_groups=core_groups,
+    )
+    chunks = list(near_total(high.reshape(1), parts))
+    for place, moves in enumerate(far_rounds):
+        chunks[1 + place] = lax.ppermute(chunks[1 + place], "head", far_moves(*moves))
     grad_w = tile_total(terms)
     grad_x = sum(chunk.astype(jnp.float32) for chunk in chunks).astype(jnp.bfloat16)
     return (grad_x, grad_w)

time: 85.5 us -> 87.8 us (1.027)
  the two profiles are of different devices: /device:TPU:1 before, /device:TPU:10 now
where the time goes in v7:
time: 87.8 us; the launch traced here: 87.1 us
  starting transfers between devices  65.9 us (75%)
  waiting for transfers between devices  10.9 us (12%)
  Pallas kernels  6.74 us (8%)
  matrix products  1.49 us (2%)
  between operations  1.04 us (1%)
    ppermute x6, starting transfers between devices, local_step(): lax.ppermute(chunks[1 + place], 'head', far_moves(*moves))  20.6 us
    ppermute x3, starting transfers between devices, local_step(): parts[step] = lax.ppermute(parts[step], 'head', near_swap(step))  9.2 us
    all_to_all x1, starting transfers between devices, local_step(): lax.all_to_all(term.reshape(TILES // 2, D // TILES, -1), 'tile', 0, 0, ax...  9.09 us
    ppermute x1, starting transfers between devices, local_step(): lax.ppermute(jnp.where(odd == 1, upper, lower), 'tile', fold_pairs)  7.17 us
    ppermute x3, waiting for transfers between devices, local_step(): parts[step] = lax.ppermute(parts[step], 'head', near_swap(step))  6.42 us
    ppermute x1, starting transfers between devices, local_step(): fold = lax.ppermute(fold, 'tile', fold_pairs)  3.83 us
    ppermute x1, starting transfers between devices, local_step(): twin = lax.ppermute(centre, 'tile', twin_pairs)  3.5 us
    ppermute x1, starting transfers between devices, local_step(): from_twin = lax.ppermute(dtwin, 'tile', twin_pairs)  3.2 us
  transfers between devices with their start and end apart: 20, of which 6 were waited for; matrix products, arithmetic and copies ran while one was open for 1% of the time, Pallas kernels for 4%

profile of v7, /device:TPU:10, one launch (start us, length us, event | category | flops | bytes accessed | tf_op | source)
XLA Modules:
  0.0 87.1 jit_solution(18047634188848631210)
XLA Ops:
  0.7 1.5 %convolution_convert_fusion = bf16[256,128]{1,0:T(8,128)(2,1)S(1)} fusion(bf16[256,1024]{1,0:T(8,128)(2,1)} %tokens_ref.1, bf16[192,1024]{1,0:T(8,128)(2,1)} %w_ref.3), kind=kOutput, calls=%fused_computation | convolution fusion | flops 67141632 | bytes 851968 | tf_op jit(solution)/shard_map/dot_general | solution.py:38
  2.2 3.8 %collective-permute-start = (bf16[192,128]{1,0:T(8,128)(2,1)S(1)}, bf16[192,128]{1,0:T(8,128)(2,1)S(1)}, u32[]{:S(2)}, u32[]{:S(2)}) collective-permute-start(bf16[192,128]{1,0:T(8,128)(2,1)S(1)} %get-tuple-element.77), channel_id=1, source_target_pairs={{0,128},{16,144},{32,160},{48,176},{64,192},{80,208},{96,224},{112... | collective-permute-start | bytes 147464 | tf_op jit(solution)/shard_map/ppermute | solution.py:368
  6.7 1.8 %prepare.1 = (bf16[256,256]{1,0:T(8,128)(2,1)S(1)}, bf16[3,640,128]{2,1,0:T(8,128)(2,1)S(1)}) custom-call(s32[1]{0:T(128)} %bitcast.3.number_ref, s32[1,8]{1,0:T(1,128)S(1)} %copy-done.3, bf16[256,1024]{1,0:T(8,128)(2,1)S(1)} %copy-done, bf16[192,1024]{1,0:T(8,128)(2,1)S(1)} %copy-done.1), custom_call_target="tpu_custom_call" | custom-call | tf_op jit(solution)/shard_map/prepare/pallas_call | solution.py:102
  8.6 1.9 %collective-permute-start.2 = (bf16[640,128]{1,0:T(8,128)(2,1)S(1)}, bf16[640,128]{1,0:T(8,128)(2,1)S(1)}, u32[]{:S(2)}, u32[]{:S(2)}) collective-permute-start(bf16[640,128]{1,0:T(8,128)(2,1)S(1)} %pad_maximum_fusion.centre_ref), channel_id=1, source_target_pairs={{16,32},{32,16},{48,64},{64,48},{80,96},{96,80},{144,160},{160,144... | collective-permute-start | bytes 491528 | tf_op jit(solution)/shard_map/ppermute | solution.py:379
  10.5 3.5 %collective-permute-start.3 = (bf16[640,128]{1,0:T(8,128)(2,1)S(1)}, bf16[640,128]{1,0:T(8,128)(2,1)S(1)}, u32[]{:S(2)}, u32[]{:S(2)}) collective-permute-start(bf16[640,128]{1,0:T(8,128)(2,1)S(1)} %pad_maximum_fusion.centre_ref), channel_id=1, source_target_pairs={{0,16},{16,0},{32,48},{48,32},{64,80},{80,64},{96,112},{112,96},{1... | collective-permute-start | bytes 491528 | tf_op jit(solution)/shard_map/ppermute | solution.py:380
  15.3 1.8 %attend.1 = (bf16[640,128]{1,0:T(8,128)(2,1)S(1)}, bf16[640,128]{1,0:T(8,128)(2,1)S(1)}, f32[640,256]{1,0:T(8,128)S(1)}, bf16[640,256]{1,0:T(8,128)(2,1)S(1)}, f...) custom-call(bf16[256,256]{1,0:T(8,128)(2,1)S(1)} %get-tuple-element.37.query_ref, bf16[64,256]{1,0:T(8,128)(2,1)S(1)} %bitcast.13, ...), custom_call_target="tpu_custom_call" | custom-call | tf_op jit(solution)/shard_map/attend/pallas_call | solution.py:205
  17.0 2.2 %collective-permute-start.4 = (bf16[640,128]{1,0:T(8,128)(2,1)S(1)}, bf16[640,128]{1,0:T(8,128)(2,1)S(1)}, u32[]{:S(2)}, u32[]{:S(2)}) collective-permute-start(bf16[640,128]{1,0:T(8,128)(2,1)S(1)} %get-tuple-element.51), channel_id=1, source_target_pairs={{16,32},{32,16},{48,64},{64,48},{80,96},{96,80},{144,160},{160,144... | collective-permute-start | bytes 491528 | tf_op jit(solution)/shard_map/ppermute | solution.py:387
  19.2 3.2 %collective-permute-start.5 = (bf16[640,128]{1,0:T(8,128)(2,1)S(1)}, bf16[640,128]{1,0:T(8,128)(2,1)S(1)}, u32[]{:S(2)}, u32[]{:S(2)}) collective-permute-start(bf16[640,128]{1,0:T(8,128)(2,1)S(1)} %get-tuple-element.52), channel_id=1, source_target_pairs={{0,16},{16,0},{32,48},{48,32},{64,80},{80,64},{96,112},{112,96},{1... | collective-permute-start | bytes 491528 | tf_op jit(solution)/shard_map/ppermute | solution.py:388
  22.4 1.9 %collective-permute-start.17 = (bf16[512,256]{1,0:T(8,128)(2,1)S(1)}, bf16[512,256]{1,0:T(8,128)(2,1)S(1)}, u32[]{:S(2)}, u32[]{:S(2)}) collective-permute-start(bf16[512,256]{1,0:T(8,128)(2,1)S(1)} %bitcast.16), channel_id=1, source_target_pairs={{0,16},{16,0},{32,48},{48,32},{64,80},{80,64},{96,112},{112,96},{1... | collective-permute-start | bytes 786440 | tf_op jit(solution)/shard_map/ppermute | solution.py:395
  25.0 7.2 %collective-permute-start.6 = (bf16[192,128]{1,0:T(8,128)(2,1)S(1)}, bf16[192,128]{1,0:T(8,128)(2,1)S(1)}, u32[]{:S(2)}, u32[]{:S(2)}) collective-permute-start(bf16[192,128]{1,0:T(8,128)(2,1)S(1)} %get-tuple-element.73), channel_id=1, source_target_pairs={{0,128},{16,144},{32,160},{48,176},{64,192},{80,208},{96,224},{112... | collective-permute-start | bytes 147464 | tf_op jit(solution)/shard_map/ppermute | solution.py:393
  32.9 1.7 %collective-permute-done.6.fold_ref = bf16[192,128]{1,0:T(8,128)(2,1)S(1)} collective-permute-done((bf16[192,128]{1,0:T(8,128)(2,1)S(1)}, bf16[192,128]{1,0:T(8,128)(2,1)S(1)}, u32[]{:S(2)}, u32[]{:S(2)}) %collective-permute-start.6) | collective-permute-done | bytes 49184 | tf_op jit(solution)/shard_map/ppermute | solution.py:393
  35.1 1.9 %collective-permute-start.18 = (bf16[256,192]{1,0:T(8,128)(2,1)S(1)}, bf16[256,192]{1,0:T(8,128)(2,1)S(1)}, u32[]{:S(2)}, u32[]{:S(2)}) collective-permute-start(bf16[256,192]{1,0:T(8,128)(2,1)S(1)} %get-tuple-element.67.dqkv_ref), channel_id=1, source_target_pairs={{0,16},{16,0},{32,48},{48,32},{64,80},{80,64},{96,112},{112,96},{1... | collective-permute-start | bytes 294920 | tf_op jit(solution)/shard_map/ppermute | solution.py:399
  37.0 1.3 %collective-permute-done.18.twin_ref = bf16[256,192]{1,0:T(8,128)(2,1)S(1)} collective-permute-done((bf16[256,192]{1,0:T(8,128)(2,1)S(1)}, bf16[256,192]{1,0:T(8,128)(2,1)S(1)}, u32[]{:S(2)}, u32[]{:S(2)}) %collective-permute-start.18) | collective-permute-done | bytes 98336 | tf_op jit(solution)/shard_map/ppermute | solution.py:399
  39.3 9.1 %all-to-all-start = ((bf16[16,32,192]{2,1,0:T(8,128)(2,1)}), bf16[16,32,192]{2,1,0:T(8,128)(2,1)S(1)}, u32[]{:S(2)}, u32[]{:S(2)}) async-start(bf16[16,32,192]{2,1,0:T(8,128)(2,1)} %bitcast.10), calls=%async_computation | async-start | bytes 524288 | tf_op jit(solution)/shard_map/all_to_all | solution.py:403
  48.4 3.5 %collective-permute-start.10 = (bf16[64,1024]{1,0:T(8,128)(2,1)S(1)}, bf16[64,1024]{1,0:T(8,128)(2,1)S(1)}, u32[]{:S(2)}, u32[]{:S(2)}) collective-permute-start(bf16[64,1024]{1,0:T(8,128)(2,1)S(1)} %get-tuple-element.57), channel_id=1, source_target_pairs={{0,3},{1,2},{2,1},{3,0},{4,7},{5,6},{6,5},{7,4},{8,11},{9,10},{10,... | collective-permute-start | bytes 393224 | tf_op jit(solution)/shard_map/ppermute | solution.py:401
  51.9 3.8 %collective-permute-start.8 = (bf16[64,1024]{1,0:T(8,128)(2,1)S(1)}, bf16[64,1024]{1,0:T(8,128)(2,1)S(1)}, u32[]{:S(2)}, u32[]{:S(2)}) collective-permute-start(bf16[64,1024]{1,0:T(8,128)(2,1)S(1)} %get-tuple-element.55), channel_id=1, source_target_pairs={{0,1},{1,0},{2,3},{3,2},{4,5},{5,4},{6,7},{7,6},{8,9},{9,8},{10,11... | collective-permute-start | bytes 393224 | tf_op jit(solution)/shard_map/ppermute | solution.py:401
  55.7 1.9 %collective-permute-start.9 = (bf16[64,1024]{1,0:T(8,128)(2,1)S(1)}, bf16[64,1024]{1,0:T(8,128)(2,1)S(1)}, u32[]{:S(2)}, u32[]{:S(2)}) collective-permute-start(bf16[64,1024]{1,0:T(8,128)(2,1)S(1)} %get-tuple-element.56), channel_id=1, source_target_pairs={{0,2},{1,3},{2,0},{3,1},{4,6},{5,7},{6,4},{7,5},{8,10},{9,11},{10,... | collective-permute-start | bytes 393224 | tf_op jit(solution)/shard_map/ppermute | solution.py:401
  57.7 1.7 %collective-permute-done.8.refs_1_ = bf16[64,1024]{1,0:T(8,128)(2,1)S(1)} collective-permute-done((bf16[64,1024]{1,0:T(8,128)(2,1)S(1)}, bf16[64,1024]{1,0:T(8,128)(2,1)S(1)}, u32[]{:S(2)}, u32[]{:S(2)}) %collective-permute-start.8) | collective-permute-done | bytes 131104 | tf_op jit(solution)/shard_map/ppermute | solution.py:401
  59.3 4.8 %collective-permute-done.9.refs_2_ = bf16[64,1024]{1,0:T(8,128)(2,1)S(1)} collective-permute-done((bf16[64,1024]{1,0:T(8,128)(2,1)S(1)}, bf16[64,1024]{1,0:T(8,128)(2,1)S(1)}, u32[]{:S(2)}, u32[]{:S(2)}) %collective-permute-start.9) | collective-permute-done | bytes 131104 | tf_op jit(solution)/shard_map/ppermute | solution.py:401
  64.2 1.3 %collective-permute-start.11 = (bf16[16,1024]{1,0:T(8,128)(2,1)S(1)}, bf16[16,1024]{1,0:T(8,128)(2,1)S(1)}, u32[]{:S(2)}, u32[]{:S(2)}) collective-permute-start(bf16[16,1024]{1,0:T(8,128)(2,1)S(1)} %get-tuple-element.59), channel_id=1, source_target_pairs={{4,0},{5,1},{6,2},{7,3},{20,16},{21,17},{22,18},{23,19},{36,32},{3... | collective-permute-start | bytes 98312 | tf_op jit(solution)/shard_map/ppermute | solution.py:409
  65.5 1.3 %collective-permute-start.12 = (bf16[16,1024]{1,0:T(8,128)(2,1)S(1)}, bf16[16,1024]{1,0:T(8,128)(2,1)S(1)}, u32[]{:S(2)}, u32[]{:S(2)}) collective-permute-start(bf16[16,1024]{1,0:T(8,128)(2,1)S(1)} %get-tuple-element.60), channel_id=1, source_target_pairs={{4,12},{5,13},{6,14},{7,15},{8,0},{9,1},{10,2},{11,3},{12,4},{13,5... | collective-permute-start | bytes 98312 | tf_op jit(solution)/shard_map/ppermute | solution.py:409
  66.8 13.3 %collective-permute-start.13 = (bf16[16,1024]{1,0:T(8,128)(2,1)S(1)}, bf16[16,1024]{1,0:T(8,128)(2,1)S(1)}, u32[]{:S(2)}, u32[]{:S(2)}) collective-permute-start(bf16[16,1024]{1,0:T(8,128)(2,1)S(1)} %get-tuple-element.61), channel_id=1, source_target_pairs={{0,8},{1,9},{2,10},{3,11},{12,0},{13,1},{14,2},{15,3},{16,24},{17,... | collective-permute-start | bytes 98312 | tf_op jit(solution)/shard_map/ppermute | solution.py:409
  80.1 2.8 %collective-permute-start.14 = (bf16[16,1024]{1,0:T(8,128)(2,1)S(1)}, bf16[16,1024]{1,0:T(8,128)(2,1)S(1)}, u32[]{:S(2)}, u32[]{:S(2)}) collective-permute-start(bf16[16,1024]{1,0:T(8,128)(2,1)S(1)} %get-tuple-element.62), channel_id=1, source_target_pairs={{0,4},{1,5},{2,6},{3,7},{4,8},{5,9},{6,10},{7,11},{16,20},{17,21},... | collective-permute-start | bytes 98312 | tf_op jit(solution)/shard_map/ppermute | solution.py:409
  82.9 1.3 %collective-permute-start.15 = (bf16[16,1024]{1,0:T(8,128)(2,1)S(1)}, bf16[16,1024]{1,0:T(8,128)(2,1)S(1)}, u32[]{:S(2)}, u32[]{:S(2)}) collective-permute-start(bf16[16,1024]{1,0:T(8,128)(2,1)S(1)} %get-tuple-element.63), channel_id=1, source_target_pairs={{0,12},{1,13},{2,14},{3,15},{12,8},{13,9},{14,10},{15,11},{8,4},{9... | collective-permute-start | bytes 98312 | tf_op jit(solution)/shard_map/ppermute | solution.py:409
  (41 shorter events, 7.6 us)
Async XLA Ops:
  0.6 6.1 %copy-start = (bf16[256,1024]{1,0:T(8,128)(2,1)S(1)}, bf16[256,1024]{1,0:T(8,128)(2,1)}, u32[]{:S(2)}) copy-start(bf16[256,1024]{1,0:T(8,128)(2,1)} %tokens_ref.1) | copy-start | bytes 1572868
  0.7 6.1 %copy-start.1 = (bf16[192,1024]{1,0:T(8,128)(2,1)S(1)}, bf16[192,1024]{1,0:T(8,128)(2,1)}, u32[]{:S(2)}) copy-start(bf16[192,1024]{1,0:T(8,128)(2,1)} %w_ref.3) | copy-start | bytes 1179652
  2.2 6.4 %collective-permute-start = (bf16[192,128]{1,0:T(8,128)(2,1)S(1)}, bf16[192,128]{1,0:T(8,128)(2,1)S(1)}, u32[]{:S(2)}, u32[]{:S(2)}) collective-permute-start(bf16[192,128]{1,0:T(8,128)(2,1)S(1)} %get-tuple-element.77), channel_id=1, source_target_pairs={{0,128},{16,144},{32,160},{48,176},{64,192},{80,208},{96,224},{112... | collective-permute-start | bytes 147464 | tf_op jit(solution)/shard_map/ppermute | solution.py:368
  6.0 0.7 copy-start.3
  6.0 2.5 %collective-permute-start.1 = (bf16[192,128]{1,0:T(8,128)(2,1)S(1)}, bf16[192,128]{1,0:T(8,128)(2,1)S(1)}, u32[]{:S(2)}, u32[]{:S(2)}) collective-permute-start(bf16[192,128]{1,0:T(8,128)(2,1)S(1)} %get-tuple-element.76), channel_id=1, source_target_pairs={{128,256},{144,272},{160,288},{176,304},{192,320},{208,336},{224,3... | collective-permute-start | bytes 147464 | tf_op jit(solution)/shard_map/ppermute | solution.py:369
  8.6 6.6 %collective-permute-start.2 = (bf16[640,128]{1,0:T(8,128)(2,1)S(1)}, bf16[640,128]{1,0:T(8,128)(2,1)S(1)}, u32[]{:S(2)}, u32[]{:S(2)}) collective-permute-start(bf16[640,128]{1,0:T(8,128)(2,1)S(1)} %pad_maximum_fusion.centre_ref), channel_id=1, source_target_pairs={{16,32},{32,16},{48,64},{64,48},{80,96},{96,80},{144,160},{160,144... | collective-permute-start | bytes 491528 | tf_op jit(solution)/shard_map/ppermute | solution.py:379
  10.5 4.7 %collective-permute-start.3 = (bf16[640,128]{1,0:T(8,128)(2,1)S(1)}, bf16[640,128]{1,0:T(8,128)(2,1)S(1)}, u32[]{:S(2)}, u32[]{:S(2)}) collective-permute-start(bf16[640,128]{1,0:T(8,128)(2,1)S(1)} %pad_maximum_fusion.centre_ref), channel_id=1, source_target_pairs={{0,16},{16,0},{32,48},{48,32},{64,80},{80,64},{96,112},{112,96},{1... | collective-permute-start | bytes 491528 | tf_op jit(solution)/shard_map/ppermute | solution.py:380
  14.3 0.9 %copy-start.2 = (bf16[256,64]{0,1:T(8,128)(2,1)S(1)}, bf16[256,64]{0,1:T(8,128)(2,1)}, u32[]{:S(2)}) copy-start(bf16[256,64]{0,1:T(8,128)(2,1)} %param.6) | copy-start | bytes 98308
  17.0 7.9 %collective-permute-start.4 = (bf16[640,128]{1,0:T(8,128)(2,1)S(1)}, bf16[640,128]{1,0:T(8,128)(2,1)S(1)}, u32[]{:S(2)}, u32[]{:S(2)}) collective-permute-start(bf16[640,128]{1,0:T(8,128)(2,1)S(1)} %get-tuple-element.51), channel_id=1, source_target_pairs={{16,32},{32,16},{48,64},{64,48},{80,96},{96,80},{144,160},{160,144... | collective-permute-start | bytes 491528 | tf_op jit(solution)/shard_map/ppermute | solution.py:387
  19.2 5.7 %collective-permute-start.5 = (bf16[640,128]{1,0:T(8,128)(2,1)S(1)}, bf16[640,128]{1,0:T(8,128)(2,1)S(1)}, u32[]{:S(2)}, u32[]{:S(2)}) collective-permute-start(bf16[640,128]{1,0:T(8,128)(2,1)S(1)} %get-tuple-element.52), channel_id=1, source_target_pairs={{0,16},{16,0},{32,48},{48,32},{64,80},{80,64},{96,112},{112,96},{1... | collective-permute-start | bytes 491528 | tf_op jit(solution)/shard_map/ppermute | solution.py:388
  22.4 14.6 %collective-permute-start.17 = (bf16[512,256]{1,0:T(8,128)(2,1)S(1)}, bf16[512,256]{1,0:T(8,128)(2,1)S(1)}, u32[]{:S(2)}, u32[]{:S(2)}) collective-permute-start(bf16[512,256]{1,0:T(8,128)(2,1)S(1)} %bitcast.16), channel_id=1, source_target_pairs={{0,16},{16,0},{32,48},{48,32},{64,80},{80,64},{96,112},{112,96},{1... | collective-permute-start | bytes 786440 | tf_op jit(solution)/shard_map/ppermute | solution.py:395
  25.0 9.6 %collective-permute-start.6 = (bf16[192,128]{1,0:T(8,128)(2,1)S(1)}, bf16[192,128]{1,0:T(8,128)(2,1)S(1)}, u32[]{:S(2)}, u32[]{:S(2)}) collective-permute-start(bf16[192,128]{1,0:T(8,128)(2,1)S(1)} %get-tuple-element.73), channel_id=1, source_target_pairs={{0,128},{16,144},{32,160},{48,176},{64,192},{80,208},{96,224},{112... | collective-permute-start | bytes 147464 | tf_op jit(solution)/shard_map/ppermute | solution.py:393
  32.2 2.4 %collective-permute-start.7 = (bf16[192,128]{1,0:T(8,128)(2,1)S(1)}, bf16[192,128]{1,0:T(8,128)(2,1)S(1)}, u32[]{:S(2)}, u32[]{:S(2)}) collective-permute-start(bf16[192,128]{1,0:T(8,128)(2,1)S(1)} %get-tuple-element.72), channel_id=1, source_target_pairs={{128,256},{144,272},{160,288},{176,304},{192,320},{208,336},{224,3... | collective-permute-start | bytes 147464 | tf_op jit(solution)/shard_map/ppermute | solution.py:394
  35.1 3.2 %collective-permute-start.18 = (bf16[256,192]{1,0:T(8,128)(2,1)S(1)}, bf16[256,192]{1,0:T(8,128)(2,1)S(1)}, u32[]{:S(2)}, u32[]{:S(2)}) collective-permute-start(bf16[256,192]{1,0:T(8,128)(2,1)S(1)} %get-tuple-element.67.dqkv_ref), channel_id=1, source_target_pairs={{0,16},{16,0},{32,48},{48,32},{64,80},{80,64},{96,112},{112,96},{1... | collective-permute-start | bytes 294920 | tf_op jit(solution)/shard_map/ppermute | solution.py:399
  39.3 47.1 %all-to-all-start = ((bf16[16,32,192]{2,1,0:T(8,128)(2,1)}), bf16[16,32,192]{2,1,0:T(8,128)(2,1)S(1)}, u32[]{:S(2)}, u32[]{:S(2)}) async-start(bf16[16,32,192]{2,1,0:T(8,128)(2,1)} %bitcast.10), calls=%async_computation | async-start | bytes 524288 | tf_op jit(solution)/shard_map/all_to_all | solution.py:403
  48.4 9.2 %collective-permute-start.10 = (bf16[64,1024]{1,0:T(8,128)(2,1)S(1)}, bf16[64,1024]{1,0:T(8,128)(2,1)S(1)}, u32[]{:S(2)}, u32[]{:S(2)}) collective-permute-start(bf16[64,1024]{1,0:T(8,128)(2,1)S(1)} %get-tuple-element.57), channel_id=1, source_target_pairs={{0,3},{1,2},{2,1},{3,0},{4,7},{5,6},{6,5},{7,4},{8,11},{9,10},{10,... | collective-permute-start | bytes 393224 | tf_op jit(solution)/shard_map/ppermute | solution.py:401
  51.9 7.4 %collective-permute-start.8 = (bf16[64,1024]{1,0:T(8,128)(2,1)S(1)}, bf16[64,1024]{1,0:T(8,128)(2,1)S(1)}, u32[]{:S(2)}, u32[]{:S(2)}) collective-permute-start(bf16[64,1024]{1,0:T(8,128)(2,1)S(1)} %get-tuple-element.55), channel_id=1, source_target_pairs={{0,1},{1,0},{2,3},{3,2},{4,5},{5,4},{6,7},{7,6},{8,9},{9,8},{10,11... | collective-permute-start | bytes 393224 | tf_op jit(solution)/shard_map/ppermute | solution.py:401
  55.7 8.4 %collective-permute-start.9 = (bf16[64,1024]{1,0:T(8,128)(2,1)S(1)}, bf16[64,1024]{1,0:T(8,128)(2,1)S(1)}, u32[]{:S(2)}, u32[]{:S(2)}) collective-permute-start(bf16[64,1024]{1,0:T(8,128)(2,1)S(1)} %get-tuple-element.56), channel_id=1, source_target_pairs={{0,2},{1,3},{2,0},{3,1},{4,6},{5,7},{6,4},{7,5},{8,10},{9,11},{10,... | collective-permute-start | bytes 393224 | tf_op jit(solution)/shard_map/ppermute | solution.py:401
  64.2 20.0 %collective-permute-start.11 = (bf16[16,1024]{1,0:T(8,128)(2,1)S(1)}, bf16[16,1024]{1,0:T(8,128)(2,1)S(1)}, u32[]{:S(2)}, u32[]{:S(2)}) collective-permute-start(bf16[16,1024]{1,0:T(8,128)(2,1)S(1)} %get-tuple-element.59), channel_id=1, source_target_pairs={{4,0},{5,1},{6,2},{7,3},{20,16},{21,17},{22,18},{23,19},{36,32},{3... | collective-permute-start | bytes 98312 | tf_op jit(solution)/shard_map/ppermute | solution.py:409
  65.5 19.4 %collective-permute-start.12 = (bf16[16,1024]{1,0:T(8,128)(2,1)S(1)}, bf16[16,1024]{1,0:T(8,128)(2,1)S(1)}, u32[]{:S(2)}, u32[]{:S(2)}) collective-permute-start(bf16[16,1024]{1,0:T(8,128)(2,1)S(1)} %get-tuple-element.60), channel_id=1, source_target_pairs={{4,12},{5,13},{6,14},{7,15},{8,0},{9,1},{10,2},{11,3},{12,4},{13,5... | collective-permute-start | bytes 98312 | tf_op jit(solution)/shard_map/ppermute | solution.py:409
  66.8 18.1 %collective-permute-start.13 = (bf16[16,1024]{1,0:T(8,128)(2,1)S(1)}, bf16[16,1024]{1,0:T(8,128)(2,1)S(1)}, u32[]{:S(2)}, u32[]{:S(2)}) collective-permute-start(bf16[16,1024]{1,0:T(8,128)(2,1)S(1)} %get-tuple-element.61), channel_id=1, source_target_pairs={{0,8},{1,9},{2,10},{3,11},{12,0},{13,1},{14,2},{15,3},{16,24},{17,... | collective-permute-start | bytes 98312 | tf_op jit(solution)/shard_map/ppermute | solution.py:409
  80.1 4.8 %collective-permute-start.14 = (bf16[16,1024]{1,0:T(8,128)(2,1)S(1)}, bf16[16,1024]{1,0:T(8,128)(2,1)S(1)}, u32[]{:S(2)}, u32[]{:S(2)}) collective-permute-start(bf16[16,1024]{1,0:T(8,128)(2,1)S(1)} %get-tuple-element.62), channel_id=1, source_target_pairs={{0,4},{1,5},{2,6},{3,7},{4,8},{5,9},{6,10},{7,11},{16,20},{17,21},... | collective-permute-start | bytes 98312 | tf_op jit(solution)/shard_map/ppermute | solution.py:409
  82.9 2.9 %collective-permute-start.15 = (bf16[16,1024]{1,0:T(8,128)(2,1)S(1)}, bf16[16,1024]{1,0:T(8,128)(2,1)S(1)}, u32[]{:S(2)}, u32[]{:S(2)}) collective-permute-start(bf16[16,1024]{1,0:T(8,128)(2,1)S(1)} %get-tuple-element.63), channel_id=1, source_target_pairs={{0,12},{1,13},{2,14},{3,15},{12,8},{13,9},{14,10},{15,11},{8,4},{9... | collective-permute-start | bytes 98312 | tf_op jit(solution)/shard_map/ppermute | solution.py:409
  84.2 1.6 %collective-permute-start.16 = (bf16[16,1024]{1,0:T(8,128)(2,1)S(1)}, bf16[16,1024]{1,0:T(8,128)(2,1)S(1)}, u32[]{:S(2)}, u32[]{:S(2)}) collective-permute-start(bf16[16,1024]{1,0:T(8,128)(2,1)S(1)} %get-tuple-element.64), channel_id=1, source_target_pairs={{8,12},{9,13},{10,14},{11,15},{24,28},{25,29},{26,30},{27,31},{40,... | collective-permute-start | bytes 98312 | tf_op jit(solution)/shard_map/ppermute | solution.py:409
